TPU v7x, 512 devices: a whole 4x4x16 slice. The times are simulated.
512 devices in a mesh: wide: 32 (over x, z_lo, core), oct: 16 (over y, z_hi).
Axes of the slice: x: 4, y: 4, z: 16 (z_hi: 4, z_lo: 4; z = z_hi * 4 + z_lo), core: 2. Of those that a mesh axis runs over, the one named last changes fastest.
Arguments:
- positions: float32 [3, 1048576], P(None, ('wide', 'oct'))
- masses: float32 [1048576], P(('wide', 'oct')), may hold values from 0.5 to 2
- counts: int32 [4096], P(('wide', 'oct')), may hold values from 64 to 256, as said below
- near_list: int32 [4096, 8], P(('wide', 'oct')), may hold values from 0 to 79, as said below
- far_list: int32 [4096, 16], P(('wide', 'oct')), may hold values from 0 to 767, as said below
Outputs:
- acceleration: float32 [3, 1048576], P(None, ('wide', 'oct'))
Inputs may be any that keep to these rules, and one draw needn't show every extreme that they name: counts lie between 64 and 256; both ends are reached. `near_list`: on every device the lists of its blocks together name every level 0 to 9; two entries of one block never name the same block. `far_list`: on every device the lists of its blocks together name every wide level 0 to 5.
All inputs are finite; a program needn't handle non-finite values.
Results may differ from a plain program's by a relative error of at most 0.0003.
Values sent between devices are 32-bit elements; how exact they have to be, the bound alone decides.
No kernel may reach another device: no remote copies, remote signals or barrier semaphores. Data moves between devices by JAX's collectives and lax.ppermute only.
A program may use at most 64 MiB of HBM per device.

v0:
```python
import jax
import jax.numpy as jnp
from jax import lax
from jax.experimental import pallas as pl
from jax.experimental.pallas import tpu as pltpu
from jax.sharding import PartitionSpec as P


near_soft = 0.01
far_soft = 0.25
BLK = 8
LEAF = 256
BODY = BLK * 8
SLOT = 16
GROUPS = 4
CHUNK = 8 * GROUPS
UNROLL = 2
F32 = jnp.float32
I32 = jnp.int32
VMEM = pl.BlockSpec(memory_space=pltpu.VMEM)
SMEM = pl.BlockSpec(memory_space=pltpu.SMEM)
HBM = pl.BlockSpec(memory_space=pltpu.HBM)
RELAY = (3, 2, 1, 0)


def planes(ref):
    half = [[ref[pl.ds(h * 4 + c, BLK, stride=8), :] for h in range(2)] for c in range(4)]
    return [jnp.concatenate(pair, axis=1) for pair in half]


def pack_kernel(counts_hbm, pos_hbm, mass_hbm, out_ref, counts_ref, pos_ref, mass_ref, sems):
    copies = [
        pltpu.make_async_copy(src, dst, sems.at[i])
        for i, (src, dst) in enumerate(((pos_hbm, pos_ref), (mass_hbm, mass_ref), (counts_hbm, counts_ref)))
    ]
    for copy in copies:
        copy.start()
    for copy in copies:
        copy.wait()
    lane = lax.broadcasted_iota(I32, (1, 128), 1)
    for b in range(BLK):
        for half in range(2):
            row = b * 8 + half * 4
            at = b * LEAF + half * 128
            for c in range(3):
                out_ref[row + c : row + c + 1, :] = pos_ref[c : c + 1, at : at + 128]
            live = lane + half * 128 < counts_ref[b]
            out_ref[row + 3 : row + 4, :] = jnp.where(live, mass_ref[2 * b + half : 2 * b + half + 1, :], 0.0)
    x, y, z, m = planes(out_ref)

    def total(a):
        return jnp.sum(a, axis=1, keepdims=True)

    mass = total(m)
    cx, cy, cz = total(x * m) / mass, total(y * m) / mass, total(z * m) / mass
    dx, dy, dz = x - cx, y - cy, z - cz
    mx, my, mz = m * dx, m * dy, m * dz
    xx, yy, zz = total(mx * dx), total(my * dy), total(mz * dz)
    trace = xx + yy + zz
    first = [mass, cx, cy, cz, 3.0 * xx - trace, 3.0 * yy - trace, 3.0 * zz - trace, 3.0 * total(mx * dy)]
    last = [3.0 * total(mx * dz), 3.0 * total(my * dz)]
    lanes = lax.broadcasted_iota(I32, (BLK, 128), 1)
    blocks = lax.broadcasted_iota(I32, (BLK, 128), 0)

    def cell_row(columns):
        tile = jnp.zeros((BLK, 128), F32)
        for k, column in enumerate(columns):
            tile = jnp.where(lanes % SLOT == k, column, tile)
        return jnp.sum(jnp.where(lanes // SLOT == blocks, tile, 0.0), axis=0, keepdims=True)

    rows = jnp.where(blocks == 0, cell_row(first), 0.0)
    out_ref[BODY:, :] = jnp.where(blocks == 1, cell_row(last), rows)


def join_kernel(*refs):
    *sets, out_ref = refs
    first = [ref[BODY : BODY + 1, :] for ref in sets]
    last = sum(pltpu.roll(jnp.broadcast_to(ref[BODY + 1 : BODY + 2, :], (8, 128)), 2 * g, 1) if g else jnp.broadcast_to(ref[BODY + 1 : BODY + 2, :], (8, 128)) for g, ref in enumerate(sets))
    at = lax.broadcasted_iota(I32, (8, 128), 0)
    tile = jnp.where(at == 3, last, 0.0)
    for g in range(0, len(sets), 2):
        pair = jnp.broadcast_to(first[g], (8, 128))
        if g + 1 < len(sets):
            pair = pair + pltpu.roll(jnp.broadcast_to(first[g + 1], (8, 128)), 8, 1)
        tile = jnp.where(at == g // 2, pair, tile)
    for k in range(out_ref.shape[0]):
        out_ref[k, :BODY, :] = sets[0][:BODY, :]
        out_ref[k, BODY:, :] = tile


def near_sums(near_ref, counts_ref, own, sets, local_of, scratch):
    source_ref, tx, ty, tz, acc_ref, list_ref = scratch
    lane8 = lax.broadcasted_iota(I32, (BLK, 128), 1)
    block8 = lax.broadcasted_iota(I32, (BLK, 128), 0)
    masks = []
    for s, body in enumerate(sets):
        for b in range(BLK):
            tile = body(b)
            source_ref[s * BODY + b * 8 : s * BODY + b * 8 + 8, :] = tile
        second = source_ref[pl.ds(s * BODY + 7, BLK, stride=8), :]
        bits = jnp.where((lane8 == 0) & (second > 0.0), jnp.left_shift(1, block8), 0)
        masks.append(jnp.sum(bits))
    empty = len(sets) * BODY
    source_ref[empty : empty + 8, :] = jnp.zeros((8, 128), F32)
    x, y, z, _ = planes(own)
    tx[...], ty[...], tz[...] = x.T, y.T, z.T
    lengths = []
    for b in range(BLK):
        n = jnp.int32(0)
        for v in range(near_ref.shape[1]):
            code = near_ref[b, v]
            local = local_of(code // BLK)
            row = local * BODY + (code % BLK) * 8
            mask = jnp.int32(0)
            for s in range(len(sets)):
                mask = jnp.where(local == s, masks[s], mask)
            list_ref[b, n] = row
            n = n + (local >= 0).astype(I32)
            list_ref[b, n] = row + 4
            n = n + ((local >= 0) & (jnp.right_shift(mask, code % BLK) % 2 == 1)).astype(I32)
        for i in range(UNROLL - 1):
            list_ref[b, n + i] = empty
        lengths.append(n)
    acc_ref[...] = jnp.zeros_like(acc_ref)
    for b in range(BLK):

        def chunk(g, carry, b=b):
            start = pl.multiple_of(g * CHUNK, CHUNK)
            t = [
                [jnp.broadcast_to(ref[pl.ds(start + 8 * i, 8), b : b + 1], (8, 128)) for ref in (tx, ty, tz)]
                for i in range(GROUPS)
            ]

            def pair(k, acc):
                acc = list(acc)
                for u in range(UNROLL):
                    row = list_ref[b, k * UNROLL + u]
                    s = [jnp.broadcast_to(source_ref[pl.ds(row + c, 1), :], (8, 128)) for c in range(4)]
                    for i in range(GROUPS):
                        dx, dy, dz = s[0] - t[i][0], s[1] - t[i][1], s[2] - t[i][2]
                        inv = lax.rsqrt(dx * dx + dy * dy + dz * dz + near_soft)
                        w = s[3] * (inv * inv * inv)
                        acc[3 * i] += dx * w
                        acc[3 * i + 1] += dy * w
                        acc[3 * i + 2] += dz * w
                return tuple(acc)

            zero = jnp.zeros((8, 128), F32)
            acc = lax.fori_loop(0, (lengths[b] + UNROLL - 1) // UNROLL, pair, (zero,) * (3 * GROUPS))
            for i in range(GROUPS):
                for c in range(3):
                    acc_ref[c, pl.ds(b * LEAF + start + 8 * i, 8), :] = acc[3 * i + c]
            return carry

        lax.fori_loop(0, (counts_ref[b] + CHUNK - 1) // CHUNK, chunk, 0)
    out = []
    lane = lax.broadcasted_iota(I32, (LEAF, BLK), 1)
    for c in range(3):
        columns = jnp.zeros((LEAF, BLK), F32)
        for b in range(BLK):
            part = jnp.sum(acc_ref[c, b * LEAF : (b + 1) * LEAF, :], axis=1, keepdims=True)
            columns = jnp.where(lane == b, part, columns)
        out.append(columns.T)
    return out


def block_of(ref):
    return lambda b: ref[b * 8 : b * 8 + 8, :]


def first_near_kernel(near_ref, counts_ref, own, *refs):
    wide, (out_ref, *scratch) = refs[:5], refs[5:]
    sums = near_sums(
        near_ref,
        counts_ref,
        own,
        [block_of(own), *map(block_of, wide)],
        lambda level: jnp.where(level == 0, 0, jnp.where(level >= 5, level - 4, -1)),
        scratch,
    )
    for c in range(3):
        out_ref[c] = sums[c]


def second_near_kernel(near_ref, counts_ref, own, z_one, y_all, before, out_ref, *scratch):
    y = lax.axis_index("oct") // 4

    def member(flip):
        return lambda b: y_all[y ^ flip, b * 8 : b * 8 + 8, :]

    sums = near_sums(
        near_ref,
        counts_ref,
        own,
        [block_of(z_one), member(1), member(2)],
        lambda level: jnp.where(level == 1, 0, jnp.where((level == 3) | (level == 4), level - 2, -1)),
        scratch,
    )
    for c in range(3):
        out_ref[c] = before[c] + sums[c]


def last_kernel(near_ref, far_ref, counts_ref, far_vec_ref, own, z_one, z_two, before, out_ref, table_ref, chosen_ref, rows_ref, *scratch):
    sums = near_sums(near_ref, counts_ref, own, [block_of(z_two)], lambda level: jnp.where(level == 2, 0, -1), scratch)
    for c in range(3):
        sums[c] = before[c] + sums[c]
    me = lax.axis_index("oct") % 4
    other = 3 - me
    n = z_one.shape[0] - BODY
    for place, rows in (
        (me, own[BODY:, :]),
        (me ^ 1, z_one[BODY:, :]),
        (other, z_two[BODY : BODY + n, :]),
        (other ^ 1, z_two[BODY + n :, :]),
    ):
        table_ref[pl.ds(pl.multiple_of(place * n, n), n), :] = rows
    members = lax.axis_size("oct")
    far_count = far_ref.shape[1]
    for v in range(far_count):
        for b in range(BLK):
            code = far_ref[b, v]
            member = code // BLK % members
            row = member % 4 * n + member // 4 * 4
            at = v * BLK + b
            chosen_ref[0, at : at + 1, :] = table_ref[pl.ds(row + code // (2 * BLK * members), 1), :]
            chosen_ref[1, at : at + 1, :] = table_ref[pl.ds(row + 3, 1), :]
    x, y, z, _ = planes(own)
    for v in range(far_count):
        code = far_vec_ref[:, v : v + 1]
        group = code // (BLK * members)
        tiles = []
        for part, shift_by in ((0, group % 2 * 8), (1, group * 2)):
            tile = chosen_ref[part, v * BLK : (v + 1) * BLK, :]
            shift = code % BLK * SLOT + shift_by
            for bit in (8, 16, 32, 64) if part == 0 else (2, 4, 8, 16, 32, 64):
                tile = jnp.where(shift // bit % 2 == 1, pltpu.roll(tile, 128 - bit, 1), tile)
            tiles.append(tile)
        mass, cx, cy, cz, xx, yy, zz, xy = (tiles[0][:, k : k + 1] for k in range(8))
        xz, yz = (tiles[1][:, k : k + 1] for k in range(2))
        rx, ry, rz = x - cx, y - cy, z - cz
        inv = lax.rsqrt(rx * rx + ry * ry + rz * rz + far_soft)
        inv2 = inv * inv
        inv3 = inv * inv2
        inv5 = inv3 * inv2
        inv7 = inv5 * inv2
        qx = xx * rx + xy * ry + xz * rz
        qy = xy * rx + yy * ry + yz * rz
        qz = xz * rx + yz * ry + zz * rz
        rqr = rx * qx + ry * qy + rz * qz
        radial = -mass * inv3 - 2.5 * rqr * inv7
        sums[0] += rx * radial + qx * inv5
        sums[1] += ry * radial + qy * inv5
        sums[2] += rz * radial + qz * inv5
    lane = lax.broadcasted_iota(I32, (1, LEAF), 1)
    grav = 1.0 / (near_ref.shape[1] * LEAF)
    for c in range(3):
        rows_ref[c] = sums[c] * grav
        for b in range(BLK):
            out_ref[c : c + 1, b * LEAF : (b + 1) * LEAF] = jnp.where(lane < counts_ref[b], rows_ref[c, b : b + 1, :], 0.0)


def near_scratch(sets):
    return [
        pltpu.VMEM((sets * BODY + 8, 128), F32),
        pltpu.VMEM((LEAF, BLK), F32),
        pltpu.VMEM((LEAF, BLK), F32),
        pltpu.VMEM((LEAF, BLK), F32),
        pltpu.VMEM((3, BLK * LEAF, 128), F32),
        pltpu.SMEM((BLK, 24), I32),
    ]


def params(mib):
    return pltpu.CompilerParams(vmem_limit_bytes=mib << 20)


def cost(flops):
    return pl.CostEstimate(flops=flops, bytes_accessed=1 << 18, transcendentals=0)


def exchange(payload, axis, flip):
    return lax.ppermute(payload, axis, [(i, flip(i)) for i in range(lax.axis_size(axis))])


def step(positions, masses, counts, near_list, far_list):
    wide_bits = lax.axis_size("wide").bit_length() - 1
    shape = (BODY + 8, 128)
    own = pl.pallas_call(
        pack_kernel,
        out_shape=jax.ShapeDtypeStruct(shape, F32),
        in_specs=[HBM, HBM, HBM],
        out_specs=VMEM,
        scratch_shapes=[
            pltpu.SMEM(counts.shape, I32),
            pltpu.VMEM(positions.shape, F32),
            pltpu.VMEM((16, 128), F32),
            pltpu.SemaphoreType.DMA((3,)),
        ],
        compiler_params=params(4),
        name="pack",
    )(*(pltpu.with_memory_space_constraint(a, pltpu.HBM) for a in (counts, positions, masses.reshape(16, 128))))
    wide = [exchange(own, "wide", lambda i, bit=bit: i ^ (1 << bit)) for bit in range(wide_bits)]
    message = pl.pallas_call(
        join_kernel,
        out_shape=jax.ShapeDtypeStruct((4, *shape), F32),
        in_specs=[VMEM] * (1 + wide_bits),
        out_specs=VMEM,
        compiler_params=params(4),
        name="join",
    )(own, *wide)
    y_groups = [[z + 4 * y for y in range(4)] for z in range(4)]
    y_all = lax.all_to_all(message, "oct", 0, 0, axis_index_groups=y_groups)
    cells = y_all[:, BODY : BODY + 4, :].reshape(16, 128)
    mine = jnp.concatenate([own[:BODY], cells], axis=0)
    z_one = exchange(mine, "oct", lambda i: i ^ 1)
    partial = jax.ShapeDtypeStruct((3, BLK, LEAF), F32)
    first = pl.pallas_call(
        first_near_kernel,
        out_shape=partial,
        in_specs=[SMEM, SMEM, VMEM] + [VMEM] * wide_bits,
        out_specs=VMEM,
        scratch_shapes=near_scratch(1 + wide_bits),
        compiler_params=params(16),
        cost_estimate=cost(40 << 20),
        name="near_one",
    )(near_list, counts, mine, *wide)
    relay = jnp.concatenate([z_one[:BODY], cells, z_one[BODY:]], axis=0)
    z_two = exchange(relay, "oct", lambda i: (i & ~3) | RELAY[i & 3])
    second = pl.pallas_call(
        second_near_kernel,
        out_shape=partial,
        in_specs=[SMEM, SMEM] + [VMEM] * 4,
        out_specs=VMEM,
        scratch_shapes=near_scratch(3),
        compiler_params=params(16),
        cost_estimate=cost(20 << 20),
        name="near_two",
    )(near_list, counts, mine, relay, y_all, first)
    return pl.pallas_call(
        last_kernel,
        out_shape=jax.ShapeDtypeStruct(positions.shape, F32),
        in_specs=[SMEM, SMEM, SMEM] + [VMEM] * 5,
        out_specs=VMEM,
        scratch_shapes=[
            pltpu.VMEM((64, 128), F32),
            pltpu.VMEM((2, BLK * far_list.shape[1], 128), F32),
            pltpu.VMEM((3, BLK, LEAF), F32),
            *near_scratch(1),
        ],
        compiler_params=params(16),
        cost_estimate=cost(20 << 20),
        name="last",
    )(near_list, far_list, counts, far_list, mine, z_one, z_two, second)


def solution(mesh):
    return jax.shard_map(
        step,
        mesh=mesh,
        in_specs=(
            P(None, ("wide", "oct")),
            P(("wide", "oct")),
            P(("wide", "oct")),
            P(("wide", "oct"), None),
            P(("wide", "oct"), None),
        ),
        out_specs=P(None, ("wide", "oct")),
        check_vma=False,
    )
```

profile of v0, /device:TPU:50, one launch (start us, length us, event | category | flops | bytes accessed | tf_op | source)
XLA Modules:
  0.0 92.2 jit_solution(4963226784603344753)
XLA Ops:
  0.0 1.0 %pack.1.refs_0_ = f32[72,128]{1,0:T(8,128)S(1)} custom-call(s32[8]{0:T(128)} %counts_ref.5, f32[3,2048]{1,0:T(4,128)} %pos_hbm.1, f32[16,128]{1,0:T(8,128)} %bitcast.4), custom_call_target="tpu_custom_call" | custom-call | tf_op jit(solution)/shard_map/pack/pallas_call | solution.py:288
  1.0 4.0 %collective-permute-start.4 = (f32[72,128]{1,0:T(8,128)S(1)}, f32[72,128]{1,0:T(8,128)S(1)}, u32[]{:S(2)}, u32[]{:S(2)}) collective-permute-start(f32[72,128]{1,0:T(8,128)S(1)} %pack.1.refs_0_), channel_id=1, source_target_pairs={{0,256},{16,272},{32,288},{48,304},{64,320},{80,336},{96,352},{112... | collective-permute-start | bytes 110600 | tf_op jit(solution)/shard_map/ppermute | solution.py:282
  5.1 3.3 %collective-permute-start.3 = (f32[72,128]{1,0:T(8,128)S(1)}, f32[72,128]{1,0:T(8,128)S(1)}, u32[]{:S(2)}, u32[]{:S(2)}) collective-permute-start(f32[72,128]{1,0:T(8,128)S(1)} %pack.1.refs_0_), channel_id=1, source_target_pairs={{0,128},{16,144},{32,160},{48,176},{64,192},{80,208},{96,224},{112... | collective-permute-start | bytes 110600 | tf_op jit(solution)/shard_map/ppermute | solution.py:282
  8.4 5.2 %collective-permute-start.2 = (f32[72,128]{1,0:T(8,128)S(1)}, f32[72,128]{1,0:T(8,128)S(1)}, u32[]{:S(2)}, u32[]{:S(2)}) collective-permute-start(f32[72,128]{1,0:T(8,128)S(1)} %pack.1.refs_0_), channel_id=1, source_target_pairs={{0,64},{16,80},{32,96},{48,112},{64,0},{80,16},{96,32},{112,48},{1... | collective-permute-start | bytes 110600 | tf_op jit(solution)/shard_map/ppermute | solution.py:282
  13.6 2.0 %collective-permute-start.1 = (f32[72,128]{1,0:T(8,128)S(1)}, f32[72,128]{1,0:T(8,128)S(1)}, u32[]{:S(2)}, u32[]{:S(2)}) collective-permute-start(f32[72,128]{1,0:T(8,128)S(1)} %pack.1.refs_0_), channel_id=1, source_target_pairs={{0,32},{16,48},{32,0},{48,16},{64,96},{80,112},{96,64},{112,80},{1... | collective-permute-start | bytes 110600 | tf_op jit(solution)/shard_map/ppermute | solution.py:282
  15.6 1.9 %collective-permute-start = (f32[72,128]{1,0:T(8,128)S(1)}, f32[72,128]{1,0:T(8,128)S(1)}, u32[]{:S(2)}, u32[]{:S(2)}) collective-permute-start(f32[72,128]{1,0:T(8,128)S(1)} %pack.1.refs_0_), channel_id=1, source_target_pairs={{0,16},{16,0},{32,48},{48,32},{64,80},{80,64},{96,112},{112,96},{1... | collective-permute-start | bytes 110600 | tf_op jit(solution)/shard_map/ppermute | solution.py:282
  17.6 0.0 collective-permute-done.4.refs_5_.refs_4_
  17.6 0.0 collective-permute-done.3.refs_4_.refs_3_
  17.6 0.0 collective-permute-done.2.refs_3_.refs_2_
  17.6 1.9 %collective-permute-done.1.refs_2_.refs_1_ = f32[72,128]{1,0:T(8,128)S(1)} collective-permute-done((f32[72,128]{1,0:T(8,128)S(1)}, f32[72,128]{1,0:T(8,128)S(1)}, u32[]{:S(2)}, u32[]{:S(2)}) %collective-permute-start.1) | collective-permute-done | bytes 36896 | tf_op jit(solution)/shard_map/ppermute | solution.py:282
  19.5 0.0 collective-permute-done.refs_1_.refs_0_
  19.5 0.7 join.1
  20.2 4.8 %all-to-all-start = ((f32[4,72,128]{2,1,0:T(8,128)}), f32[4,72,128]{2,1,0:T(8,128)S(1)}, u32[]{:S(2)}, u32[]{:S(2)}) async-start(f32[4,72,128]{2,1,0:T(8,128)} %join.1), calls=%async_computation | async-start | bytes 294912 | tf_op jit(solution)/shard_map/all_to_all | solution.py:312
  25.0 3.3 %all-to-all-done.y_all = f32[4,72,128]{2,1,0:T(8,128)S(1)} async-done(((f32[4,72,128]{2,1,0:T(8,128)}), f32[4,72,128]{2,1,0:T(8,128)S(1)}, u32[]{:S(2)}, u32[]{:S(2)}) %all-to-all-start) | async-done | bytes 147488 | tf_op jit(solution)/shard_map/all_to_all | solution.py:312
  28.3 9.1 %collective-permute-start.5 = (f32[80,128]{1,0:T(8,128)S(1)}, f32[80,128]{1,0:T(8,128)S(1)}, u32[]{:S(2)}, u32[]{:S(2)}) collective-permute-start(f32[80,128]{1,0:T(8,128)S(1)} %pad_maximum_fusion.1.own), channel_id=1, source_target_pairs={{0,1},{1,0},{2,3},{3,2},{4,5},{5,4},{6,7},{7,6},{8,9},{9,8},{10,11... | collective-permute-start | bytes 122888 | tf_op jit(solution)/shard_map/ppermute | solution.py:282
  37.4 2.0 %collective-permute-done.5.z_one = f32[80,128]{1,0:T(8,128)S(1)} collective-permute-done((f32[80,128]{1,0:T(8,128)S(1)}, f32[80,128]{1,0:T(8,128)S(1)}, u32[]{:S(2)}, u32[]{:S(2)}) %collective-permute-start.5) | collective-permute-done | bytes 40992 | tf_op jit(solution)/shard_map/ppermute | solution.py:282
  39.4 0.0 copy-start
  39.4 0.0 copy-start.2
  39.5 8.9 %collective-permute-start.6 = (f32[96,128]{1,0:T(8,128)S(1)}, f32[96,128]{1,0:T(8,128)S(1)}, u32[]{:S(2)}, u32[]{:S(2)}) collective-permute-start(f32[96,128]{1,0:T(8,128)S(1)} %pad_maximum_fusion.z_one), channel_id=1, source_target_pairs={{0,3},{1,2},{2,1},{3,0},{4,7},{5,6},{6,5},{7,4},{8,11},{9,10},{10,... | collective-permute-start | bytes 147464 | tf_op jit(solution)/shard_map/ppermute | solution.py:282
  48.4 0.0 copy-done
  48.4 0.0 copy-done.2
  48.4 14.7 %near_one.1.before = f32[3,8,256]{2,1,0:T(8,128)S(1)} custom-call(s32[8,8]{1,0:T(8,128)S(1)} %copy-done, s32[8]{0:T(128)S(1)} %copy-done.2, f32[80,128]{1,0:T(8,128)S(1)} %pad_maximum_fusion.1.own, f32[72,128]{1,0:T(8,128)S(1)} %collective-permute-done.refs_1_.refs_0_, f32[72,128]{1,0:T(8,128)S(1)} %collective-permute-done.1.refs_2_.refs_1_, ...), custom_call_target="tpu_custom_call" | custom-call | flops 41943040 | bytes 262144 | tf_op jit(solution)/shard_map/near_one/pallas_call | solution.py:317
  63.1 0.0 copy-start.1
  63.1 11.4 %near_two.1.before = f32[3,8,256]{2,1,0:T(8,128)S(1)} custom-call(s32[8,8]{1,0:T(8,128)S(1)} %copy-done, s32[8]{0:T(128)S(1)} %copy-done.2, f32[80,128]{1,0:T(8,128)S(1)} %pad_maximum_fusion.1.own, f32[96,128]{1,0:T(8,128)S(1)} %pad_maximum_fusion.z_one, f32[4,72,128]{2,1,0:T(8,128)S(1)} %all-to-all-done.y_all, f32[3,8,256]{2,1,0:T(8,128)S(1)} %near_one.1.before), custom_call_target="tpu_custom_call" | custom-call | flops 20971520 | bytes 262144 | tf_op jit(solution)/shard_map/near_two/pallas_call | solution.py:329
  74.5 0.0 collective-permute-done.6.z_two
  74.5 0.0 copy-done.1
  74.5 17.7 %last.1 = f32[3,2048]{1,0:T(4,128)} custom-call(s32[8,8]{1,0:T(8,128)S(1)} %copy-done, s32[8,16]{1,0:T(8,128)S(1)} %copy-done.1, s32[8]{0:T(128)S(1)} %copy-done.2, s32[8,16]{1,0:T(8,128)S(1)} %copy-done.1, f32[80,128]{1,0:T(8,128)S(1)} %pad_maximum_fusion.1.own, f32[80,128]{1,0:T(8,128)S(1)} %collective-permute-done.5.z_one, ...), custom_call_target="tpu_custom_call" | custom-call | flops 20971520 | bytes 262144 | tf_op jit(solution)/shard_map/last/pallas_call | solution.py:339
  (6 shorter events, 0.0 us)
Async XLA Ops:
  1.0 16.5 %collective-permute-start.4 = (f32[72,128]{1,0:T(8,128)S(1)}, f32[72,128]{1,0:T(8,128)S(1)}, u32[]{:S(2)}, u32[]{:S(2)}) collective-permute-start(f32[72,128]{1,0:T(8,128)S(1)} %pack.1.refs_0_), channel_id=1, source_target_pairs={{0,256},{16,272},{32,288},{48,304},{64,320},{80,336},{96,352},{112... | collective-permute-start | bytes 110600 | tf_op jit(solution)/shard_map/ppermute | solution.py:282
  5.1 12.5 %collective-permute-start.3 = (f32[72,128]{1,0:T(8,128)S(1)}, f32[72,128]{1,0:T(8,128)S(1)}, u32[]{:S(2)}, u32[]{:S(2)}) collective-permute-start(f32[72,128]{1,0:T(8,128)S(1)} %pack.1.refs_0_), channel_id=1, source_target_pairs={{0,128},{16,144},{32,160},{48,176},{64,192},{80,208},{96,224},{112... | collective-permute-start | bytes 110600 | tf_op jit(solution)/shard_map/ppermute | solution.py:282
  8.4 9.2 %collective-permute-start.2 = (f32[72,128]{1,0:T(8,128)S(1)}, f32[72,128]{1,0:T(8,128)S(1)}, u32[]{:S(2)}, u32[]{:S(2)}) collective-permute-start(f32[72,128]{1,0:T(8,128)S(1)} %pack.1.refs_0_), channel_id=1, source_target_pairs={{0,64},{16,80},{32,96},{48,112},{64,0},{80,16},{96,32},{112,48},{1... | collective-permute-start | bytes 110600 | tf_op jit(solution)/shard_map/ppermute | solution.py:282
  13.6 5.9 %collective-permute-start.1 = (f32[72,128]{1,0:T(8,128)S(1)}, f32[72,128]{1,0:T(8,128)S(1)}, u32[]{:S(2)}, u32[]{:S(2)}) collective-permute-start(f32[72,128]{1,0:T(8,128)S(1)} %pack.1.refs_0_), channel_id=1, source_target_pairs={{0,32},{16,48},{32,0},{48,16},{64,96},{80,112},{96,64},{112,80},{1... | collective-permute-start | bytes 110600 | tf_op jit(solution)/shard_map/ppermute | solution.py:282
  15.6 3.8 %collective-permute-start = (f32[72,128]{1,0:T(8,128)S(1)}, f32[72,128]{1,0:T(8,128)S(1)}, u32[]{:S(2)}, u32[]{:S(2)}) collective-permute-start(f32[72,128]{1,0:T(8,128)S(1)} %pack.1.refs_0_), channel_id=1, source_target_pairs={{0,16},{16,0},{32,48},{48,32},{64,80},{80,64},{96,112},{112,96},{1... | collective-permute-start | bytes 110600 | tf_op jit(solution)/shard_map/ppermute | solution.py:282
  20.2 8.1 %all-to-all-start = ((f32[4,72,128]{2,1,0:T(8,128)}), f32[4,72,128]{2,1,0:T(8,128)S(1)}, u32[]{:S(2)}, u32[]{:S(2)}) async-start(f32[4,72,128]{2,1,0:T(8,128)} %join.1), calls=%async_computation | async-start | bytes 294912 | tf_op jit(solution)/shard_map/all_to_all | solution.py:312
  28.3 11.1 %collective-permute-start.5 = (f32[80,128]{1,0:T(8,128)S(1)}, f32[80,128]{1,0:T(8,128)S(1)}, u32[]{:S(2)}, u32[]{:S(2)}) collective-permute-start(f32[80,128]{1,0:T(8,128)S(1)} %pad_maximum_fusion.1.own), channel_id=1, source_target_pairs={{0,1},{1,0},{2,3},{3,2},{4,5},{5,4},{6,7},{7,6},{8,9},{9,8},{10,11... | collective-permute-start | bytes 122888 | tf_op jit(solution)/shard_map/ppermute | solution.py:282
  39.4 8.9 %copy-start = (s32[8,8]{1,0:T(8,128)S(1)}, s32[8,8]{1,0:T(8,128)}, u32[]{:S(2)}) copy-start(s32[8,8]{1,0:T(8,128)} %near_ref.5) | copy-start | bytes 772
  39.4 8.9 %copy-start.2 = (s32[8]{0:T(128)S(1)}, s32[8]{0:T(128)}, u32[]{:S(2)}) copy-start(s32[8]{0:T(128)} %counts_ref.5) | copy-start | bytes 100
  39.5 35.1 %collective-permute-start.6 = (f32[96,128]{1,0:T(8,128)S(1)}, f32[96,128]{1,0:T(8,128)S(1)}, u32[]{:S(2)}, u32[]{:S(2)}) collective-permute-start(f32[96,128]{1,0:T(8,128)S(1)} %pad_maximum_fusion.z_one), channel_id=1, source_target_pairs={{0,3},{1,2},{2,1},{3,0},{4,7},{5,6},{6,5},{7,4},{8,11},{9,10},{10,... | collective-permute-start | bytes 147464 | tf_op jit(solution)/shard_map/ppermute | solution.py:282
  63.1 11.4 %copy-start.1 = (s32[8,16]{1,0:T(8,128)S(1)}, s32[8,16]{1,0:T(8,128)}, u32[]{:S(2)}) copy-start(s32[8,16]{1,0:T(8,128)} %far_vec_ref.1) | copy-start | bytes 1540
where the time goes:
time: 92.7 us; the launch traced here: 92.2 us
  Pallas kernels  45.5 us (49%)
  starting transfers between devices  39.3 us (42%)
  waiting for transfers between devices  7.21 us (8%)
    ppermute x7, starting transfers between devices, exchange(): lax.ppermute(payload, axis, [(i, flip(i)) for i in range(lax.axis_size(ax...  34.5 us
    pallas_call x1, Pallas kernels, step(): pl.pallas_call(last_kernel, out_shape=jax.ShapeDtypeStruct(positions.shap...  17.7 us
    pallas_call x1, Pallas kernels, step(): pl.pallas_call(first_near_kernel, out_shape=partial, in_specs=[SMEM, SMEM...  14.7 us
    pallas_call x1, Pallas kernels, step(): pl.pallas_call(second_near_kernel, out_shape=partial, in_specs=[SMEM, SME...  11.4 us
    all_to_all x1, starting transfers between devices, step(): y_all = lax.all_to_all(message, 'oct', 0, 0, axis_index_groups=y_groups)  4.8 us
    ppermute x7, waiting for transfers between devices, exchange(): lax.ppermute(payload, axis, [(i, flip(i)) for i in range(lax.axis_size(ax...  3.9 us
    all_to_all x1, waiting for transfers between devices, step(): y_all = lax.all_to_all(message, 'oct', 0, 0, axis_index_groups=y_groups)  3.31 us
  transfers between devices with their start and end apart: 8, of which 3 were waited for; matrix products, arithmetic and copies ran while one was open for 0% of the time, Pallas kernels for 28%

commit v1 on v0

v1 whole, which is shorter than its diff:
```python
import jax
import jax.numpy as jnp
from jax import lax
from jax.experimental import pallas as pl
from jax.experimental.pallas import tpu as pltpu
from jax.sharding import PartitionSpec as P


near_soft = 0.01
far_soft = 0.25
BLK = 8
LEAF = 256
BODY = BLK * 8
SLOT = 16
F32 = jnp.float32
I32 = jnp.int32
VMEM = pl.BlockSpec(memory_space=pltpu.VMEM)
SMEM = pl.BlockSpec(memory_space=pltpu.SMEM)
HBM = pl.BlockSpec(memory_space=pltpu.HBM)
RELAY = (3, 2, 1, 0)


def planes(ref):
    half = [[ref[pl.ds(h * 4 + c, BLK, stride=8), :] for h in range(2)] for c in range(4)]
    return [jnp.concatenate(pair, axis=1) for pair in half]


def pack_kernel(counts_hbm, pos_hbm, mass_hbm, out_ref, counts_ref, pos_ref, mass_ref, sems):
    copies = [
        pltpu.make_async_copy(src, dst, sems.at[i])
        for i, (src, dst) in enumerate(((pos_hbm, pos_ref), (mass_hbm, mass_ref), (counts_hbm, counts_ref)))
    ]
    for copy in copies:
        copy.start()
    for copy in copies:
        copy.wait()
    lane = lax.broadcasted_iota(I32, (1, 128), 1)
    for b in range(BLK):
        for half in range(2):
            row = b * 8 + half * 4
            at = b * LEAF + half * 128
            for c in range(3):
                out_ref[row + c : row + c + 1, :] = pos_ref[c : c + 1, at : at + 128]
            live = lane + half * 128 < counts_ref[b]
            out_ref[row + 3 : row + 4, :] = jnp.where(live, mass_ref[2 * b + half : 2 * b + half + 1, :], 0.0)
    x, y, z, m = planes(out_ref)

    def total(a):
        return jnp.sum(a, axis=1, keepdims=True)

    mass = total(m)
    cx, cy, cz = total(x * m) / mass, total(y * m) / mass, total(z * m) / mass
    dx, dy, dz = x - cx, y - cy, z - cz
    mx, my, mz = m * dx, m * dy, m * dz
    xx, yy, zz = total(mx * dx), total(my * dy), total(mz * dz)
    trace = xx + yy + zz
    first = [mass, cx, cy, cz, 3.0 * xx - trace, 3.0 * yy - trace, 3.0 * zz - trace, 3.0 * total(mx * dy)]
    last = [3.0 * total(mx * dz), 3.0 * total(my * dz)]
    lanes = lax.broadcasted_iota(I32, (BLK, 128), 1)
    blocks = lax.broadcasted_iota(I32, (BLK, 128), 0)

    def cell_row(columns):
        tile = jnp.zeros((BLK, 128), F32)
        for k, column in enumerate(columns):
            tile = jnp.where(lanes % SLOT == k, column, tile)
        return jnp.sum(jnp.where(lanes // SLOT == blocks, tile, 0.0), axis=0, keepdims=True)

    rows = jnp.where(blocks == 0, cell_row(first), 0.0)
    out_ref[BODY:, :] = jnp.where(blocks == 1, cell_row(last), rows)


def join_kernel(*refs):
    *sets, out_ref = refs
    first = [ref[BODY : BODY + 1, :] for ref in sets]
    last = sum(pltpu.roll(jnp.broadcast_to(ref[BODY + 1 : BODY + 2, :], (8, 128)), 2 * g, 1) if g else jnp.broadcast_to(ref[BODY + 1 : BODY + 2, :], (8, 128)) for g, ref in enumerate(sets))
    at = lax.broadcasted_iota(I32, (8, 128), 0)
    tile = jnp.where(at == 3, last, 0.0)
    for g in range(0, len(sets), 2):
        pair = jnp.broadcast_to(first[g], (8, 128))
        if g + 1 < len(sets):
            pair = pair + pltpu.roll(jnp.broadcast_to(first[g + 1], (8, 128)), 8, 1)
        tile = jnp.where(at == g // 2, pair, tile)
    for k in range(out_ref.shape[0]):
        out_ref[k, :BODY, :] = sets[0][:BODY, :]
        out_ref[k, BODY:, :] = tile


def spread_targets(own, target_ref):
    for c, plane in enumerate(planes(own)[:3]):
        columns = plane.T
        for b in range(BLK):
            target_ref[c, b * LEAF : (b + 1) * LEAF, :] = jnp.broadcast_to(columns[:, b : b + 1], (LEAF, 128))


def near_part(near_ref, counts_ref, target_ref, sums_ref, source_ref, bodies, levels):
    lane8 = lax.broadcasted_iota(I32, (BLK, 128), 1)
    block8 = lax.broadcasted_iota(I32, (BLK, 128), 0)
    masks = []
    for s, body in enumerate(bodies):
        for b in range(BLK):
            source_ref[s * BODY + b * 8 : s * BODY + b * 8 + 8, :] = body(b)
        second = source_ref[pl.ds(s * BODY + 7, BLK, stride=8), :]
        masks.append(jnp.sum(jnp.where((lane8 == 0) & (second > 0.0), jnp.left_shift(1, block8), 0)))
    entries = near_ref.shape[1]

    def run(row, first, count, groups, halves):
        s = [
            [jnp.broadcast_to(source_ref[pl.ds(row + 4 * h + c, 1), :], (8, 128)) for c in range(4)]
            for h in range(halves)
        ]

        def chunk(g, carry):
            start = pl.multiple_of(first + g * (8 * groups), 8)
            for i in range(groups):
                at = pl.ds(start + 8 * i, 8)
                t = [target_ref[c, at, :] for c in range(3)]
                sums = [sums_ref[c, at, :] for c in range(3)]
                for h in range(halves):
                    dx, dy, dz = s[h][0] - t[0], s[h][1] - t[1], s[h][2] - t[2]
                    inv = lax.rsqrt(dx * dx + dy * dy + dz * dz + near_soft)
                    w = s[h][3] * (inv * inv * inv)
                    sums = [sums[0] + dx * w, sums[1] + dy * w, sums[2] + dz * w]
                for c in range(3):
                    sums_ref[c, at, :] = sums[c]
            return carry

        lax.fori_loop(0, (count + 8 * groups - 1) // (8 * groups), chunk, 0)

    def item(k, carry):
        b = k // entries
        code = near_ref[b, k % entries]
        level, slot = code // BLK, code % BLK
        local = jnp.int32(-1)
        mask = jnp.int32(0)
        for s, name in enumerate(levels):
            local = jnp.where(level == name, s, local)
            mask = jnp.where(level == name, masks[s], mask)
        row = local * BODY + slot * 8
        both = jnp.right_shift(mask, slot) % 2 == 1
        first, count = b * LEAF, counts_ref[b]

        @pl.when((local >= 0) & both)
        def _():
            run(row, first, count, 4, 2)

        @pl.when((local >= 0) & jnp.logical_not(both))
        def _():
            run(row, first, count, 8, 1)

        return carry

    lax.fori_loop(0, BLK * entries, item, 0)


def block_of(ref):
    return lambda b: ref[b * 8 : b * 8 + 8, :]


LEVELS_ONE, LEVELS_TWO, LEVELS_THREE, LEVELS_LAST = (0, 5, 6), (7, 8, 9), (1, 3, 4), (2,)


def near_one_kernel(near_ref, counts_ref, own, wide_a, wide_b, sums_ref, target_ref, source_ref):
    spread_targets(own, target_ref)
    sums_ref[...] = jnp.zeros_like(sums_ref)
    bodies = [*map(block_of, (own, wide_a, wide_b))]
    near_part(near_ref, counts_ref, target_ref, sums_ref, source_ref, bodies, LEVELS_ONE)


def near_two_kernel(near_ref, counts_ref, wide_a, wide_b, wide_c, mine, before, target_ref, sums_ref, source_ref):
    spread_targets(mine, target_ref)
    bodies = [*map(block_of, (wide_a, wide_b, wide_c))]
    near_part(near_ref, counts_ref, target_ref, sums_ref, source_ref, bodies, LEVELS_TWO)


def near_three_kernel(near_ref, counts_ref, z_one, y_all, target_ref, before, sums_ref, source_ref):
    y = lax.axis_index("oct") // 4

    def member(flip):
        return lambda b: y_all[y ^ flip, b * 8 : b * 8 + 8, :]

    bodies = [block_of(z_one), member(1), member(2)]
    near_part(near_ref, counts_ref, target_ref, sums_ref, source_ref, bodies, LEVELS_THREE)


def three_parts(a):
    hi = a.astype(jnp.bfloat16)
    rest = a - hi.astype(F32)
    mid = rest.astype(jnp.bfloat16)
    return hi, mid, (rest - mid.astype(F32)).astype(jnp.bfloat16)


def last_kernel(near_ref, far_ref, counts_ref, own, z_one, z_two, target_ref, before, out_ref, sums_ref, table_ref, rows_ref, source_ref):
    near_part(near_ref, counts_ref, target_ref, sums_ref, source_ref, [block_of(z_two)], LEVELS_LAST)
    sums = []
    lane8 = lax.broadcasted_iota(I32, (LEAF, BLK), 1)
    for c in range(3):
        columns = jnp.zeros((LEAF, BLK), F32)
        for b in range(BLK):
            part = jnp.sum(sums_ref[c, b * LEAF : (b + 1) * LEAF, :], axis=1, keepdims=True)
            columns = jnp.where(lane8 == b, part, columns)
        sums.append(columns.T)
    me = lax.axis_index("oct") % 4
    other = 3 - me
    n = z_one.shape[0] - BODY
    for place, rows in (
        (me, own[BODY:, :]),
        (me ^ 1, z_one[BODY:, :]),
        (other, z_two[BODY : BODY + n, :]),
        (other ^ 1, z_two[BODY + n :, :]),
    ):
        table_ref[pl.ds(pl.multiple_of(place * n, n), n), :] = rows
    members = lax.axis_size("oct")
    far_count = far_ref.shape[1]
    picks = BLK * far_count
    lanes = lax.broadcasted_iota(I32, (picks, 128), 1)
    code = jnp.concatenate([jnp.broadcast_to(far_ref[:, v : v + 1], (BLK, 128)) for v in range(far_count)], axis=0)
    group, member, slot = code // (BLK * members), code // BLK % members, code % BLK
    row = member % 4 * n + member // 4 * 4
    table = jnp.concatenate(three_parts(table_ref[...]), axis=1)
    folded = jnp.zeros((picks, 128), F32)
    lhs, rhs = [], []
    fold_from = lax.broadcasted_iota(I32, (128, 128), 0)
    fold_to = lax.broadcasted_iota(I32, (128, 128), 1)
    for at_row, low, width, base in (
        (row + group // 2, slot * SLOT + group % 2 * 8, 8, 0),
        (row + 3, slot * SLOT + group * 2, 2, 8),
    ):
        hot = (lanes == at_row)[:, : table_ref.shape[0]].astype(F32).astype(jnp.bfloat16)
        rows = jnp.dot(hot, table, preferred_element_type=F32)
        keep = (lanes >= low) & (lanes < low + width)
        fold = (fold_from % width + base == fold_to).astype(F32).astype(jnp.bfloat16)
        for part in range(3):
            chosen = jnp.where(keep, rows[:, part * 128 : (part + 1) * 128], 0.0)
            lhs.append(chosen.astype(jnp.bfloat16))
            rhs.append(fold)
    folded = jnp.dot(jnp.concatenate(lhs, axis=1), jnp.concatenate(rhs, axis=0), preferred_element_type=F32)
    x, y, z, _ = planes(own)
    for v in range(far_count):
        tile = folded[v * BLK : (v + 1) * BLK, :]
        mass, cx, cy, cz, xx, yy, zz, xy, xz, yz = (tile[:, k : k + 1] for k in range(10))
        rx, ry, rz = x - cx, y - cy, z - cz
        inv = lax.rsqrt(rx * rx + ry * ry + rz * rz + far_soft)
        inv2 = inv * inv
        inv3 = inv * inv2
        inv5 = inv3 * inv2
        inv7 = inv5 * inv2
        qx = xx * rx + xy * ry + xz * rz
        qy = xy * rx + yy * ry + yz * rz
        qz = xz * rx + yz * ry + zz * rz
        rqr = rx * qx + ry * qy + rz * qz
        radial = -mass * inv3 - 2.5 * rqr * inv7
        sums[0] += rx * radial + qx * inv5
        sums[1] += ry * radial + qy * inv5
        sums[2] += rz * radial + qz * inv5
    lane = lax.broadcasted_iota(I32, (1, LEAF), 1)
    grav = 1.0 / (near_ref.shape[1] * LEAF)
    for c in range(3):
        rows_ref[c] = sums[c] * grav
        for b in range(BLK):
            out_ref[c : c + 1, b * LEAF : (b + 1) * LEAF] = jnp.where(lane < counts_ref[b], rows_ref[c, b : b + 1, :], 0.0)


def sources(sets):
    return pltpu.VMEM((sets * BODY, 128), F32)


def params(mib):
    return pltpu.CompilerParams(vmem_limit_bytes=mib << 20)


def cost(flops):
    return pl.CostEstimate(flops=flops, bytes_accessed=1 << 18, transcendentals=0)


def mine_kernel(own, y_all, out_ref):
    out_ref[:BODY, :] = own[:BODY, :]
    for y in range(4):
        out_ref[BODY + 4 * y : BODY + 4 * y + 4, :] = y_all[y, BODY : BODY + 4, :]


def relay_kernel(mine, z_one, out_ref):
    n = z_one.shape[0] - BODY
    out_ref[:BODY, :] = z_one[:BODY, :]
    out_ref[BODY : BODY + n, :] = mine[BODY:, :]
    out_ref[BODY + n :, :] = z_one[BODY:, :]


def small_call(kernel, rows, *operands):
    return pl.pallas_call(
        kernel,
        out_shape=jax.ShapeDtypeStruct((rows, 128), F32),
        in_specs=[VMEM] * len(operands),
        out_specs=VMEM,
        compiler_params=params(2),
    )(*operands)


def exchange(payload, axis, flip):
    return lax.ppermute(payload, axis, [(i, flip(i)) for i in range(lax.axis_size(axis))])


def step(positions, masses, counts, near_list, far_list):
    wide_bits = lax.axis_size("wide").bit_length() - 1
    shape = (BODY + 8, 128)
    own = pl.pallas_call(
        pack_kernel,
        out_shape=jax.ShapeDtypeStruct(shape, F32),
        in_specs=[HBM, HBM, HBM],
        out_specs=VMEM,
        scratch_shapes=[
            pltpu.SMEM(counts.shape, I32),
            pltpu.VMEM(positions.shape, F32),
            pltpu.VMEM((16, 128), F32),
            pltpu.SemaphoreType.DMA((3,)),
        ],
        compiler_params=params(4),
        name="pack",
    )(*(pltpu.with_memory_space_constraint(a, pltpu.HBM) for a in (counts, positions, masses.reshape(16, 128))))
    wide = [exchange(own, "wide", lambda i, bit=bit: i ^ (1 << bit)) for bit in range(wide_bits)]
    message = pl.pallas_call(
        join_kernel,
        out_shape=jax.ShapeDtypeStruct((4, *shape), F32),
        in_specs=[VMEM] * (1 + wide_bits),
        out_specs=VMEM,
        compiler_params=params(4),
        name="join",
    )(own, *wide)
    y_groups = [[z + 4 * y for y in range(4)] for z in range(4)]
    y_all = lax.all_to_all(message, "oct", 0, 0, axis_index_groups=y_groups)
    state = jax.ShapeDtypeStruct((3, BLK * LEAF, 128), F32)
    sums = pl.pallas_call(
        near_one_kernel,
        out_shape=state,
        in_specs=[SMEM, SMEM] + [VMEM] * 3,
        out_specs=VMEM,
        scratch_shapes=[pltpu.VMEM(state.shape, F32), sources(3)],
        compiler_params=params(8),
        cost_estimate=cost(20 << 20),
        name="near_one",
    )(near_list, counts, own, wide[0], wide[1])
    mine = small_call(mine_kernel, BODY + 16, own, y_all)
    z_one = exchange(mine, "oct", lambda i: i ^ 1)
    targets, sums = pl.pallas_call(
        near_two_kernel,
        out_shape=[state, state],
        in_specs=[SMEM, SMEM] + [VMEM] * 5,
        out_specs=[VMEM, VMEM],
        scratch_shapes=[sources(3)],
        input_output_aliases={6: 1},
        compiler_params=params(8),
        cost_estimate=cost(20 << 20),
        name="near_two",
    )(near_list, counts, *wide[2:], mine, sums)
    relay = small_call(relay_kernel, BODY + 32, mine, z_one)
    z_two = exchange(relay, "oct", lambda i: (i & ~3) | RELAY[i & 3])
    sums = pl.pallas_call(
        near_three_kernel,
        out_shape=state,
        in_specs=[SMEM, SMEM] + [VMEM] * 4,
        out_specs=VMEM,
        scratch_shapes=[sources(3)],
        input_output_aliases={5: 0},
        compiler_params=params(8),
        cost_estimate=cost(20 << 20),
        name="near_three",
    )(near_list, counts, relay, y_all, targets, sums)
    return pl.pallas_call(
        last_kernel,
        out_shape=[jax.ShapeDtypeStruct(positions.shape, F32), state],
        in_specs=[SMEM, VMEM, SMEM] + [VMEM] * 5,
        out_specs=[VMEM, VMEM],
        scratch_shapes=[
            pltpu.VMEM((64, 128), F32),
            pltpu.VMEM((3, BLK, LEAF), F32),
            sources(1),
        ],
        input_output_aliases={7: 1},
        compiler_params=params(8),
        cost_estimate=cost(20 << 20),
        name="last",
    )(near_list, far_list, counts, mine, z_one, z_two, targets, sums)[0]


def solution(mesh):
    return jax.shard_map(
        step,
        mesh=mesh,
        in_specs=(
            P(None, ("wide", "oct")),
            P(("wide", "oct")),
            P(("wide", "oct")),
            P(("wide", "oct"), None),
            P(("wide", "oct"), None),
        ),
        out_specs=P(None, ("wide", "oct")),
        check_vma=False,
    )
```

time: 92.7 us -> 82 us (0.88)
  the two profiles are of different devices: /device:TPU:50 before, /device:TPU:8 now
where the time goes in v1:
time: 82 us; the launch traced here: 81.6 us
  starting transfers between devices  36.2 us (44%)
  Pallas kernels  29.3 us (36%)
  blocking collectives  9.31 us (11%)
  waiting for transfers between devices  5.28 us (6%)
  local copies, waits for them, and re-layouts  1.34 us (2%)
    ppermute x7, starting transfers between devices, exchange(): lax.ppermute(payload, axis, [(i, flip(i)) for i in range(lax.axis_size(ax...  36.2 us
    all_to_all x1, blocking collectives, step(): y_all = lax.all_to_all(message, 'oct', 0, 0, axis_index_groups=y_groups)  9.31 us
    pallas_call x1, Pallas kernels, step(): pl.pallas_call(near_two_kernel, out_shape=[state, state], in_specs=[SMEM,...  7.33 us
    pallas_call x1, Pallas kernels, step(): pl.pallas_call(near_one_kernel, out_shape=state, in_specs=[SMEM, SMEM] +...  7.26 us
    pallas_call x1, Pallas kernels, step(): pl.pallas_call(last_kernel, out_shape=[jax.ShapeDtypeStruct(positions.sha...  6.98 us
    pallas_call x1, Pallas kernels, step(): pl.pallas_call(near_three_kernel, out_shape=state, in_specs=[SMEM, SMEM]...  6.63 us
    ppermute x7, waiting for transfers between devices, exchange(): lax.ppermute(payload, axis, [(i, flip(i)) for i in range(lax.axis_size(ax...  5.28 us
  transfers between devices with their start and end apart: 7, of which 2 were waited for; matrix products, arithmetic and copies ran while one was open for 0% of the time, Pallas kernels for 26%

profile of v1, /device:TPU:8, one launch (start us, length us, event | category | flops | bytes accessed | tf_op | source)
XLA Modules:
  0.0 81.6 jit_solution(17588925742412567604)
XLA Ops:
  0.0 1.0 %pack.1.refs_0_.own = f32[72,128]{1,0:T(8,128)S(1)} custom-call(s32[8]{0:T(128)} %counts_ref.7, f32[3,2048]{1,0:T(4,128)} %pos_hbm.1, f32[16,128]{1,0:T(8,128)} %bitcast.1), custom_call_target="tpu_custom_call" | custom-call | tf_op jit(solution)/shard_map/pack/pallas_call | solution.py:305
  1.0 1.9 %collective-permute-start = (f32[72,128]{1,0:T(8,128)S(1)}, f32[72,128]{1,0:T(8,128)S(1)}, u32[]{:S(2)}, u32[]{:S(2)}) collective-permute-start(f32[72,128]{1,0:T(8,128)S(1)} %pack.1.refs_0_.own), channel_id=1, source_target_pairs={{0,16},{16,0},{32,48},{48,32},{64,80},{80,64},{96,112},{112,96},{1... | collective-permute-start | bytes 110600 | tf_op jit(solution)/shard_map/ppermute | solution.py:299
  3.0 3.8 %collective-permute-start.1 = (f32[72,128]{1,0:T(8,128)S(1)}, f32[72,128]{1,0:T(8,128)S(1)}, u32[]{:S(2)}, u32[]{:S(2)}) collective-permute-start(f32[72,128]{1,0:T(8,128)S(1)} %pack.1.refs_0_.own), channel_id=1, source_target_pairs={{0,32},{16,48},{32,0},{48,16},{64,96},{80,112},{96,64},{112,80},{1... | collective-permute-start | bytes 110600 | tf_op jit(solution)/shard_map/ppermute | solution.py:299
  6.8 5.2 %collective-permute-start.2 = (f32[72,128]{1,0:T(8,128)S(1)}, f32[72,128]{1,0:T(8,128)S(1)}, u32[]{:S(2)}, u32[]{:S(2)}) collective-permute-start(f32[72,128]{1,0:T(8,128)S(1)} %pack.1.refs_0_.own), channel_id=1, source_target_pairs={{0,64},{16,80},{32,96},{48,112},{64,0},{80,16},{96,32},{112,48},{1... | collective-permute-start | bytes 110600 | tf_op jit(solution)/shard_map/ppermute | solution.py:299
  12.0 3.4 %collective-permute-start.3 = (f32[72,128]{1,0:T(8,128)S(1)}, f32[72,128]{1,0:T(8,128)S(1)}, u32[]{:S(2)}, u32[]{:S(2)}) collective-permute-start(f32[72,128]{1,0:T(8,128)S(1)} %pack.1.refs_0_.own), channel_id=1, source_target_pairs={{0,128},{16,144},{32,160},{48,176},{64,192},{80,208},{96,224},{112... | collective-permute-start | bytes 110600 | tf_op jit(solution)/shard_map/ppermute | solution.py:299
  15.4 4.6 %collective-permute-start.4 = (f32[72,128]{1,0:T(8,128)S(1)}, f32[72,128]{1,0:T(8,128)S(1)}, u32[]{:S(2)}, u32[]{:S(2)}) collective-permute-start(f32[72,128]{1,0:T(8,128)S(1)} %pack.1.refs_0_.own), channel_id=1, source_target_pairs={{0,256},{16,272},{32,288},{48,304},{64,320},{80,336},{96,352},{112... | collective-permute-start | bytes 110600 | tf_op jit(solution)/shard_map/ppermute | solution.py:299
  20.0 0.0 collective-permute-done.refs_1_.wide_a
  20.0 0.0 collective-permute-done.1.refs_2_.wide_b
  20.1 0.0 collective-permute-done.2.refs_3_.wide_a
  20.1 0.0 collective-permute-done.3.refs_4_.wide_b
  20.1 2.7 %collective-permute-done.4.refs_5_.wide_c = f32[72,128]{1,0:T(8,128)S(1)} collective-permute-done((f32[72,128]{1,0:T(8,128)S(1)}, f32[72,128]{1,0:T(8,128)S(1)}, u32[]{:S(2)}, u32[]{:S(2)}) %collective-permute-start.4) | collective-permute-done | bytes 36896 | tf_op jit(solution)/shard_map/ppermute | solution.py:299
  22.7 0.1 join.1
  22.8 9.3 %all_to_all.5.y_all = f32[4,72,128]{2,1,0:T(8,128)S(1)} all-to-all(f32[4,72,128]{2,1,0:T(8,128)S(1)} %join.1), channel_id=1, replica_groups={{0,4,8,12},{1,5,9,13},{2,6,10,14},{3,7,11,15},{16,20,24,28},{17,21,25,2..., dimensions={0} | all-to-all | bytes 294912 | tf_op jit(solution)/shard_map/all_to_all | solution.py:329
  32.1 9.1 %collective-permute-start.5 = (f32[80,128]{1,0:T(8,128)S(1)}, f32[80,128]{1,0:T(8,128)S(1)}, u32[]{:S(2)}, u32[]{:S(2)}) collective-permute-start(f32[80,128]{1,0:T(8,128)S(1)} %shard_map.55.mine.own), channel_id=1, source_target_pairs={{0,1},{1,0},{2,3},{3,2},{4,5},{5,4},{6,7},{7,6},{8,9},{9,8},{10,11... | collective-permute-start | bytes 122888 | tf_op jit(solution)/shard_map/ppermute | solution.py:299
  41.2 2.6 %collective-permute-done.5.z_one = f32[80,128]{1,0:T(8,128)S(1)} collective-permute-done((f32[80,128]{1,0:T(8,128)S(1)}, f32[80,128]{1,0:T(8,128)S(1)}, u32[]{:S(2)}, u32[]{:S(2)}) %collective-permute-start.5) | collective-permute-done | bytes 40992 | tf_op jit(solution)/shard_map/ppermute | solution.py:299
  43.8 8.1 %collective-permute-start.6 = (f32[96,128]{1,0:T(8,128)S(1)}, f32[96,128]{1,0:T(8,128)S(1)}, u32[]{:S(2)}, u32[]{:S(2)}) collective-permute-start(f32[96,128]{1,0:T(8,128)S(1)} %shard_map.56.z_one), channel_id=1, source_target_pairs={{0,3},{1,2},{2,1},{3,0},{4,7},{5,6},{6,5},{7,4},{8,11},{9,10},{10,... | collective-permute-start | bytes 147464 | tf_op jit(solution)/shard_map/ppermute | solution.py:299
  52.0 0.0 copy-start
  52.0 0.7 copy-done
  52.7 0.0 copy-start.1
  52.7 0.7 copy-done.1
  53.3 7.3 %near_one.1.before = f32[3,2048,128]{2,1,0:T(8,128)S(1)} custom-call(s32[8,8]{1,0:T(8,128)S(1)} %copy-done, s32[8]{0:T(128)S(1)} %copy-done.1, f32[72,128]{1,0:T(8,128)S(1)} %pack.1.refs_0_.own, f32[72,128]{1,0:T(8,128)S(1)} %collective-permute-done.refs_1_.wide_a, f32[72,128]{1,0:T(8,128)S(1)} %collective-permute-done.1.refs_2_.wide_b), custom_call_target="tpu_custom_call" | custom-call | flops 20971520 | bytes 262144 | tf_op jit(solution)/shard_map/near_one/pallas_call | solution.py:331
  60.6 7.3 %near_two.1 = (f32[3,2048,128]{2,1,0:T(8,128)S(1)}, f32[3,2048,128]{2,1,0:T(8,128)S(1)}) custom-call(s32[8,8]{1,0:T(8,128)S(1)} %copy-done, s32[8]{0:T(128)S(1)} %copy-done.1, f32[72,128]{1,0:T(8,128)S(1)} %collective-permute-done.2.refs_3_.wide_a, f32[72,128]{1,0:T(8,128)S(1)} %collective-permute-done.3.refs_4_.wide_b, ...), custom_call_target="tpu_custom_call", output_to_operand_aliasing={{1}: (6, {})} | custom-call | flops 20971520 | bytes 262144 | tf_op jit(solution)/shard_map/near_two/pallas_call | solution.py:343
  67.9 0.0 copy-start.2
  67.9 6.6 %near_three.1.before = f32[3,2048,128]{2,1,0:T(8,128)S(1)} custom-call(s32[8,8]{1,0:T(8,128)S(1)} %copy-done, s32[8]{0:T(128)S(1)} %copy-done.1, f32[96,128]{1,0:T(8,128)S(1)} %shard_map.56.z_one, f32[4,72,128]{2,1,0:T(8,128)S(1)} %all_to_all.5.y_all, f32[3,2048,128]{2,1,0:T(8,128)S(1)} %get-tuple-element.8.target_ref, ...), custom_call_target="tpu_custom_call", output_to_operand_aliasing={{}: (5, {})} | custom-call | flops 20971520 | bytes 262144 | tf_op jit(solution)/shard_map/near_three/pallas_call | solution.py:356
  74.6 0.0 collective-permute-done.6.z_two
  74.6 0.0 copy-done.2
  74.6 7.0 %last.1 = (f32[3,2048]{1,0:T(4,128)}, f32[3,2048,128]{2,1,0:T(8,128)S(1)}) custom-call(s32[8,8]{1,0:T(8,128)S(1)} %copy-done, s32[8,16]{1,0:T(8,128)S(1)} %copy-done.2, s32[8]{0:T(128)S(1)} %copy-done.1, f32[80,128]{1,0:T(8,128)S(1)} %shard_map.55.mine.own, f32[80,128]{1,0:T(8,128)S(1)} %collective-permute-done.5.z_one, ...), custom_call_target="tpu_custom_call", output_to_operand_aliasing={{1}: (7, {})} | custom-call | flops 20971520 | bytes 262144 | tf_op jit(solution)/shard_map/last/pallas_call | solution.py:367
  (2 shorter events, 0.0 us)
Async XLA Ops:
  1.0 19.0 %collective-permute-start = (f32[72,128]{1,0:T(8,128)S(1)}, f32[72,128]{1,0:T(8,128)S(1)}, u32[]{:S(2)}, u32[]{:S(2)}) collective-permute-start(f32[72,128]{1,0:T(8,128)S(1)} %pack.1.refs_0_.own), channel_id=1, source_target_pairs={{0,16},{16,0},{32,48},{48,32},{64,80},{80,64},{96,112},{112,96},{1... | collective-permute-start | bytes 110600 | tf_op jit(solution)/shard_map/ppermute | solution.py:299
  3.0 17.1 %collective-permute-start.1 = (f32[72,128]{1,0:T(8,128)S(1)}, f32[72,128]{1,0:T(8,128)S(1)}, u32[]{:S(2)}, u32[]{:S(2)}) collective-permute-start(f32[72,128]{1,0:T(8,128)S(1)} %pack.1.refs_0_.own), channel_id=1, source_target_pairs={{0,32},{16,48},{32,0},{48,16},{64,96},{80,112},{96,64},{112,80},{1... | collective-permute-start | bytes 110600 | tf_op jit(solution)/shard_map/ppermute | solution.py:299
  6.8 13.3 %collective-permute-start.2 = (f32[72,128]{1,0:T(8,128)S(1)}, f32[72,128]{1,0:T(8,128)S(1)}, u32[]{:S(2)}, u32[]{:S(2)}) collective-permute-start(f32[72,128]{1,0:T(8,128)S(1)} %pack.1.refs_0_.own), channel_id=1, source_target_pairs={{0,64},{16,80},{32,96},{48,112},{64,0},{80,16},{96,32},{112,48},{1... | collective-permute-start | bytes 110600 | tf_op jit(solution)/shard_map/ppermute | solution.py:299
  12.0 8.1 %collective-permute-start.3 = (f32[72,128]{1,0:T(8,128)S(1)}, f32[72,128]{1,0:T(8,128)S(1)}, u32[]{:S(2)}, u32[]{:S(2)}) collective-permute-start(f32[72,128]{1,0:T(8,128)S(1)} %pack.1.refs_0_.own), channel_id=1, source_target_pairs={{0,128},{16,144},{32,160},{48,176},{64,192},{80,208},{96,224},{112... | collective-permute-start | bytes 110600 | tf_op jit(solution)/shard_map/ppermute | solution.py:299
  15.4 7.4 %collective-permute-start.4 = (f32[72,128]{1,0:T(8,128)S(1)}, f32[72,128]{1,0:T(8,128)S(1)}, u32[]{:S(2)}, u32[]{:S(2)}) collective-permute-start(f32[72,128]{1,0:T(8,128)S(1)} %pack.1.refs_0_.own), channel_id=1, source_target_pairs={{0,256},{16,272},{32,288},{48,304},{64,320},{80,336},{96,352},{112... | collective-permute-start | bytes 110600 | tf_op jit(solution)/shard_map/ppermute | solution.py:299
  32.1 11.7 %collective-permute-start.5 = (f32[80,128]{1,0:T(8,128)S(1)}, f32[80,128]{1,0:T(8,128)S(1)}, u32[]{:S(2)}, u32[]{:S(2)}) collective-permute-start(f32[80,128]{1,0:T(8,128)S(1)} %shard_map.55.mine.own), channel_id=1, source_target_pairs={{0,1},{1,0},{2,3},{3,2},{4,5},{5,4},{6,7},{7,6},{8,9},{9,8},{10,11... | collective-permute-start | bytes 122888 | tf_op jit(solution)/shard_map/ppermute | solution.py:299
  43.8 30.7 %collective-permute-start.6 = (f32[96,128]{1,0:T(8,128)S(1)}, f32[96,128]{1,0:T(8,128)S(1)}, u32[]{:S(2)}, u32[]{:S(2)}) collective-permute-start(f32[96,128]{1,0:T(8,128)S(1)} %shard_map.56.z_one), channel_id=1, source_target_pairs={{0,3},{1,2},{2,1},{3,0},{4,7},{5,6},{6,5},{7,4},{8,11},{9,10},{10,... | collective-permute-start | bytes 147464 | tf_op jit(solution)/shard_map/ppermute | solution.py:299
  52.0 0.7 copy-start
  52.7 0.7 copy-start.1
  67.9 6.7 %copy-start.2 = (s32[8,16]{1,0:T(8,128)S(1)}, s32[8,16]{1,0:T(8,128)}, u32[]{:S(2)}) copy-start(s32[8,16]{1,0:T(8,128)} %far_ref.1) | copy-start | bytes 1540

commit v2 on v1

--- a/solution.py
+++ b/solution.py
@@ -1,3 +1,5 @@
+import functools
+
 import jax
 import jax.numpy as jnp
 from jax import lax
@@ -11,6 +13,7 @@
 BLK = 8
 LEAF = 256
 BODY = BLK * 8
+GROUPS = 8
 SLOT = 16
 F32 = jnp.float32
 I32 = jnp.int32
@@ -18,6 +21,8 @@
 SMEM = pl.BlockSpec(memory_space=pltpu.SMEM)
 HBM = pl.BlockSpec(memory_space=pltpu.HBM)
 RELAY = (3, 2, 1, 0)
+COUNT = 16
+STAGES = ((0, 5, 6), (7, 8, 9), (1, 3, 4), (2,))
 
 
 def planes(ref):
@@ -25,11 +30,9 @@
     return [jnp.concatenate(pair, axis=1) for pair in half]
 
 
-def pack_kernel(counts_hbm, pos_hbm, mass_hbm, out_ref, counts_ref, pos_ref, mass_ref, sems):
-    copies = [
-        pltpu.make_async_copy(src, dst, sems.at[i])
-        for i, (src, dst) in enumerate(((pos_hbm, pos_ref), (mass_hbm, mass_ref), (counts_hbm, counts_ref)))
-    ]
+def pack_kernel(counts_hbm, pos_hbm, mass_hbm, near_hbm, out_ref, control_ref, counts_ref, pos_ref, mass_ref, near_ref, sems):
+    moves = ((pos_hbm, pos_ref), (mass_hbm, mass_ref), (counts_hbm, counts_ref), (near_hbm, near_ref))
+    copies = [pltpu.make_async_copy(src, dst, sems.at[i]) for i, (src, dst) in enumerate(moves)]
     for copy in copies:
         copy.start()
     for copy in copies:
@@ -67,6 +70,18 @@
 
     rows = jnp.where(blocks == 0, cell_row(first), 0.0)
     out_ref[BODY:, :] = jnp.where(blocks == 1, cell_row(last), rows)
+    code = near_ref[...]
+    level = code // BLK
+    entry = jnp.zeros_like(code)
+    for stage, names in enumerate(STAGES):
+        for place, name in enumerate(names):
+            entry = jnp.where(level == name, stage * 4096 + place * BODY, entry)
+    entry = entry + code % BLK * 8
+    control = jnp.concatenate([entry, jnp.zeros((BLK, 128 - entry.shape[1]), I32)], axis=1)
+    count = jnp.zeros((BLK, 128), I32)
+    for b in range(BLK):
+        count = jnp.where(blocks == b, counts_ref[b], count)
+    control_ref[...] = jnp.where(lanes == COUNT, count, control)
 
 
 def join_kernel(*refs):
@@ -86,32 +101,35 @@
 
 
 def spread_targets(own, target_ref):
+    k = lax.broadcasted_iota(I32, (3 * BLK, BLK * 128), 0)
+    n = lax.broadcasted_iota(I32, (3 * BLK, BLK * 128), 1)
+    ones = (k % BLK == n // 128).astype(F32).astype(jnp.bfloat16)
     for c, plane in enumerate(planes(own)[:3]):
-        columns = plane.T
+        parts = jnp.concatenate([part.astype(F32) for part in three_parts(plane)], axis=0).astype(jnp.bfloat16)
+        spread = lax.dot_general(parts, ones, (((0,), (0,)), ((), ())), preferred_element_type=F32)
         for b in range(BLK):
-            target_ref[c, b * LEAF : (b + 1) * LEAF, :] = jnp.broadcast_to(columns[:, b : b + 1], (LEAF, 128))
-
-
-def near_part(near_ref, counts_ref, target_ref, sums_ref, source_ref, bodies, levels):
+            target_ref[c, b * LEAF : (b + 1) * LEAF, :] = spread[:, b * 128 : (b + 1) * 128]
+
+
+def near_part(control_ref, target_ref, sums_ref, source_ref, masks_ref, bodies, stage, entries):
     lane8 = lax.broadcasted_iota(I32, (BLK, 128), 1)
     block8 = lax.broadcasted_iota(I32, (BLK, 128), 0)
-    masks = []
     for s, body in enumerate(bodies):
         for b in range(BLK):
             source_ref[s * BODY + b * 8 : s * BODY + b * 8 + 8, :] = body(b)
+    for s in range(len(bodies)):
         second = source_ref[pl.ds(s * BODY + 7, BLK, stride=8), :]
-        masks.append(jnp.sum(jnp.where((lane8 == 0) & (second > 0.0), jnp.left_shift(1, block8), 0)))
-    entries = near_ref.shape[1]
-
-    def run(row, first, count, groups, halves):
+        masks_ref[s] = jnp.sum(jnp.where((lane8 == 0) & (second > 0.0), jnp.left_shift(1, block8), 0))
+
+    def run(row, first, count, halves):
         s = [
             [jnp.broadcast_to(source_ref[pl.ds(row + 4 * h + c, 1), :], (8, 128)) for c in range(4)]
             for h in range(halves)
         ]
 
         def chunk(g, carry):
-            start = pl.multiple_of(first + g * (8 * groups), 8)
-            for i in range(groups):
+            start = pl.multiple_of(first + g * (8 * GROUPS), 8)
+            for i in range(GROUPS):
                 at = pl.ds(start + 8 * i, 8)
                 t = [target_ref[c, at, :] for c in range(3)]
                 sums = [sums_ref[c, at, :] for c in range(3)]
@@ -124,62 +142,55 @@
                     sums_ref[c, at, :] = sums[c]
             return carry
 
-        lax.fori_loop(0, (count + 8 * groups - 1) // (8 * groups), chunk, 0)
-
-    def item(k, carry):
-        b = k // entries
-        code = near_ref[b, k % entries]
-        level, slot = code // BLK, code % BLK
-        local = jnp.int32(-1)
-        mask = jnp.int32(0)
-        for s, name in enumerate(levels):
-            local = jnp.where(level == name, s, local)
-            mask = jnp.where(level == name, masks[s], mask)
-        row = local * BODY + slot * 8
-        both = jnp.right_shift(mask, slot) % 2 == 1
-        first, count = b * LEAF, counts_ref[b]
-
-        @pl.when((local >= 0) & both)
-        def _():
-            run(row, first, count, 4, 2)
-
-        @pl.when((local >= 0) & jnp.logical_not(both))
-        def _():
-            run(row, first, count, 8, 1)
+        lax.fori_loop(0, (count + 8 * GROUPS - 1) // (8 * GROUPS), chunk, 0)
+
+    def block(b, carry):
+        first, count = b * LEAF, control_ref[b, COUNT]
+        for v in range(entries):
+            entry = control_ref[b, v]
+            row = entry % 4096
+            both = jnp.right_shift(masks_ref[row // BODY], row // 8 % BLK) % 2
+
+            @pl.when(entry // 4096 == stage)
+            def _():
+                @pl.when(both == 1)
+                def _():
+                    run(row, first, count, 2)
+
+                @pl.when(both == 0)
+                def _():
+                    run(row, first, count, 1)
 
         return carry
 
-    lax.fori_loop(0, BLK * entries, item, 0)
+    lax.fori_loop(0, BLK, block, 0)
 
 
 def block_of(ref):
     return lambda b: ref[b * 8 : b * 8 + 8, :]
 
 
-LEVELS_ONE, LEVELS_TWO, LEVELS_THREE, LEVELS_LAST = (0, 5, 6), (7, 8, 9), (1, 3, 4), (2,)
-
-
-def near_one_kernel(near_ref, counts_ref, own, wide_a, wide_b, sums_ref, target_ref, source_ref):
+def near_one_kernel(control_ref, own, wide_a, wide_b, sums_ref, target_ref, source_ref, masks_ref, *, entries):
     spread_targets(own, target_ref)
     sums_ref[...] = jnp.zeros_like(sums_ref)
     bodies = [*map(block_of, (own, wide_a, wide_b))]
-    near_part(near_ref, counts_ref, target_ref, sums_ref, source_ref, bodies, LEVELS_ONE)
-
-
-def near_two_kernel(near_ref, counts_ref, wide_a, wide_b, wide_c, mine, before, target_ref, sums_ref, source_ref):
+    near_part(control_ref, target_ref, sums_ref, source_ref, masks_ref, bodies, 0, entries)
+
+
+def near_two_kernel(control_ref, wide_a, wide_b, wide_c, mine, before, target_ref, sums_ref, source_ref, masks_ref, *, entries):
     spread_targets(mine, target_ref)
     bodies = [*map(block_of, (wide_a, wide_b, wide_c))]
-    near_part(near_ref, counts_ref, target_ref, sums_ref, source_ref, bodies, LEVELS_TWO)
-
-
-def near_three_kernel(near_ref, counts_ref, z_one, y_all, target_ref, before, sums_ref, source_ref):
+    near_part(control_ref, target_ref, sums_ref, source_ref, masks_ref, bodies, 1, entries)
+
+
+def near_three_kernel(control_ref, z_one, y_all, target_ref, before, sums_ref, source_ref, masks_ref, *, entries):
     y = lax.axis_index("oct") // 4
 
     def member(flip):
         return lambda b: y_all[y ^ flip, b * 8 : b * 8 + 8, :]
 
     bodies = [block_of(z_one), member(1), member(2)]
-    near_part(near_ref, counts_ref, target_ref, sums_ref, source_ref, bodies, LEVELS_THREE)
+    near_part(control_ref, target_ref, sums_ref, source_ref, masks_ref, bodies, 2, entries)
 
 
 def three_parts(a):
@@ -189,8 +200,8 @@
     return hi, mid, (rest - mid.astype(F32)).astype(jnp.bfloat16)
 
 
-def last_kernel(near_ref, far_ref, counts_ref, own, z_one, z_two, target_ref, before, out_ref, sums_ref, table_ref, rows_ref, source_ref):
-    near_part(near_ref, counts_ref, target_ref, sums_ref, source_ref, [block_of(z_two)], LEVELS_LAST)
+def last_kernel(control_ref, far_ref, own, z_one, z_two, target_ref, before, out_ref, sums_ref, table_ref, rows_ref, source_ref, masks_ref, *, entries):
+    near_part(control_ref, target_ref, sums_ref, source_ref, masks_ref, [block_of(z_two)], 3, entries)
     sums = []
     lane8 = lax.broadcasted_iota(I32, (LEAF, BLK), 1)
     for c in range(3):
@@ -253,15 +264,15 @@
         sums[1] += ry * radial + qy * inv5
         sums[2] += rz * radial + qz * inv5
     lane = lax.broadcasted_iota(I32, (1, LEAF), 1)
-    grav = 1.0 / (near_ref.shape[1] * LEAF)
+    grav = 1.0 / (entries * LEAF)
     for c in range(3):
         rows_ref[c] = sums[c] * grav
         for b in range(BLK):
-            out_ref[c : c + 1, b * LEAF : (b + 1) * LEAF] = jnp.where(lane < counts_ref[b], rows_ref[c, b : b + 1, :], 0.0)
+            out_ref[c : c + 1, b * LEAF : (b + 1) * LEAF] = jnp.where(lane < control_ref[b, COUNT], rows_ref[c, b : b + 1, :], 0.0)
 
 
 def sources(sets):
-    return pltpu.VMEM((sets * BODY, 128), F32)
+    return [pltpu.VMEM((sets * BODY, 128), F32), pltpu.SMEM((4,), I32)]
 
 
 def params(mib):
@@ -302,21 +313,25 @@
 def step(positions, masses, counts, near_list, far_list):
     wide_bits = lax.axis_size("wide").bit_length() - 1
     shape = (BODY + 8, 128)
-    own = pl.pallas_call(
+    entries = near_list.shape[1]
+    own, control = pl.pallas_call(
         pack_kernel,
-        out_shape=jax.ShapeDtypeStruct(shape, F32),
-        in_specs=[HBM, HBM, HBM],
-        out_specs=VMEM,
+        out_shape=[jax.ShapeDtypeStruct(shape, F32), jax.ShapeDtypeStruct((BLK, 128), I32)],
+        in_specs=[HBM] * 4,
+        out_specs=[VMEM, VMEM],
         scratch_shapes=[
             pltpu.SMEM(counts.shape, I32),
             pltpu.VMEM(positions.shape, F32),
             pltpu.VMEM((16, 128), F32),
-            pltpu.SemaphoreType.DMA((3,)),
+            pltpu.VMEM(near_list.shape, I32),
+            pltpu.SemaphoreType.DMA((4,)),
         ],
         compiler_params=params(4),
         name="pack",
-    )(*(pltpu.with_memory_space_constraint(a, pltpu.HBM) for a in (counts, positions, masses.reshape(16, 128))))
-    wide = [exchange(own, "wide", lambda i, bit=bit: i ^ (1 << bit)) for bit in range(wide_bits)]
+    )(*(pltpu.with_memory_space_constraint(a, pltpu.HBM) for a in (counts, positions, masses.reshape(16, 128), near_list)))
+    wide = []
+    for bit in range(wide_bits):
+        wide.append(exchange(own, "wide", lambda i, bit=bit: i ^ (1 << bit)))
     message = pl.pallas_call(
         join_kernel,
         out_shape=jax.ShapeDtypeStruct((4, *shape), F32),
@@ -329,56 +344,56 @@
     y_all = lax.all_to_all(message, "oct", 0, 0, axis_index_groups=y_groups)
     state = jax.ShapeDtypeStruct((3, BLK * LEAF, 128), F32)
     sums = pl.pallas_call(
-        near_one_kernel,
+        functools.partial(near_one_kernel, entries=entries),
         out_shape=state,
-        in_specs=[SMEM, SMEM] + [VMEM] * 3,
+        in_specs=[SMEM] + [VMEM] * 3,
         out_specs=VMEM,
-        scratch_shapes=[pltpu.VMEM(state.shape, F32), sources(3)],
+        scratch_shapes=[pltpu.VMEM(state.shape, F32), *sources(3)],
         compiler_params=params(8),
         cost_estimate=cost(20 << 20),
         name="near_one",
-    )(near_list, counts, own, wide[0], wide[1])
+    )(control, own, wide[0], wide[1])
     mine = small_call(mine_kernel, BODY + 16, own, y_all)
     z_one = exchange(mine, "oct", lambda i: i ^ 1)
     targets, sums = pl.pallas_call(
-        near_two_kernel,
+        functools.partial(near_two_kernel, entries=entries),
         out_shape=[state, state],
-        in_specs=[SMEM, SMEM] + [VMEM] * 5,
+        in_specs=[SMEM] + [VMEM] * 5,
         out_specs=[VMEM, VMEM],
-        scratch_shapes=[sources(3)],
-        input_output_aliases={6: 1},
+        scratch_shapes=sources(3),
+        input_output_aliases={5: 1},
         compiler_params=params(8),
         cost_estimate=cost(20 << 20),
         name="near_two",
-    )(near_list, counts, *wide[2:], mine, sums)
+    )(control, *wide[2:], mine, sums)
     relay = small_call(relay_kernel, BODY + 32, mine, z_one)
     z_two = exchange(relay, "oct", lambda i: (i & ~3) | RELAY[i & 3])
     sums = pl.pallas_call(
-        near_three_kernel,
+        functools.partial(near_three_kernel, entries=entries),
         out_shape=state,
-        in_specs=[SMEM, SMEM] + [VMEM] * 4,
+        in_specs=[SMEM] + [VMEM] * 4,
         out_specs=VMEM,
-        scratch_shapes=[sources(3)],
-        input_output_aliases={5: 0},
+        scratch_shapes=sources(3),
+        input_output_aliases={4: 0},
         compiler_params=params(8),
         cost_estimate=cost(20 << 20),
         name="near_three",
-    )(near_list, counts, relay, y_all, targets, sums)
+    )(control, relay, y_all, targets, sums)
     return pl.pallas_call(
-        last_kernel,
+        functools.partial(last_kernel, entries=entries),
         out_shape=[jax.ShapeDtypeStruct(positions.shape, F32), state],
-        in_specs=[SMEM, VMEM, SMEM] + [VMEM] * 5,
+        in_specs=[SMEM] + [VMEM] * 6,
         out_specs=[VMEM, VMEM],
         scratch_shapes=[
             pltpu.VMEM((64, 128), F32),
             pltpu.VMEM((3, BLK, LEAF), F32),
-            sources(1),
+            *sources(1),
         ],
-        input_output_aliases={7: 1},
+        input_output_aliases={6: 1},
         compiler_params=params(8),
         cost_estimate=cost(20 << 20),
         name="last",
-    )(near_list, far_list, counts, mine, z_one, z_two, targets, sums)[0]
+    )(control, far_list, mine, z_one, z_two, targets, sums)[0]
 
 
 def solution(mesh):

time: 82 us -> 75.8 us (0.924)
  the two profiles are of different devices: /device:TPU:8 before, /device:TPU:32 now
where the time goes in v2:
time: 75.8 us; the launch traced here: 75.4 us
  starting transfers between devices  35.2 us (46%)
  Pallas kernels  24.4 us (32%)
  blocking collectives  9.71 us (13%)
  waiting for transfers between devices  5.97 us (8%)
    ppermute x7, starting transfers between devices, exchange(): lax.ppermute(payload, axis, [(i, flip(i)) for i in range(lax.axis_size(ax...  35.2 us
    all_to_all x1, blocking collectives, step(): y_all = lax.all_to_all(message, 'oct', 0, 0, axis_index_groups=y_groups)  9.71 us
    ppermute x7, waiting for transfers between devices, exchange(): lax.ppermute(payload, axis, [(i, flip(i)) for i in range(lax.axis_size(ax...  5.97 us
    pallas_call x1, Pallas kernels, step(): pl.pallas_call(functools.partial(near_three_kernel, entries=entries), out...  5.86 us
    pallas_call x1, Pallas kernels, step(): pl.pallas_call(functools.partial(last_kernel, entries=entries), out_shape...  5.84 us
    pallas_call x1, Pallas kernels, step(): pl.pallas_call(functools.partial(near_one_kernel, entries=entries), out_s...  5.84 us
    pallas_call x1, Pallas kernels, step(): pl.pallas_call(functools.partial(near_two_kernel, entries=entries), out_s...  5.71 us
  transfers between devices with their start and end apart: 7, of which 2 were waited for; matrix products, arithmetic and copies ran while one was open for 0% of the time, Pallas kernels for 23%

profile of v2, /device:TPU:32, one launch (start us, length us, event | category | flops | bytes accessed | tf_op | source)
XLA Modules:
  0.0 75.4 jit_solution(5180887592843431966)
XLA Ops:
  0.0 1.0 %pack.1 = (f32[72,128]{1,0:T(8,128)S(1)}, s32[8,128]{1,0:T(8,128)S(1)}) custom-call(s32[8]{0:T(128)} %counts_hbm.1, f32[3,2048]{1,0:T(4,128)} %pos_hbm.1, f32[16,128]{1,0:T(8,128)} %bitcast.1, s32[8,8]{1,0:T(8,128)} %near_hbm.1), custom_call_target="tpu_custom_call" | custom-call | tf_op jit(solution)/shard_map/pack/pallas_call | solution.py:317
  1.0 1.9 %collective-permute-start = (f32[72,128]{1,0:T(8,128)S(1)}, f32[72,128]{1,0:T(8,128)S(1)}, u32[]{:S(2)}, u32[]{:S(2)}) collective-permute-start(f32[72,128]{1,0:T(8,128)S(1)} %get-tuple-element.11.refs_0_.own), channel_id=1, source_target_pairs={{0,16},{16,0},{32,48},{48,32},{64,80},{80,64},{96,112},{112,96},{1... | collective-permute-start | bytes 110600 | tf_op jit(solution)/shard_map/ppermute | solution.py:310
  3.0 7.4 %collective-permute-start.1 = (f32[72,128]{1,0:T(8,128)S(1)}, f32[72,128]{1,0:T(8,128)S(1)}, u32[]{:S(2)}, u32[]{:S(2)}) collective-permute-start(f32[72,128]{1,0:T(8,128)S(1)} %get-tuple-element.11.refs_0_.own), channel_id=1, source_target_pairs={{0,32},{16,48},{32,0},{48,16},{64,96},{80,112},{96,64},{112,80},{1... | collective-permute-start | bytes 110600 | tf_op jit(solution)/shard_map/ppermute | solution.py:310
  10.3 1.9 %collective-permute-start.2 = (f32[72,128]{1,0:T(8,128)S(1)}, f32[72,128]{1,0:T(8,128)S(1)}, u32[]{:S(2)}, u32[]{:S(2)}) collective-permute-start(f32[72,128]{1,0:T(8,128)S(1)} %get-tuple-element.11.refs_0_.own), channel_id=1, source_target_pairs={{0,64},{16,80},{32,96},{48,112},{64,0},{80,16},{96,32},{112,48},{1... | collective-permute-start | bytes 110600 | tf_op jit(solution)/shard_map/ppermute | solution.py:310
  12.3 1.9 %collective-permute-start.3 = (f32[72,128]{1,0:T(8,128)S(1)}, f32[72,128]{1,0:T(8,128)S(1)}, u32[]{:S(2)}, u32[]{:S(2)}) collective-permute-start(f32[72,128]{1,0:T(8,128)S(1)} %get-tuple-element.11.refs_0_.own), channel_id=1, source_target_pairs={{0,128},{16,144},{32,160},{48,176},{64,192},{80,208},{96,224},{112... | collective-permute-start | bytes 110600 | tf_op jit(solution)/shard_map/ppermute | solution.py:310
  14.2 4.0 %collective-permute-start.4 = (f32[72,128]{1,0:T(8,128)S(1)}, f32[72,128]{1,0:T(8,128)S(1)}, u32[]{:S(2)}, u32[]{:S(2)}) collective-permute-start(f32[72,128]{1,0:T(8,128)S(1)} %get-tuple-element.11.refs_0_.own), channel_id=1, source_target_pairs={{0,256},{16,272},{32,288},{48,304},{64,320},{80,336},{96,352},{112... | collective-permute-start | bytes 110600 | tf_op jit(solution)/shard_map/ppermute | solution.py:310
  18.2 0.0 collective-permute-done.refs_1_.wide_a
  18.2 0.0 collective-permute-done.1.refs_2_.wide_b
  18.3 0.0 collective-permute-done.2.refs_3_.wide_a
  18.3 0.0 collective-permute-done.3.refs_4_.wide_b
  18.3 3.3 %collective-permute-done.4.refs_5_.wide_c = f32[72,128]{1,0:T(8,128)S(1)} collective-permute-done((f32[72,128]{1,0:T(8,128)S(1)}, f32[72,128]{1,0:T(8,128)S(1)}, u32[]{:S(2)}, u32[]{:S(2)}) %collective-permute-start.4) | collective-permute-done | bytes 36896 | tf_op jit(solution)/shard_map/ppermute | solution.py:310
  21.6 0.1 join.1
  21.6 9.7 %all_to_all.5.y_all = f32[4,72,128]{2,1,0:T(8,128)S(1)} all-to-all(f32[4,72,128]{2,1,0:T(8,128)S(1)} %join.1), channel_id=1, replica_groups={{0,4,8,12},{1,5,9,13},{2,6,10,14},{3,7,11,15},{16,20,24,28},{17,21,25,2..., dimensions={0} | all-to-all | bytes 294912 | tf_op jit(solution)/shard_map/all_to_all | solution.py:344
  31.3 9.1 %collective-permute-start.5 = (f32[80,128]{1,0:T(8,128)S(1)}, f32[80,128]{1,0:T(8,128)S(1)}, u32[]{:S(2)}, u32[]{:S(2)}) collective-permute-start(f32[80,128]{1,0:T(8,128)S(1)} %shard_map.55.mine.own), channel_id=1, source_target_pairs={{0,1},{1,0},{2,3},{3,2},{4,5},{5,4},{6,7},{7,6},{8,9},{9,8},{10,11... | collective-permute-start | bytes 122888 | tf_op jit(solution)/shard_map/ppermute | solution.py:310
  40.4 2.7 %collective-permute-done.5.z_one = f32[80,128]{1,0:T(8,128)S(1)} collective-permute-done((f32[80,128]{1,0:T(8,128)S(1)}, f32[80,128]{1,0:T(8,128)S(1)}, u32[]{:S(2)}, u32[]{:S(2)}) %collective-permute-start.5) | collective-permute-done | bytes 40992 | tf_op jit(solution)/shard_map/ppermute | solution.py:310
  43.1 9.0 %collective-permute-start.6 = (f32[96,128]{1,0:T(8,128)S(1)}, f32[96,128]{1,0:T(8,128)S(1)}, u32[]{:S(2)}, u32[]{:S(2)}) collective-permute-start(f32[96,128]{1,0:T(8,128)S(1)} %shard_map.56.z_one), channel_id=1, source_target_pairs={{0,3},{1,2},{2,1},{3,0},{4,7},{5,6},{6,5},{7,4},{8,11},{9,10},{10,... | collective-permute-start | bytes 147464 | tf_op jit(solution)/shard_map/ppermute | solution.py:310
  52.1 5.8 %near_one.1.before = f32[3,2048,128]{2,1,0:T(8,128)S(1)} custom-call(s32[8,128]{1,0:T(8,128)S(1)} %get-tuple-element.10.control_ref, f32[72,128]{1,0:T(8,128)S(1)} %get-tuple-element.11.refs_0_.own, f32[72,128]{1,0:T(8,128)S(1)} %collective-permute-done.refs_1_.wide_a, f32[72,128]{1,0:T(8,128)S(1)} %collective-permute-done.1.refs_2_.wide_b), custom_call_target="tpu_custom_call" | custom-call | flops 20971520 | bytes 262144 | tf_op jit(solution)/shard_map/near_one/pallas_call | solution.py:346
  57.9 5.7 %near_two.1 = (f32[3,2048,128]{2,1,0:T(8,128)S(1)}, f32[3,2048,128]{2,1,0:T(8,128)S(1)}) custom-call(s32[8,128]{1,0:T(8,128)S(1)} %get-tuple-element.10.control_ref, f32[72,128]{1,0:T(8,128)S(1)} %collective-permute-done.2.refs_3_.wide_a, f32[72,128]{1,0:T(8,128)S(1)} %collective-permute-done.3.refs_4_.wide_b, ...), custom_call_target="tpu_custom_call", output_to_operand_aliasing={{1}: (5, {})} | custom-call | flops 20971520 | bytes 262144 | tf_op jit(solution)/shard_map/near_two/pallas_call | solution.py:358
  63.7 0.0 copy-start
  63.7 5.9 %near_three.1.before = f32[3,2048,128]{2,1,0:T(8,128)S(1)} custom-call(s32[8,128]{1,0:T(8,128)S(1)} %get-tuple-element.10.control_ref, f32[96,128]{1,0:T(8,128)S(1)} %shard_map.56.z_one, f32[4,72,128]{2,1,0:T(8,128)S(1)} %all_to_all.5.y_all, f32[3,2048,128]{2,1,0:T(8,128)S(1)} %get-tuple-element.12.target_ref, ...), custom_call_target="tpu_custom_call", output_to_operand_aliasing={{}: (4, {})} | custom-call | flops 20971520 | bytes 262144 | tf_op jit(solution)/shard_map/near_three/pallas_call | solution.py:371
  69.5 0.0 collective-permute-done.6.z_two
  69.6 0.0 copy-done
  69.6 5.8 %last.1 = (f32[3,2048]{1,0:T(4,128)}, f32[3,2048,128]{2,1,0:T(8,128)S(1)}) custom-call(s32[8,128]{1,0:T(8,128)S(1)} %get-tuple-element.10.control_ref, s32[8,16]{1,0:T(8,128)S(1)} %copy-done, f32[80,128]{1,0:T(8,128)S(1)} %shard_map.55.mine.own, f32[80,128]{1,0:T(8,128)S(1)} %collective-permute-done.5.z_one, ...), custom_call_target="tpu_custom_call", output_to_operand_aliasing={{1}: (6, {})} | custom-call | flops 20971520 | bytes 262144 | tf_op jit(solution)/shard_map/last/pallas_call | solution.py:382
  (2 shorter events, 0.0 us)
Async XLA Ops:
  1.0 17.2 %collective-permute-start = (f32[72,128]{1,0:T(8,128)S(1)}, f32[72,128]{1,0:T(8,128)S(1)}, u32[]{:S(2)}, u32[]{:S(2)}) collective-permute-start(f32[72,128]{1,0:T(8,128)S(1)} %get-tuple-element.11.refs_0_.own), channel_id=1, source_target_pairs={{0,16},{16,0},{32,48},{48,32},{64,80},{80,64},{96,112},{112,96},{1... | collective-permute-start | bytes 110600 | tf_op jit(solution)/shard_map/ppermute | solution.py:310
  3.0 15.3 %collective-permute-start.1 = (f32[72,128]{1,0:T(8,128)S(1)}, f32[72,128]{1,0:T(8,128)S(1)}, u32[]{:S(2)}, u32[]{:S(2)}) collective-permute-start(f32[72,128]{1,0:T(8,128)S(1)} %get-tuple-element.11.refs_0_.own), channel_id=1, source_target_pairs={{0,32},{16,48},{32,0},{48,16},{64,96},{80,112},{96,64},{112,80},{1... | collective-permute-start | bytes 110600 | tf_op jit(solution)/shard_map/ppermute | solution.py:310
  10.3 7.9 %collective-permute-start.2 = (f32[72,128]{1,0:T(8,128)S(1)}, f32[72,128]{1,0:T(8,128)S(1)}, u32[]{:S(2)}, u32[]{:S(2)}) collective-permute-start(f32[72,128]{1,0:T(8,128)S(1)} %get-tuple-element.11.refs_0_.own), channel_id=1, source_target_pairs={{0,64},{16,80},{32,96},{48,112},{64,0},{80,16},{96,32},{112,48},{1... | collective-permute-start | bytes 110600 | tf_op jit(solution)/shard_map/ppermute | solution.py:310
  12.3 6.0 %collective-permute-start.3 = (f32[72,128]{1,0:T(8,128)S(1)}, f32[72,128]{1,0:T(8,128)S(1)}, u32[]{:S(2)}, u32[]{:S(2)}) collective-permute-start(f32[72,128]{1,0:T(8,128)S(1)} %get-tuple-element.11.refs_0_.own), channel_id=1, source_target_pairs={{0,128},{16,144},{32,160},{48,176},{64,192},{80,208},{96,224},{112... | collective-permute-start | bytes 110600 | tf_op jit(solution)/shard_map/ppermute | solution.py:310
  14.2 7.4 %collective-permute-start.4 = (f32[72,128]{1,0:T(8,128)S(1)}, f32[72,128]{1,0:T(8,128)S(1)}, u32[]{:S(2)}, u32[]{:S(2)}) collective-permute-start(f32[72,128]{1,0:T(8,128)S(1)} %get-tuple-element.11.refs_0_.own), channel_id=1, source_target_pairs={{0,256},{16,272},{32,288},{48,304},{64,320},{80,336},{96,352},{112... | collective-permute-start | bytes 110600 | tf_op jit(solution)/shard_map/ppermute | solution.py:310
  31.3 11.8 %collective-permute-start.5 = (f32[80,128]{1,0:T(8,128)S(1)}, f32[80,128]{1,0:T(8,128)S(1)}, u32[]{:S(2)}, u32[]{:S(2)}) collective-permute-start(f32[80,128]{1,0:T(8,128)S(1)} %shard_map.55.mine.own), channel_id=1, source_target_pairs={{0,1},{1,0},{2,3},{3,2},{4,5},{5,4},{6,7},{7,6},{8,9},{9,8},{10,11... | collective-permute-start | bytes 122888 | tf_op jit(solution)/shard_map/ppermute | solution.py:310
  43.1 26.4 %collective-permute-start.6 = (f32[96,128]{1,0:T(8,128)S(1)}, f32[96,128]{1,0:T(8,128)S(1)}, u32[]{:S(2)}, u32[]{:S(2)}) collective-permute-start(f32[96,128]{1,0:T(8,128)S(1)} %shard_map.56.z_one), channel_id=1, source_target_pairs={{0,3},{1,2},{2,1},{3,0},{4,7},{5,6},{6,5},{7,4},{8,11},{9,10},{10,... | collective-permute-start | bytes 147464 | tf_op jit(solution)/shard_map/ppermute | solution.py:310
  63.7 5.9 %copy-start = (s32[8,16]{1,0:T(8,128)S(1)}, s32[8,16]{1,0:T(8,128)}, u32[]{:S(2)}) copy-start(s32[8,16]{1,0:T(8,128)} %far_ref.1) | copy-start | bytes 1540

commit v3 on v2

--- a/solution.py
+++ b/solution.py
@@ -21,7 +21,8 @@
 SMEM = pl.BlockSpec(memory_space=pltpu.SMEM)
 HBM = pl.BlockSpec(memory_space=pltpu.HBM)
 RELAY = (3, 2, 1, 0)
-COUNT = 16
+COUNT = 127
+ITEMS = 64
 STAGES = ((0, 5, 6), (7, 8, 9), (1, 3, 4), (2,))
 
 
@@ -71,17 +72,30 @@
     rows = jnp.where(blocks == 0, cell_row(first), 0.0)
     out_ref[BODY:, :] = jnp.where(blocks == 1, cell_row(last), rows)
     code = near_ref[...]
-    level = code // BLK
-    entry = jnp.zeros_like(code)
-    for stage, names in enumerate(STAGES):
+    entries = code.shape[1]
+    stage = jnp.zeros_like(code)
+    value = lax.broadcasted_iota(I32, code.shape, 0) * 32 + code % BLK
+    for number, names in enumerate(STAGES):
         for place, name in enumerate(names):
-            entry = jnp.where(level == name, stage * 4096 + place * BODY, entry)
-    entry = entry + code % BLK * 8
-    control = jnp.concatenate([entry, jnp.zeros((BLK, 128 - entry.shape[1]), I32)], axis=1)
-    count = jnp.zeros((BLK, 128), I32)
+            stage = jnp.where(code // BLK == name, number, stage)
+            value = value + jnp.where(code // BLK == name, place * BLK, 0)
+
+    def column(a):
+        return jnp.concatenate([jnp.broadcast_to(a[:, v : v + 1], (BLK, 128)) for v in range(entries)], axis=0).astype(F32)
+
+    stages = column(stage)
+    items = BLK * entries
+    down = lax.broadcasted_iota(I32, (items, 128), 0).astype(F32)
+    across = lax.broadcasted_iota(I32, (items, 128), 1).astype(F32)
+    key = stages * items + down
+    rank = jnp.sum((key.T[:items, :] < key[:, :items]).astype(F32), axis=1, keepdims=True)
+    sorted_items = jnp.where(rank == across, column(value), 0.0)
+    starts = (stages < across - ITEMS).astype(F32)
+    row = jnp.sum(jnp.where(across < ITEMS, sorted_items, starts), axis=0, keepdims=True).astype(I32)
+    control = jnp.where(blocks == 0, row, 0)
     for b in range(BLK):
-        count = jnp.where(blocks == b, counts_ref[b], count)
-    control_ref[...] = jnp.where(lanes == COUNT, count, control)
+        control = jnp.where((blocks == b) & (lanes == COUNT), counts_ref[b], control)
+    control_ref[...] = control
 
 
 def join_kernel(*refs):
@@ -111,7 +125,7 @@
             target_ref[c, b * LEAF : (b + 1) * LEAF, :] = spread[:, b * 128 : (b + 1) * 128]
 
 
-def near_part(control_ref, target_ref, sums_ref, source_ref, masks_ref, bodies, stage, entries):
+def near_part(control_ref, target_ref, sums_ref, source_ref, masks_ref, bodies, stage):
     lane8 = lax.broadcasted_iota(I32, (BLK, 128), 1)
     block8 = lax.broadcasted_iota(I32, (BLK, 128), 0)
     for s, body in enumerate(bodies):
@@ -144,72 +158,117 @@
 
         lax.fori_loop(0, (count + 8 * GROUPS - 1) // (8 * GROUPS), chunk, 0)
 
-    def block(b, carry):
+    def item(k, carry):
+        value = control_ref[0, k]
+        b, place = value // 32, value % 32
+        row = place * 8
         first, count = b * LEAF, control_ref[b, COUNT]
-        for v in range(entries):
-            entry = control_ref[b, v]
-            row = entry % 4096
-            both = jnp.right_shift(masks_ref[row // BODY], row // 8 % BLK) % 2
-
-            @pl.when(entry // 4096 == stage)
-            def _():
-                @pl.when(both == 1)
-                def _():
-                    run(row, first, count, 2)
-
-                @pl.when(both == 0)
-                def _():
-                    run(row, first, count, 1)
+        both = jnp.right_shift(masks_ref[place // BLK], place % BLK) % 2
+
+        @pl.when(both == 1)
+        def _():
+            run(row, first, count, 2)
+
+        @pl.when(both == 0)
+        def _():
+            run(row, first, count, 1)
 
         return carry
 
-    lax.fori_loop(0, BLK, block, 0)
+    lax.fori_loop(control_ref[0, ITEMS + stage], control_ref[0, ITEMS + stage + 1], item, 0)
 
 
 def block_of(ref):
     return lambda b: ref[b * 8 : b * 8 + 8, :]
 
 
-def near_one_kernel(control_ref, own, wide_a, wide_b, sums_ref, target_ref, source_ref, masks_ref, *, entries):
+def near_one_kernel(control_ref, own, wide_a, wide_b, sums_ref, target_ref, source_ref, masks_ref):
     spread_targets(own, target_ref)
     sums_ref[...] = jnp.zeros_like(sums_ref)
     bodies = [*map(block_of, (own, wide_a, wide_b))]
-    near_part(control_ref, target_ref, sums_ref, source_ref, masks_ref, bodies, 0, entries)
-
-
-def near_two_kernel(control_ref, wide_a, wide_b, wide_c, mine, before, target_ref, sums_ref, source_ref, masks_ref, *, entries):
+    near_part(control_ref, target_ref, sums_ref, source_ref, masks_ref, bodies, 0)
+
+
+def near_two_kernel(control_ref, wide_a, wide_b, wide_c, mine, before, target_ref, sums_ref, source_ref, masks_ref):
     spread_targets(mine, target_ref)
     bodies = [*map(block_of, (wide_a, wide_b, wide_c))]
-    near_part(control_ref, target_ref, sums_ref, source_ref, masks_ref, bodies, 1, entries)
-
-
-def near_three_kernel(control_ref, z_one, y_all, target_ref, before, sums_ref, source_ref, masks_ref, *, entries):
+    near_part(control_ref, target_ref, sums_ref, source_ref, masks_ref, bodies, 1)
+
+
+def near_three_kernel(control_ref, z_one, y_all, target_ref, before, out_ref, sums_ref, source_ref, masks_ref):
     y = lax.axis_index("oct") // 4
 
     def member(flip):
         return lambda b: y_all[y ^ flip, b * 8 : b * 8 + 8, :]
 
     bodies = [block_of(z_one), member(1), member(2)]
-    near_part(control_ref, target_ref, sums_ref, source_ref, masks_ref, bodies, 2, entries)
-
-
-def three_parts(a):
-    hi = a.astype(jnp.bfloat16)
-    rest = a - hi.astype(F32)
-    mid = rest.astype(jnp.bfloat16)
-    return hi, mid, (rest - mid.astype(F32)).astype(jnp.bfloat16)
-
-
-def last_kernel(control_ref, far_ref, own, z_one, z_two, target_ref, before, out_ref, sums_ref, table_ref, rows_ref, source_ref, masks_ref, *, entries):
-    near_part(control_ref, target_ref, sums_ref, source_ref, masks_ref, [block_of(z_two)], 3, entries)
-    sums = []
+    near_part(control_ref, target_ref, sums_ref, source_ref, masks_ref, bodies, 2)
     lane8 = lax.broadcasted_iota(I32, (LEAF, BLK), 1)
     for c in range(3):
         columns = jnp.zeros((LEAF, BLK), F32)
         for b in range(BLK):
             part = jnp.sum(sums_ref[c, b * LEAF : (b + 1) * LEAF, :], axis=1, keepdims=True)
             columns = jnp.where(lane8 == b, part, columns)
-        sums.append(columns.T)
+        out_ref[c] = columns.T
+
+
+def three_parts(a):
+    hi = a.astype(jnp.bfloat16)
+    rest = a - hi.astype(F32)
+    mid = rest.astype(jnp.bfloat16)
+    return hi, mid, (rest - mid.astype(F32)).astype(jnp.bfloat16)
+
+
+def last_items(control_ref, own, body_ref, sums_ref, flipped_ref, stage):
+    lane8 = lax.broadcasted_iota(I32, (BLK, 128), 1)
+    block8 = lax.broadcasted_iota(I32, (BLK, 128), 0)
+    second = body_ref[pl.ds(7, BLK, stride=8), :]
+    mask = jnp.sum(jnp.where((lane8 == 0) & (second > 0.0), jnp.left_shift(1, block8), 0))
+    for b in range(BLK):
+        flipped_ref[b] = body_ref[b * 8 : b * 8 + 8, :].T
+
+    def item(k, carry):
+        value = control_ref[0, k]
+        b, slot = value // 32, value % 32
+
+        def run(h):
+            acc = [jnp.zeros((8, 128), F32)] * 6
+            t = [
+                [jnp.broadcast_to(own[pl.ds(b * 8 + half * 4 + c, 1), :], (8, 128)) for c in range(3)]
+                for half in range(2)
+            ]
+            for i in range(16):
+                columns = flipped_ref[slot, 8 * i : 8 * i + 8, :]
+                s = [jnp.broadcast_to(columns[:, h * 4 + c : h * 4 + c + 1], (8, 128)) for c in range(4)]
+                for half in range(2):
+                    dx, dy, dz = s[0] - t[half][0], s[1] - t[half][1], s[2] - t[half][2]
+                    inv = lax.rsqrt(dx * dx + dy * dy + dz * dz + near_soft)
+                    w = s[3] * (inv * inv * inv)
+                    acc[3 * half] += dx * w
+                    acc[3 * half + 1] += dy * w
+                    acc[3 * half + 2] += dz * w
+            for half in range(2):
+                for c in range(3):
+                    total = jnp.sum(acc[3 * half + c], axis=0, keepdims=True)
+                    sums_ref[c * 2 + half, pl.ds(b, 1), :] += total
+
+        run(0)
+
+        @pl.when(jnp.right_shift(mask, slot) % 2 == 1)
+        def _():
+            run(1)
+
+        return carry
+
+    lax.fori_loop(control_ref[0, ITEMS + stage], control_ref[0, ITEMS + stage + 1], item, 0)
+
+
+def last_kernel(control_ref, far_ref, own, z_one, z_two, before, out_ref, sums_ref, table_ref, rows_ref, flipped_ref, *, entries):
+    for c in range(3):
+        for half in range(2):
+            sums_ref[2 * c + half] = before[c, :, half * 128 : half * 128 + 128]
+    last_items(control_ref, own, z_two, sums_ref, flipped_ref, 3)
+    sums = [jnp.concatenate([sums_ref[2 * c], sums_ref[2 * c + 1]], axis=1) for c in range(3)]
     me = lax.axis_index("oct") % 4
     other = 3 - me
     n = z_one.shape[0] - BODY
@@ -245,10 +304,17 @@
             lhs.append(chosen.astype(jnp.bfloat16))
             rhs.append(fold)
     folded = jnp.dot(jnp.concatenate(lhs, axis=1), jnp.concatenate(rhs, axis=0), preferred_element_type=F32)
+    hi, mid, low = (part.astype(F32) for part in three_parts(folded))
+    parts = (hi + pltpu.roll(mid, SLOT, 1) + pltpu.roll(low, 2 * SLOT, 1)).astype(jnp.bfloat16)
+    k = lax.broadcasted_iota(I32, (128, 10 * 128), 0)
+    n = lax.broadcasted_iota(I32, (128, 10 * 128), 1)
+    ones = ((k % SLOT == n // 128) & (k < 3 * SLOT)).astype(F32).astype(jnp.bfloat16)
+    spread = jnp.dot(parts, ones, preferred_element_type=F32)
     x, y, z, _ = planes(own)
     for v in range(far_count):
-        tile = folded[v * BLK : (v + 1) * BLK, :]
-        mass, cx, cy, cz, xx, yy, zz, xy, xz, yz = (tile[:, k : k + 1] for k in range(10))
+        mass, cx, cy, cz, xx, yy, zz, xy, xz, yz = (
+            jnp.concatenate([spread[v * BLK : (v + 1) * BLK, k * 128 : k * 128 + 128]] * 2, axis=1) for k in range(10)
+        )
         rx, ry, rz = x - cx, y - cy, z - cz
         inv = lax.rsqrt(rx * rx + ry * ry + rz * rz + far_soft)
         inv2 = inv * inv
@@ -344,7 +410,7 @@
     y_all = lax.all_to_all(message, "oct", 0, 0, axis_index_groups=y_groups)
     state = jax.ShapeDtypeStruct((3, BLK * LEAF, 128), F32)
     sums = pl.pallas_call(
-        functools.partial(near_one_kernel, entries=entries),
+        near_one_kernel,
         out_shape=state,
         in_specs=[SMEM] + [VMEM] * 3,
         out_specs=VMEM,
@@ -356,7 +422,7 @@
     mine = small_call(mine_kernel, BODY + 16, own, y_all)
     z_one = exchange(mine, "oct", lambda i: i ^ 1)
     targets, sums = pl.pallas_call(
-        functools.partial(near_two_kernel, entries=entries),
+        near_two_kernel,
         out_shape=[state, state],
         in_specs=[SMEM] + [VMEM] * 5,
         out_specs=[VMEM, VMEM],
@@ -369,31 +435,31 @@
     relay = small_call(relay_kernel, BODY + 32, mine, z_one)
     z_two = exchange(relay, "oct", lambda i: (i & ~3) | RELAY[i & 3])
     sums = pl.pallas_call(
-        functools.partial(near_three_kernel, entries=entries),
-        out_shape=state,
+        near_three_kernel,
+        out_shape=[jax.ShapeDtypeStruct((3, BLK, LEAF), F32), state],
         in_specs=[SMEM] + [VMEM] * 4,
-        out_specs=VMEM,
+        out_specs=[VMEM, VMEM],
         scratch_shapes=sources(3),
-        input_output_aliases={4: 0},
+        input_output_aliases={4: 1},
         compiler_params=params(8),
         cost_estimate=cost(20 << 20),
         name="near_three",
-    )(control, relay, y_all, targets, sums)
+    )(control, relay, y_all, targets, sums)[0]
     return pl.pallas_call(
         functools.partial(last_kernel, entries=entries),
-        out_shape=[jax.ShapeDtypeStruct(positions.shape, F32), state],
-        in_specs=[SMEM] + [VMEM] * 6,
-        out_specs=[VMEM, VMEM],
+        out_shape=jax.ShapeDtypeStruct(positions.shape, F32),
+        in_specs=[SMEM] + [VMEM] * 5,
+        out_specs=VMEM,
         scratch_shapes=[
+            pltpu.VMEM((6, BLK, 128), F32),
             pltpu.VMEM((64, 128), F32),
             pltpu.VMEM((3, BLK, LEAF), F32),
-            *sources(1),
+            pltpu.VMEM((BLK, 128, 8), F32),
         ],
-        input_output_aliases={6: 1},
         compiler_params=params(8),
         cost_estimate=cost(20 << 20),
         name="last",
-    )(control, far_list, mine, z_one, z_two, targets, sums)[0]
+    )(control, far_list, mine, z_one, z_two, sums)
 
 
 def solution(mesh):

time: 75.8 us -> 72.3 us (0.954)
  Pallas kernels: 24.4 us -> 20.9 us
    pallas_call x3, Pallas kernels: 17.4 us -> 15.1 us  [the longest x1 5.77 us: step(): pl.pallas_call(near_three_kernel, out_shape=[jax.ShapeDtypeStruct((3, BLK...]
    pallas_call x1, Pallas kernels: 5.84 us -> 4.52 us  [step(): pl.pallas_call(functools.partial(last_kernel, entries=entries), out_shape...]
  transfers between devices with their start and end apart: 7 -> 7, of which waited for: 2 -> 2; matrix products, arithmetic and copies ran while one was open for 0% -> 0% of each run, Pallas kernels for 23% -> 21%
where the time goes in v3:
time: 72.3 us; the launch traced here: 71.9 us
  starting transfers between devices  35.2 us (49%)
  Pallas kernels  20.9 us (29%)
  blocking collectives  9.71 us (13%)
  waiting for transfers between devices  5.97 us (8%)
    ppermute x7, starting transfers between devices, exchange(): lax.ppermute(payload, axis, [(i, flip(i)) for i in range(lax.axis_size(ax...  35.2 us
    all_to_all x1, blocking collectives, step(): y_all = lax.all_to_all(message, 'oct', 0, 0, axis_index_groups=y_groups)  9.71 us
    ppermute x7, waiting for transfers between devices, exchange(): lax.ppermute(payload, axis, [(i, flip(i)) for i in range(lax.axis_size(ax...  5.97 us
    pallas_call x1, Pallas kernels, step(): pl.pallas_call(near_three_kernel, out_shape=[jax.ShapeDtypeStruct((3, BLK...  5.77 us
    pallas_call x1, Pallas kernels, step(): pl.pallas_call(near_one_kernel, out_shape=state, in_specs=[SMEM] + [VMEM]...  4.71 us
    pallas_call x1, Pallas kernels, step(): pl.pallas_call(near_two_kernel, out_shape=[state, state], in_specs=[SMEM]...  4.61 us
    pallas_call x1, Pallas kernels, step(): pl.pallas_call(functools.partial(last_kernel, entries=entries), out_shape...  4.52 us
  transfers between devices with their start and end apart: 7, of which 2 were waited for; matrix products, arithmetic and copies ran while one was open for 0% of the time, Pallas kernels for 21%

profile of v3, /device:TPU:32, one launch (start us, length us, event | category | flops | bytes accessed | tf_op | source)
XLA Modules:
  0.0 71.9 jit_solution(2106819570259882246)
XLA Ops:
  0.0 1.2 %pack.1 = (f32[72,128]{1,0:T(8,128)S(1)}, s32[8,128]{1,0:T(8,128)S(1)}) custom-call(s32[8]{0:T(128)} %counts_hbm.1, f32[3,2048]{1,0:T(4,128)} %pos_hbm.1, f32[16,128]{1,0:T(8,128)} %bitcast.1, s32[8,8]{1,0:T(8,128)} %near_hbm.1), custom_call_target="tpu_custom_call" | custom-call | tf_op jit(solution)/shard_map/pack/pallas_call | solution.py:383
  1.2 1.9 %collective-permute-start = (f32[72,128]{1,0:T(8,128)S(1)}, f32[72,128]{1,0:T(8,128)S(1)}, u32[]{:S(2)}, u32[]{:S(2)}) collective-permute-start(f32[72,128]{1,0:T(8,128)S(1)} %get-tuple-element.11.refs_0_.own), channel_id=1, source_target_pairs={{0,16},{16,0},{32,48},{48,32},{64,80},{80,64},{96,112},{112,96},{1... | collective-permute-start | bytes 110600 | tf_op jit(solution)/shard_map/ppermute | solution.py:376
  3.1 7.4 %collective-permute-start.1 = (f32[72,128]{1,0:T(8,128)S(1)}, f32[72,128]{1,0:T(8,128)S(1)}, u32[]{:S(2)}, u32[]{:S(2)}) collective-permute-start(f32[72,128]{1,0:T(8,128)S(1)} %get-tuple-element.11.refs_0_.own), channel_id=1, source_target_pairs={{0,32},{16,48},{32,0},{48,16},{64,96},{80,112},{96,64},{112,80},{1... | collective-permute-start | bytes 110600 | tf_op jit(solution)/shard_map/ppermute | solution.py:376
  10.5 1.9 %collective-permute-start.2 = (f32[72,128]{1,0:T(8,128)S(1)}, f32[72,128]{1,0:T(8,128)S(1)}, u32[]{:S(2)}, u32[]{:S(2)}) collective-permute-start(f32[72,128]{1,0:T(8,128)S(1)} %get-tuple-element.11.refs_0_.own), channel_id=1, source_target_pairs={{0,64},{16,80},{32,96},{48,112},{64,0},{80,16},{96,32},{112,48},{1... | collective-permute-start | bytes 110600 | tf_op jit(solution)/shard_map/ppermute | solution.py:376
  12.4 1.9 %collective-permute-start.3 = (f32[72,128]{1,0:T(8,128)S(1)}, f32[72,128]{1,0:T(8,128)S(1)}, u32[]{:S(2)}, u32[]{:S(2)}) collective-permute-start(f32[72,128]{1,0:T(8,128)S(1)} %get-tuple-element.11.refs_0_.own), channel_id=1, source_target_pairs={{0,128},{16,144},{32,160},{48,176},{64,192},{80,208},{96,224},{112... | collective-permute-start | bytes 110600 | tf_op jit(solution)/shard_map/ppermute | solution.py:376
  14.3 4.0 %collective-permute-start.4 = (f32[72,128]{1,0:T(8,128)S(1)}, f32[72,128]{1,0:T(8,128)S(1)}, u32[]{:S(2)}, u32[]{:S(2)}) collective-permute-start(f32[72,128]{1,0:T(8,128)S(1)} %get-tuple-element.11.refs_0_.own), channel_id=1, source_target_pairs={{0,256},{16,272},{32,288},{48,304},{64,320},{80,336},{96,352},{112... | collective-permute-start | bytes 110600 | tf_op jit(solution)/shard_map/ppermute | solution.py:376
  18.4 0.0 collective-permute-done.refs_1_.wide_a
  18.4 0.0 collective-permute-done.1.refs_2_.wide_b
  18.4 0.0 collective-permute-done.2.refs_3_.wide_a
  18.4 0.0 collective-permute-done.3.refs_4_.wide_b
  18.4 3.3 %collective-permute-done.4.refs_5_.wide_c = f32[72,128]{1,0:T(8,128)S(1)} collective-permute-done((f32[72,128]{1,0:T(8,128)S(1)}, f32[72,128]{1,0:T(8,128)S(1)}, u32[]{:S(2)}, u32[]{:S(2)}) %collective-permute-start.4) | collective-permute-done | bytes 36896 | tf_op jit(solution)/shard_map/ppermute | solution.py:376
  21.7 0.1 join.1
  21.8 9.7 %all_to_all.5.y_all = f32[4,72,128]{2,1,0:T(8,128)S(1)} all-to-all(f32[4,72,128]{2,1,0:T(8,128)S(1)} %join.1), channel_id=1, replica_groups={{0,4,8,12},{1,5,9,13},{2,6,10,14},{3,7,11,15},{16,20,24,28},{17,21,25,2..., dimensions={0} | all-to-all | bytes 294912 | tf_op jit(solution)/shard_map/all_to_all | solution.py:410
  31.5 9.1 %collective-permute-start.5 = (f32[80,128]{1,0:T(8,128)S(1)}, f32[80,128]{1,0:T(8,128)S(1)}, u32[]{:S(2)}, u32[]{:S(2)}) collective-permute-start(f32[80,128]{1,0:T(8,128)S(1)} %shard_map.55.mine.own), channel_id=1, source_target_pairs={{0,1},{1,0},{2,3},{3,2},{4,5},{5,4},{6,7},{7,6},{8,9},{9,8},{10,11... | collective-permute-start | bytes 122888 | tf_op jit(solution)/shard_map/ppermute | solution.py:376
  40.6 2.7 %collective-permute-done.5.z_one = f32[80,128]{1,0:T(8,128)S(1)} collective-permute-done((f32[80,128]{1,0:T(8,128)S(1)}, f32[80,128]{1,0:T(8,128)S(1)}, u32[]{:S(2)}, u32[]{:S(2)}) %collective-permute-start.5) | collective-permute-done | bytes 40992 | tf_op jit(solution)/shard_map/ppermute | solution.py:376
  43.3 9.0 %collective-permute-start.6 = (f32[96,128]{1,0:T(8,128)S(1)}, f32[96,128]{1,0:T(8,128)S(1)}, u32[]{:S(2)}, u32[]{:S(2)}) collective-permute-start(f32[96,128]{1,0:T(8,128)S(1)} %shard_map.56.z_one), channel_id=1, source_target_pairs={{0,3},{1,2},{2,1},{3,0},{4,7},{5,6},{6,5},{7,4},{8,11},{9,10},{10,... | collective-permute-start | bytes 147464 | tf_op jit(solution)/shard_map/ppermute | solution.py:376
  52.2 4.7 %near_one.1.before = f32[3,2048,128]{2,1,0:T(8,128)S(1)} custom-call(s32[8,128]{1,0:T(8,128)S(1)} %get-tuple-element.10.control_ref, f32[72,128]{1,0:T(8,128)S(1)} %get-tuple-element.11.refs_0_.own, f32[72,128]{1,0:T(8,128)S(1)} %collective-permute-done.refs_1_.wide_a, f32[72,128]{1,0:T(8,128)S(1)} %collective-permute-done.1.refs_2_.wide_b), custom_call_target="tpu_custom_call" | custom-call | flops 20971520 | bytes 262144 | tf_op jit(solution)/shard_map/near_one/pallas_call | solution.py:412
  56.9 4.6 %near_two.1 = (f32[3,2048,128]{2,1,0:T(8,128)S(1)}, f32[3,2048,128]{2,1,0:T(8,128)S(1)}) custom-call(s32[8,128]{1,0:T(8,128)S(1)} %get-tuple-element.10.control_ref, f32[72,128]{1,0:T(8,128)S(1)} %collective-permute-done.2.refs_3_.wide_a, f32[72,128]{1,0:T(8,128)S(1)} %collective-permute-done.3.refs_4_.wide_b, ...), custom_call_target="tpu_custom_call", output_to_operand_aliasing={{1}: (5, {})} | custom-call | flops 20971520 | bytes 262144 | tf_op jit(solution)/shard_map/near_two/pallas_call | solution.py:424
  61.6 0.0 copy-start
  61.6 5.8 %near_three.1 = (f32[3,8,256]{2,1,0:T(8,128)S(1)}, f32[3,2048,128]{2,1,0:T(8,128)S(1)}) custom-call(s32[8,128]{1,0:T(8,128)S(1)} %get-tuple-element.10.control_ref, f32[96,128]{1,0:T(8,128)S(1)} %shard_map.56.z_one, f32[4,72,128]{2,1,0:T(8,128)S(1)} %all_to_all.5.y_all, ...), custom_call_target="tpu_custom_call", output_to_operand_aliasing={{1}: (4, {})} | custom-call | flops 20971520 | bytes 262144 | tf_op jit(solution)/shard_map/near_three/pallas_call | solution.py:437
  67.3 0.0 collective-permute-done.6.z_two
  67.3 0.0 copy-done
  67.4 4.5 %last.1 = f32[3,2048]{1,0:T(4,128)} custom-call(s32[8,128]{1,0:T(8,128)S(1)} %get-tuple-element.10.control_ref, s32[8,16]{1,0:T(8,128)S(1)} %copy-done, f32[80,128]{1,0:T(8,128)S(1)} %shard_map.55.mine.own, f32[80,128]{1,0:T(8,128)S(1)} %collective-permute-done.5.z_one, f32[96,128]{1,0:T(8,128)S(1)} %collective-permute-done.6.z_two, ...), custom_call_target="tpu_custom_call" | custom-call | flops 20971520 | bytes 262144 | tf_op jit(solution)/shard_map/last/pallas_call | solution.py:448
  (2 shorter events, 0.0 us)
Async XLA Ops:
  1.2 17.2 %collective-permute-start = (f32[72,128]{1,0:T(8,128)S(1)}, f32[72,128]{1,0:T(8,128)S(1)}, u32[]{:S(2)}, u32[]{:S(2)}) collective-permute-start(f32[72,128]{1,0:T(8,128)S(1)} %get-tuple-element.11.refs_0_.own), channel_id=1, source_target_pairs={{0,16},{16,0},{32,48},{48,32},{64,80},{80,64},{96,112},{112,96},{1... | collective-permute-start | bytes 110600 | tf_op jit(solution)/shard_map/ppermute | solution.py:376
  3.1 15.3 %collective-permute-start.1 = (f32[72,128]{1,0:T(8,128)S(1)}, f32[72,128]{1,0:T(8,128)S(1)}, u32[]{:S(2)}, u32[]{:S(2)}) collective-permute-start(f32[72,128]{1,0:T(8,128)S(1)} %get-tuple-element.11.refs_0_.own), channel_id=1, source_target_pairs={{0,32},{16,48},{32,0},{48,16},{64,96},{80,112},{96,64},{112,80},{1... | collective-permute-start | bytes 110600 | tf_op jit(solution)/shard_map/ppermute | solution.py:376
  10.5 7.9 %collective-permute-start.2 = (f32[72,128]{1,0:T(8,128)S(1)}, f32[72,128]{1,0:T(8,128)S(1)}, u32[]{:S(2)}, u32[]{:S(2)}) collective-permute-start(f32[72,128]{1,0:T(8,128)S(1)} %get-tuple-element.11.refs_0_.own), channel_id=1, source_target_pairs={{0,64},{16,80},{32,96},{48,112},{64,0},{80,16},{96,32},{112,48},{1... | collective-permute-start | bytes 110600 | tf_op jit(solution)/shard_map/ppermute | solution.py:376
  12.4 6.0 %collective-permute-start.3 = (f32[72,128]{1,0:T(8,128)S(1)}, f32[72,128]{1,0:T(8,128)S(1)}, u32[]{:S(2)}, u32[]{:S(2)}) collective-permute-start(f32[72,128]{1,0:T(8,128)S(1)} %get-tuple-element.11.refs_0_.own), channel_id=1, source_target_pairs={{0,128},{16,144},{32,160},{48,176},{64,192},{80,208},{96,224},{112... | collective-permute-start | bytes 110600 | tf_op jit(solution)/shard_map/ppermute | solution.py:376
  14.3 7.4 %collective-permute-start.4 = (f32[72,128]{1,0:T(8,128)S(1)}, f32[72,128]{1,0:T(8,128)S(1)}, u32[]{:S(2)}, u32[]{:S(2)}) collective-permute-start(f32[72,128]{1,0:T(8,128)S(1)} %get-tuple-element.11.refs_0_.own), channel_id=1, source_target_pairs={{0,256},{16,272},{32,288},{48,304},{64,320},{80,336},{96,352},{112... | collective-permute-start | bytes 110600 | tf_op jit(solution)/shard_map/ppermute | solution.py:376
  31.5 11.8 %collective-permute-start.5 = (f32[80,128]{1,0:T(8,128)S(1)}, f32[80,128]{1,0:T(8,128)S(1)}, u32[]{:S(2)}, u32[]{:S(2)}) collective-permute-start(f32[80,128]{1,0:T(8,128)S(1)} %shard_map.55.mine.own), channel_id=1, source_target_pairs={{0,1},{1,0},{2,3},{3,2},{4,5},{5,4},{6,7},{7,6},{8,9},{9,8},{10,11... | collective-permute-start | bytes 122888 | tf_op jit(solution)/shard_map/ppermute | solution.py:376
  43.3 24.1 %collective-permute-start.6 = (f32[96,128]{1,0:T(8,128)S(1)}, f32[96,128]{1,0:T(8,128)S(1)}, u32[]{:S(2)}, u32[]{:S(2)}) collective-permute-start(f32[96,128]{1,0:T(8,128)S(1)} %shard_map.56.z_one), channel_id=1, source_target_pairs={{0,3},{1,2},{2,1},{3,0},{4,7},{5,6},{6,5},{7,4},{8,11},{9,10},{10,... | collective-permute-start | bytes 147464 | tf_op jit(solution)/shard_map/ppermute | solution.py:376
  61.6 5.8 %copy-start = (s32[8,16]{1,0:T(8,128)S(1)}, s32[8,16]{1,0:T(8,128)}, u32[]{:S(2)}) copy-start(s32[8,16]{1,0:T(8,128)} %far_ref.1) | copy-start | bytes 1540

commit v4 on v3

--- a/solution.py
+++ b/solution.py
@@ -13,7 +13,8 @@
 BLK = 8
 LEAF = 256
 BODY = BLK * 8
-GROUPS = 8
+STEP = 32
+FEWEST = 3
 SLOT = 16
 F32 = jnp.float32
 I32 = jnp.int32
@@ -98,8 +99,13 @@
     control_ref[...] = control
 
 
+def other_core():
+    return 1 - lax.axis_index("wide") % 2
+
+
 def join_kernel(*refs):
-    *sets, out_ref = refs
+    own, pair, *others, out_ref = refs
+    sets = [own, pair.at[other_core()], *others]
     first = [ref[BODY : BODY + 1, :] for ref in sets]
     last = sum(pltpu.roll(jnp.broadcast_to(ref[BODY + 1 : BODY + 2, :], (8, 128)), 2 * g, 1) if g else jnp.broadcast_to(ref[BODY + 1 : BODY + 2, :], (8, 128)) for g, ref in enumerate(sets))
     at = lax.broadcasted_iota(I32, (8, 128), 0)
@@ -135,57 +141,65 @@
         second = source_ref[pl.ds(s * BODY + 7, BLK, stride=8), :]
         masks_ref[s] = jnp.sum(jnp.where((lane8 == 0) & (second > 0.0), jnp.left_shift(1, block8), 0))
 
-    def run(row, first, count, halves):
+    last = jnp.int32(ITEMS - 1)
+
+    def decode(k):
+        value = control_ref[0, jnp.minimum(k, last)]
+        b, place = value // 32, value % 32
+        steps = (control_ref[b, COUNT] + STEP - 1) // STEP
+        both = jnp.right_shift(masks_ref[place // BLK], place % BLK) % 2
+        return place * 8, b * LEAF, jnp.maximum(steps - FEWEST, 0), both
+
+    def run(steps, halves, k, row, first):
         s = [
             [jnp.broadcast_to(source_ref[pl.ds(row + 4 * h + c, 1), :], (8, 128)) for c in range(4)]
             for h in range(halves)
         ]
-
-        def chunk(g, carry):
-            start = pl.multiple_of(first + g * (8 * GROUPS), 8)
-            for i in range(GROUPS):
-                at = pl.ds(start + 8 * i, 8)
-                t = [target_ref[c, at, :] for c in range(3)]
-                sums = [sums_ref[c, at, :] for c in range(3)]
-                for h in range(halves):
-                    dx, dy, dz = s[h][0] - t[0], s[h][1] - t[1], s[h][2] - t[2]
-                    inv = lax.rsqrt(dx * dx + dy * dy + dz * dz + near_soft)
-                    w = s[h][3] * (inv * inv * inv)
-                    sums = [sums[0] + dx * w, sums[1] + dy * w, sums[2] + dz * w]
-                for c in range(3):
-                    sums_ref[c, at, :] = sums[c]
-            return carry
-
-        lax.fori_loop(0, (count + 8 * GROUPS - 1) // (8 * GROUPS), chunk, 0)
-
-    def item(k, carry):
-        value = control_ref[0, k]
-        b, place = value // 32, value % 32
-        row = place * 8
-        first, count = b * LEAF, control_ref[b, COUNT]
-        both = jnp.right_shift(masks_ref[place // BLK], place % BLK) % 2
-
-        @pl.when(both == 1)
-        def _():
-            run(row, first, count, 2)
-
-        @pl.when(both == 0)
-        def _():
-            run(row, first, count, 1)
-
-        return carry
-
-    lax.fori_loop(control_ref[0, ITEMS + stage], control_ref[0, ITEMS + stage + 1], item, 0)
+        first = pl.multiple_of(first, LEAF)
+        for i in range(steps * STEP // 8):
+            at = pl.ds(first + 8 * i, 8)
+            t = [target_ref[c, at, :] for c in range(3)]
+            sums = [sums_ref[c, at, :] for c in range(3)]
+            for h in range(halves):
+                dx, dy, dz = s[h][0] - t[0], s[h][1] - t[1], s[h][2] - t[2]
+                inv = lax.rsqrt(dx * dx + dy * dy + dz * dz + near_soft)
+                w = s[h][3] * (inv * inv * inv)
+                sums = [sums[0] + dx * w, sums[1] + dy * w, sums[2] + dz * w]
+            for c in range(3):
+                sums_ref[c, at, :] = sums[c]
+        return decode(k + 1)
+
+    def choose(low, high, halves, k, row, first, extra):
+        if low == high:
+            return run(low + FEWEST, halves, k, row, first)
+        mid = (low + high) // 2
+        return lax.cond(
+            extra <= mid,
+            lambda: choose(low, mid, halves, k, row, first, extra),
+            lambda: choose(mid + 1, high, halves, k, row, first, extra),
+        )
+
+    def item(k, now):
+        row, first, extra, both = now
+        most = LEAF // STEP - FEWEST
+        return lax.cond(
+            both == 1,
+            lambda: choose(0, most, 2, k, row, first, extra),
+            lambda: choose(0, most, 1, k, row, first, extra),
+        )
+
+    begin = control_ref[0, ITEMS + stage]
+    lax.fori_loop(begin, control_ref[0, ITEMS + stage + 1], item, decode(begin))
 
 
 def block_of(ref):
     return lambda b: ref[b * 8 : b * 8 + 8, :]
 
 
-def near_one_kernel(control_ref, own, wide_a, wide_b, sums_ref, target_ref, source_ref, masks_ref):
+def near_one_kernel(control_ref, own, pair, wide_a, sums_ref, target_ref, source_ref, masks_ref):
     spread_targets(own, target_ref)
     sums_ref[...] = jnp.zeros_like(sums_ref)
-    bodies = [*map(block_of, (own, wide_a, wide_b))]
+    bodies = [block_of(own), block_of(pair.at[other_core()]), block_of(wide_a)]
     near_part(control_ref, target_ref, sums_ref, source_ref, masks_ref, bodies, 0)
 
 
@@ -219,7 +233,7 @@
     return hi, mid, (rest - mid.astype(F32)).astype(jnp.bfloat16)
 
 
-def last_items(control_ref, own, body_ref, sums_ref, flipped_ref, stage):
+def last_items(control_ref, own, body_ref, sums_ref, flipped_ref, spread_ref, stage):
     lane8 = lax.broadcasted_iota(I32, (BLK, 128), 1)
     block8 = lax.broadcasted_iota(I32, (BLK, 128), 0)
     second = body_ref[pl.ds(7, BLK, stride=8), :]
@@ -237,9 +251,12 @@
                 [jnp.broadcast_to(own[pl.ds(b * 8 + half * 4 + c, 1), :], (8, 128)) for c in range(3)]
                 for half in range(2)
             ]
+            for c in range(4):
+                for i in range(16):
+                    column = flipped_ref[slot, 8 * i : 8 * i + 8, h * 4 + c : h * 4 + c + 1]
+                    spread_ref[c, 8 * i : 8 * i + 8, :] = jnp.broadcast_to(column, (8, 128))
             for i in range(16):
-                columns = flipped_ref[slot, 8 * i : 8 * i + 8, :]
-                s = [jnp.broadcast_to(columns[:, h * 4 + c : h * 4 + c + 1], (8, 128)) for c in range(4)]
+                s = [spread_ref[c, 8 * i : 8 * i + 8, :] for c in range(4)]
                 for half in range(2):
                     dx, dy, dz = s[0] - t[half][0], s[1] - t[half][1], s[2] - t[half][2]
                     inv = lax.rsqrt(dx * dx + dy * dy + dz * dz + near_soft)
@@ -263,11 +280,11 @@
     lax.fori_loop(control_ref[0, ITEMS + stage], control_ref[0, ITEMS + stage + 1], item, 0)
 
 
-def last_kernel(control_ref, far_ref, own, z_one, z_two, before, out_ref, sums_ref, table_ref, rows_ref, flipped_ref, *, entries):
+def last_kernel(control_ref, far_ref, own, z_one, z_two, before, out_ref, sums_ref, table_ref, rows_ref, flipped_ref, spread_ref, *, entries):
     for c in range(3):
         for half in range(2):
             sums_ref[2 * c + half] = before[c, :, half * 128 : half * 128 + 128]
-    last_items(control_ref, own, z_two, sums_ref, flipped_ref, 3)
+    last_items(control_ref, own, z_two, sums_ref, flipped_ref, spread_ref, 3)
     sums = [jnp.concatenate([sums_ref[2 * c], sums_ref[2 * c + 1]], axis=1) for c in range(3)]
     me = lax.axis_index("oct") % 4
     other = 3 - me
@@ -396,7 +413,9 @@
         name="pack",
     )(*(pltpu.with_memory_space_constraint(a, pltpu.HBM) for a in (counts, positions, masses.reshape(16, 128), near_list)))
     wide = []
-    for bit in range(wide_bits):
+    cores = [[i, i + 1] for i in range(0, lax.axis_size("wide"), 2)]
+    pair = lax.all_gather(own, "wide", axis_index_groups=cores)
+    for bit in range(1, wide_bits):
         wide.append(exchange(own, "wide", lambda i, bit=bit: i ^ (1 << bit)))
     message = pl.pallas_call(
         join_kernel,
@@ -405,7 +424,7 @@
         out_specs=VMEM,
         compiler_params=params(4),
         name="join",
-    )(own, *wide)
+    )(own, pair, *wide)
     y_groups = [[z + 4 * y for y in range(4)] for z in range(4)]
     y_all = lax.all_to_all(message, "oct", 0, 0, axis_index_groups=y_groups)
     state = jax.ShapeDtypeStruct((3, BLK * LEAF, 128), F32)
@@ -418,7 +437,7 @@
         compiler_params=params(8),
         cost_estimate=cost(20 << 20),
         name="near_one",
-    )(control, own, wide[0], wide[1])
+    )(control, own, pair, wide[0])
     mine = small_call(mine_kernel, BODY + 16, own, y_all)
     z_one = exchange(mine, "oct", lambda i: i ^ 1)
     targets, sums = pl.pallas_call(
@@ -431,7 +450,7 @@
         compiler_params=params(8),
         cost_estimate=cost(20 << 20),
         name="near_two",
-    )(control, *wide[2:], mine, sums)
+    )(control, *wide[1:], mine, sums)
     relay = small_call(relay_kernel, BODY + 32, mine, z_one)
     z_two = exchange(relay, "oct", lambda i: (i & ~3) | RELAY[i & 3])
     sums = pl.pallas_call(
@@ -455,6 +474,7 @@
             pltpu.VMEM((64, 128), F32),
             pltpu.VMEM((3, BLK, LEAF), F32),
             pltpu.VMEM((BLK, 128, 8), F32),
+            pltpu.VMEM((4, 128, 128), F32),
         ],
         compiler_params=params(8),
         cost_estimate=cost(20 << 20),

time: 72.3 us -> 68 us (0.941)
  the two profiles are of different devices: /device:TPU:32 before, /device:TPU:8 now
where the time goes in v4:
time: 68 us; the launch traced here: 67.7 us
  starting transfers between devices  34.2 us (50%)
  Pallas kernels  18.7 us (28%)
  blocking collectives  11.2 us (16%)
  waiting for transfers between devices  3.45 us (5%)
    ppermute x6, starting transfers between devices, exchange(): lax.ppermute(payload, axis, [(i, flip(i)) for i in range(lax.axis_size(ax...  34.2 us
    all_to_all x1, blocking collectives, step(): y_all = lax.all_to_all(message, 'oct', 0, 0, axis_index_groups=y_groups)  9.32 us
    pallas_call x1, Pallas kernels, step(): pl.pallas_call(functools.partial(last_kernel, entries=entries), out_shape...  4.92 us
    pallas_call x1, Pallas kernels, step(): pl.pallas_call(near_three_kernel, out_shape=[jax.ShapeDtypeStruct((3, BLK...  4.72 us
    pallas_call x1, Pallas kernels, step(): pl.pallas_call(near_one_kernel, out_shape=state, in_specs=[SMEM] + [VMEM]...  3.92 us
    pallas_call x1, Pallas kernels, step(): pl.pallas_call(near_two_kernel, out_shape=[state, state], in_specs=[SMEM]...  3.9 us
    ppermute x6, waiting for transfers between devices, exchange(): lax.ppermute(payload, axis, [(i, flip(i)) for i in range(lax.axis_size(ax...  3.45 us
    all_gather x1, blocking collectives, step(): pair = lax.all_gather(own, 'wide', axis_index_groups=cores)  1.86 us
  transfers between devices with their start and end apart: 6, of which 2 were waited for; matrix products, arithmetic and copies ran while one was open for 0% of the time, Pallas kernels for 19%

profile of v4, /device:TPU:8, one launch (start us, length us, event | category | flops | bytes accessed | tf_op | source)
XLA Modules:
  0.0 67.7 jit_solution(14678902565719038507)
XLA Ops:
  0.0 1.2 %pack.1 = (f32[72,128]{1,0:T(8,128)S(1)}, s32[8,128]{1,0:T(8,128)S(1)}) custom-call(s32[8]{0:T(128)} %counts_hbm.1, f32[3,2048]{1,0:T(4,128)} %pos_hbm.1, f32[16,128]{1,0:T(8,128)} %bitcast.4, s32[8,8]{1,0:T(8,128)} %near_hbm.1), custom_call_target="tpu_custom_call" | custom-call | tf_op jit(solution)/shard_map/pack/pallas_call | solution.py:400
  1.2 3.8 %collective-permute-start = (f32[72,128]{1,0:T(8,128)S(1)}, f32[72,128]{1,0:T(8,128)S(1)}, u32[]{:S(2)}, u32[]{:S(2)}) collective-permute-start(f32[72,128]{1,0:T(8,128)S(1)} %get-tuple-element.11.refs_0_.own), channel_id=1, source_target_pairs={{0,32},{16,48},{32,0},{48,16},{64,96},{80,112},{96,64},{112,80},{1... | collective-permute-start | bytes 110600 | tf_op jit(solution)/shard_map/ppermute | solution.py:393
  5.0 5.2 %collective-permute-start.1 = (f32[72,128]{1,0:T(8,128)S(1)}, f32[72,128]{1,0:T(8,128)S(1)}, u32[]{:S(2)}, u32[]{:S(2)}) collective-permute-start(f32[72,128]{1,0:T(8,128)S(1)} %get-tuple-element.11.refs_0_.own), channel_id=1, source_target_pairs={{0,64},{16,80},{32,96},{48,112},{64,0},{80,16},{96,32},{112,48},{1... | collective-permute-start | bytes 110600 | tf_op jit(solution)/shard_map/ppermute | solution.py:393
  10.2 3.4 %collective-permute-start.2 = (f32[72,128]{1,0:T(8,128)S(1)}, f32[72,128]{1,0:T(8,128)S(1)}, u32[]{:S(2)}, u32[]{:S(2)}) collective-permute-start(f32[72,128]{1,0:T(8,128)S(1)} %get-tuple-element.11.refs_0_.own), channel_id=1, source_target_pairs={{0,128},{16,144},{32,160},{48,176},{64,192},{80,208},{96,224},{112... | collective-permute-start | bytes 110600 | tf_op jit(solution)/shard_map/ppermute | solution.py:393
  13.6 4.6 %collective-permute-start.3 = (f32[72,128]{1,0:T(8,128)S(1)}, f32[72,128]{1,0:T(8,128)S(1)}, u32[]{:S(2)}, u32[]{:S(2)}) collective-permute-start(f32[72,128]{1,0:T(8,128)S(1)} %get-tuple-element.11.refs_0_.own), channel_id=1, source_target_pairs={{0,256},{16,272},{32,288},{48,304},{64,320},{80,336},{96,352},{112... | collective-permute-start | bytes 110600 | tf_op jit(solution)/shard_map/ppermute | solution.py:393
  18.2 1.9 %all-gather = f32[144,128]{1,0:T(8,128)S(1)} all-gather(f32[72,128]{1,0:T(8,128)S(1)} %get-tuple-element.11.refs_0_.own), channel_id=2, replica_groups={{0,16},{32,48},{64,80},{96,112},{128,144},{160,176},{192,208},{224,240}..., dimensions={0}, use_global_device_ids=true | all-gather | bytes 110592 | tf_op jit(solution)/shard_map/all_gather | solution.py:417
  20.1 0.0 collective-permute-done.refs_2_.wide_a
  20.1 0.0 collective-permute-done.1.refs_3_.wide_a
  20.1 0.0 collective-permute-done.2.refs_4_.wide_b
  20.1 0.8 %collective-permute-done.3.refs_5_.wide_c = f32[72,128]{1,0:T(8,128)S(1)} collective-permute-done((f32[72,128]{1,0:T(8,128)S(1)}, f32[72,128]{1,0:T(8,128)S(1)}, u32[]{:S(2)}, u32[]{:S(2)}) %collective-permute-start.3) | collective-permute-done | bytes 36896 | tf_op jit(solution)/shard_map/ppermute | solution.py:393
  21.0 0.1 join.1
  21.0 9.3 %all_to_all.5.y_all = f32[4,72,128]{2,1,0:T(8,128)S(1)} all-to-all(f32[4,72,128]{2,1,0:T(8,128)S(1)} %join.1), channel_id=1, replica_groups={{0,4,8,12},{1,5,9,13},{2,6,10,14},{3,7,11,15},{16,20,24,28},{17,21,25,2..., dimensions={0} | all-to-all | bytes 294912 | tf_op jit(solution)/shard_map/all_to_all | solution.py:429
  30.4 9.1 %collective-permute-start.4 = (f32[80,128]{1,0:T(8,128)S(1)}, f32[80,128]{1,0:T(8,128)S(1)}, u32[]{:S(2)}, u32[]{:S(2)}) collective-permute-start(f32[80,128]{1,0:T(8,128)S(1)} %shard_map.55.mine.own), channel_id=1, source_target_pairs={{0,1},{1,0},{2,3},{3,2},{4,5},{5,4},{6,7},{7,6},{8,9},{9,8},{10,11... | collective-permute-start | bytes 122888 | tf_op jit(solution)/shard_map/ppermute | solution.py:393
  39.4 2.6 %collective-permute-done.4.z_one = f32[80,128]{1,0:T(8,128)S(1)} collective-permute-done((f32[80,128]{1,0:T(8,128)S(1)}, f32[80,128]{1,0:T(8,128)S(1)}, u32[]{:S(2)}, u32[]{:S(2)}) %collective-permute-start.4) | collective-permute-done | bytes 40992 | tf_op jit(solution)/shard_map/ppermute | solution.py:393
  42.1 8.1 %collective-permute-start.5 = (f32[96,128]{1,0:T(8,128)S(1)}, f32[96,128]{1,0:T(8,128)S(1)}, u32[]{:S(2)}, u32[]{:S(2)}) collective-permute-start(f32[96,128]{1,0:T(8,128)S(1)} %shard_map.56.z_one), channel_id=1, source_target_pairs={{0,3},{1,2},{2,1},{3,0},{4,7},{5,6},{6,5},{7,4},{8,11},{9,10},{10,... | collective-permute-start | bytes 147464 | tf_op jit(solution)/shard_map/ppermute | solution.py:393
  50.2 3.9 %near_one.1.before = f32[3,2048,128]{2,1,0:T(8,128)S(1)} custom-call(s32[8,128]{1,0:T(8,128)S(1)} %get-tuple-element.10.control_ref, f32[72,128]{1,0:T(8,128)S(1)} %get-tuple-element.11.refs_0_.own, f32[2,72,128]{2,1,0:T(8,128)S(1)} %bitcast.3, f32[72,128]{1,0:T(8,128)S(1)} %collective-permute-done.refs_2_.wide_a), custom_call_target="tpu_custom_call" | custom-call | flops 20971520 | bytes 262144 | tf_op jit(solution)/shard_map/near_one/pallas_call | solution.py:431
  54.1 3.9 %near_two.1 = (f32[3,2048,128]{2,1,0:T(8,128)S(1)}, f32[3,2048,128]{2,1,0:T(8,128)S(1)}) custom-call(s32[8,128]{1,0:T(8,128)S(1)} %get-tuple-element.10.control_ref, f32[72,128]{1,0:T(8,128)S(1)} %collective-permute-done.1.refs_3_.wide_a, f32[72,128]{1,0:T(8,128)S(1)} %collective-permute-done.2.refs_4_.wide_b, ...), custom_call_target="tpu_custom_call", output_to_operand_aliasing={{1}: (5, {})} | custom-call | flops 20971520 | bytes 262144 | tf_op jit(solution)/shard_map/near_two/pallas_call | solution.py:443
  58.0 0.0 copy-start
  58.0 4.7 %near_three.1 = (f32[3,8,256]{2,1,0:T(8,128)S(1)}, f32[3,2048,128]{2,1,0:T(8,128)S(1)}) custom-call(s32[8,128]{1,0:T(8,128)S(1)} %get-tuple-element.10.control_ref, f32[96,128]{1,0:T(8,128)S(1)} %shard_map.56.z_one, f32[4,72,128]{2,1,0:T(8,128)S(1)} %all_to_all.5.y_all, ...), custom_call_target="tpu_custom_call", output_to_operand_aliasing={{1}: (4, {})} | custom-call | flops 20971520 | bytes 262144 | tf_op jit(solution)/shard_map/near_three/pallas_call | solution.py:456
  62.7 0.0 collective-permute-done.5.z_two
  62.8 0.0 copy-done
  62.8 4.9 %last.1 = f32[3,2048]{1,0:T(4,128)} custom-call(s32[8,128]{1,0:T(8,128)S(1)} %get-tuple-element.10.control_ref, s32[8,16]{1,0:T(8,128)S(1)} %copy-done, f32[80,128]{1,0:T(8,128)S(1)} %shard_map.55.mine.own, f32[80,128]{1,0:T(8,128)S(1)} %collective-permute-done.4.z_one, f32[96,128]{1,0:T(8,128)S(1)} %collective-permute-done.5.z_two, ...), custom_call_target="tpu_custom_call" | custom-call | flops 20971520 | bytes 262144 | tf_op jit(solution)/shard_map/last/pallas_call | solution.py:467
  (2 shorter events, 0.0 us)
Async XLA Ops:
  1.2 18.9 %collective-permute-start = (f32[72,128]{1,0:T(8,128)S(1)}, f32[72,128]{1,0:T(8,128)S(1)}, u32[]{:S(2)}, u32[]{:S(2)}) collective-permute-start(f32[72,128]{1,0:T(8,128)S(1)} %get-tuple-element.11.refs_0_.own), channel_id=1, source_target_pairs={{0,32},{16,48},{32,0},{48,16},{64,96},{80,112},{96,64},{112,80},{1... | collective-permute-start | bytes 110600 | tf_op jit(solution)/shard_map/ppermute | solution.py:393
  5.0 15.1 %collective-permute-start.1 = (f32[72,128]{1,0:T(8,128)S(1)}, f32[72,128]{1,0:T(8,128)S(1)}, u32[]{:S(2)}, u32[]{:S(2)}) collective-permute-start(f32[72,128]{1,0:T(8,128)S(1)} %get-tuple-element.11.refs_0_.own), channel_id=1, source_target_pairs={{0,64},{16,80},{32,96},{48,112},{64,0},{80,16},{96,32},{112,48},{1... | collective-permute-start | bytes 110600 | tf_op jit(solution)/shard_map/ppermute | solution.py:393
  10.2 9.9 %collective-permute-start.2 = (f32[72,128]{1,0:T(8,128)S(1)}, f32[72,128]{1,0:T(8,128)S(1)}, u32[]{:S(2)}, u32[]{:S(2)}) collective-permute-start(f32[72,128]{1,0:T(8,128)S(1)} %get-tuple-element.11.refs_0_.own), channel_id=1, source_target_pairs={{0,128},{16,144},{32,160},{48,176},{64,192},{80,208},{96,224},{112... | collective-permute-start | bytes 110600 | tf_op jit(solution)/shard_map/ppermute | solution.py:393
  13.6 7.4 %collective-permute-start.3 = (f32[72,128]{1,0:T(8,128)S(1)}, f32[72,128]{1,0:T(8,128)S(1)}, u32[]{:S(2)}, u32[]{:S(2)}) collective-permute-start(f32[72,128]{1,0:T(8,128)S(1)} %get-tuple-element.11.refs_0_.own), channel_id=1, source_target_pairs={{0,256},{16,272},{32,288},{48,304},{64,320},{80,336},{96,352},{112... | collective-permute-start | bytes 110600 | tf_op jit(solution)/shard_map/ppermute | solution.py:393
  30.4 11.7 %collective-permute-start.4 = (f32[80,128]{1,0:T(8,128)S(1)}, f32[80,128]{1,0:T(8,128)S(1)}, u32[]{:S(2)}, u32[]{:S(2)}) collective-permute-start(f32[80,128]{1,0:T(8,128)S(1)} %shard_map.55.mine.own), channel_id=1, source_target_pairs={{0,1},{1,0},{2,3},{3,2},{4,5},{5,4},{6,7},{7,6},{8,9},{9,8},{10,11... | collective-permute-start | bytes 122888 | tf_op jit(solution)/shard_map/ppermute | solution.py:393
  42.1 20.7 %collective-permute-start.5 = (f32[96,128]{1,0:T(8,128)S(1)}, f32[96,128]{1,0:T(8,128)S(1)}, u32[]{:S(2)}, u32[]{:S(2)}) collective-permute-start(f32[96,128]{1,0:T(8,128)S(1)} %shard_map.56.z_one), channel_id=1, source_target_pairs={{0,3},{1,2},{2,1},{3,0},{4,7},{5,6},{6,5},{7,4},{8,11},{9,10},{10,... | collective-permute-start | bytes 147464 | tf_op jit(solution)/shard_map/ppermute | solution.py:393
  58.0 4.7 %copy-start = (s32[8,16]{1,0:T(8,128)S(1)}, s32[8,16]{1,0:T(8,128)}, u32[]{:S(2)}) copy-start(s32[8,16]{1,0:T(8,128)} %far_ref.1) | copy-start | bytes 1540

commit v5 on v4

--- a/solution.py
+++ b/solution.py
@@ -24,7 +24,7 @@
 RELAY = (3, 2, 1, 0)
 COUNT = 127
 ITEMS = 64
-STAGES = ((0, 5, 6), (7, 8, 9), (1, 3, 4), (2,))
+STAGES = ((0, 5, 6, 7), (8, 9), (1, 3, 4), (2,))
 
 
 def planes(ref):
@@ -196,96 +196,69 @@
     return lambda b: ref[b * 8 : b * 8 + 8, :]
 
 
-def near_one_kernel(control_ref, own, pair, wide_a, sums_ref, target_ref, source_ref, masks_ref):
+def y_member(y_all, flip):
+    y = lax.axis_index("oct") // 4
+    return lambda b: y_all[y ^ flip, b * 8 : b * 8 + 8, :]
+
+
+def near_one_kernel(control_ref, own, pair, wide_a, wide_b, sums_ref, target_ref, source_ref, masks_ref):
     spread_targets(own, target_ref)
     sums_ref[...] = jnp.zeros_like(sums_ref)
-    bodies = [block_of(own), block_of(pair.at[other_core()]), block_of(wide_a)]
+    bodies = [block_of(own), block_of(pair.at[other_core()]), block_of(wide_a), block_of(wide_b)]
     near_part(control_ref, target_ref, sums_ref, source_ref, masks_ref, bodies, 0)
 
 
-def near_two_kernel(control_ref, wide_a, wide_b, wide_c, mine, before, target_ref, sums_ref, source_ref, masks_ref):
+def near_two_kernel(control_ref, wide_a, wide_b, mine, before, target_ref, sums_ref, source_ref, masks_ref):
     spread_targets(mine, target_ref)
-    bodies = [*map(block_of, (wide_a, wide_b, wide_c))]
+    bodies = [block_of(wide_a), block_of(wide_b)]
     near_part(control_ref, target_ref, sums_ref, source_ref, masks_ref, bodies, 1)
 
 
-def near_three_kernel(control_ref, z_one, y_all, target_ref, before, out_ref, sums_ref, source_ref, masks_ref):
-    y = lax.axis_index("oct") // 4
-
-    def member(flip):
-        return lambda b: y_all[y ^ flip, b * 8 : b * 8 + 8, :]
-
-    bodies = [block_of(z_one), member(1), member(2)]
+def near_three_kernel(
+    control_ref, far_ref, z_one, y_all, target_ref, before, sums_ref, hot_ref, keep_ref, fold_ref, ones_ref, source_ref, masks_ref
+):
+    bodies = [block_of(z_one), y_member(y_all, 1), y_member(y_all, 2)]
     near_part(control_ref, target_ref, sums_ref, source_ref, masks_ref, bodies, 2)
+    members = lax.axis_size("oct")
+    far_count = far_ref.shape[1]
+    lanes = lax.broadcasted_iota(I32, (BLK * far_count, 128), 1)
+    code = jnp.concatenate([jnp.broadcast_to(far_ref[:, v : v + 1], (BLK, 128)) for v in range(far_count)], axis=0)
+    group, member, slot = code // (BLK * members), code // BLK % members, code % BLK
+    row = member % 4 * 16 + member // 4 * 4
+    fold_from = lax.broadcasted_iota(I32, (128, 128), 0)
+    fold_to = lax.broadcasted_iota(I32, (128, 128), 1)
+    for part, (at_row, low, width, base) in enumerate(
+        ((row + group // 2, slot * SLOT + group % 2 * 8, 8, 0), (row + 3, slot * SLOT + group * 2, 2, 8))
+    ):
+        hot_ref[part] = (lanes == at_row).astype(F32).astype(jnp.bfloat16)
+        keep_ref[part] = ((lanes >= low) & (lanes < low + width)).astype(F32)
+        fold_ref[part] = (fold_from % width + base == fold_to).astype(F32).astype(jnp.bfloat16)
+    k = lax.broadcasted_iota(I32, ones_ref.shape, 0)
+    n = lax.broadcasted_iota(I32, ones_ref.shape, 1)
+    ones_ref[...] = ((k % SLOT == n // 128) & (k < 3 * SLOT)).astype(F32).astype(jnp.bfloat16)
+
+
+def three_parts(a):
+    hi = a.astype(jnp.bfloat16)
+    rest = a - hi.astype(F32)
+    mid = rest.astype(jnp.bfloat16)
+    return hi, mid, (rest - mid.astype(F32)).astype(jnp.bfloat16)
+
+
+def last_kernel(
+    control_ref, hot_ref, keep_ref, fold_ref, ones_ref, own, z_one, z_two, target_ref, before,
+    out_ref, sums_ref, table_ref, rows_ref, source_ref, masks_ref, *, entries, far_count
+):
+    near_part(control_ref, target_ref, sums_ref, source_ref, masks_ref, [block_of(z_two)], 3)
+    sums = []
     lane8 = lax.broadcasted_iota(I32, (LEAF, BLK), 1)
     for c in range(3):
         columns = jnp.zeros((LEAF, BLK), F32)
         for b in range(BLK):
             part = jnp.sum(sums_ref[c, b * LEAF : (b + 1) * LEAF, :], axis=1, keepdims=True)
             columns = jnp.where(lane8 == b, part, columns)
-        out_ref[c] = columns.T
-
-
-def three_parts(a):
-    hi = a.astype(jnp.bfloat16)
-    rest = a - hi.astype(F32)
-    mid = rest.astype(jnp.bfloat16)
-    return hi, mid, (rest - mid.astype(F32)).astype(jnp.bfloat16)
-
-
-def last_items(control_ref, own, body_ref, sums_ref, flipped_ref, spread_ref, stage):
-    lane8 = lax.broadcasted_iota(I32, (BLK, 128), 1)
-    block8 = lax.broadcasted_iota(I32, (BLK, 128), 0)
-    second = body_ref[pl.ds(7, BLK, stride=8), :]
-    mask = jnp.sum(jnp.where((lane8 == 0) & (second > 0.0), jnp.left_shift(1, block8), 0))
-    for b in range(BLK):
-        flipped_ref[b] = body_ref[b * 8 : b * 8 + 8, :].T
-
-    def item(k, carry):
-        value = control_ref[0, k]
-        b, slot = value // 32, value % 32
-
-        def run(h):
-            acc = [jnp.zeros((8, 128), F32)] * 6
-            t = [
-                [jnp.broadcast_to(own[pl.ds(b * 8 + half * 4 + c, 1), :], (8, 128)) for c in range(3)]
-                for half in range(2)
-            ]
-            for c in range(4):
-                for i in range(16):
-                    column = flipped_ref[slot, 8 * i : 8 * i + 8, h * 4 + c : h * 4 + c + 1]
-                    spread_ref[c, 8 * i : 8 * i + 8, :] = jnp.broadcast_to(column, (8, 128))
-            for i in range(16):
-                s = [spread_ref[c, 8 * i : 8 * i + 8, :] for c in range(4)]
-                for half in range(2):
-                    dx, dy, dz = s[0] - t[half][0], s[1] - t[half][1], s[2] - t[half][2]
-                    inv = lax.rsqrt(dx * dx + dy * dy + dz * dz + near_soft)
-                    w = s[3] * (inv * inv * inv)
-                    acc[3 * half] += dx * w
-                    acc[3 * half + 1] += dy * w
-                    acc[3 * half + 2] += dz * w
-            for half in range(2):
-                for c in range(3):
-                    total = jnp.sum(acc[3 * half + c], axis=0, keepdims=True)
-                    sums_ref[c * 2 + half, pl.ds(b, 1), :] += total
-
-        run(0)
-
-        @pl.when(jnp.right_shift(mask, slot) % 2 == 1)
-        def _():
-            run(1)
-
-        return carry
-
-    lax.fori_loop(control_ref[0, ITEMS + stage], control_ref[0, ITEMS + stage + 1], item, 0)
-
-
-def last_kernel(control_ref, far_ref, own, z_one, z_two, before, out_ref, sums_ref, table_ref, rows_ref, flipped_ref, spread_ref, *, entries):
-    for c in range(3):
-        for half in range(2):
-            sums_ref[2 * c + half] = before[c, :, half * 128 : half * 128 + 128]
-    last_items(control_ref, own, z_two, sums_ref, flipped_ref, spread_ref, 3)
-    sums = [jnp.concatenate([sums_ref[2 * c], sums_ref[2 * c + 1]], axis=1) for c in range(3)]
+        sums.append(columns.T)
+    table_ref[64:, :] = jnp.zeros((64, 128), F32)
     me = lax.axis_index("oct") % 4
     other = 3 - me
     n = z_one.shape[0] - BODY
@@ -296,37 +269,18 @@
         (other ^ 1, z_two[BODY + n :, :]),
     ):
         table_ref[pl.ds(pl.multiple_of(place * n, n), n), :] = rows
-    members = lax.axis_size("oct")
-    far_count = far_ref.shape[1]
-    picks = BLK * far_count
-    lanes = lax.broadcasted_iota(I32, (picks, 128), 1)
-    code = jnp.concatenate([jnp.broadcast_to(far_ref[:, v : v + 1], (BLK, 128)) for v in range(far_count)], axis=0)
-    group, member, slot = code // (BLK * members), code // BLK % members, code % BLK
-    row = member % 4 * n + member // 4 * 4
     table = jnp.concatenate(three_parts(table_ref[...]), axis=1)
-    folded = jnp.zeros((picks, 128), F32)
     lhs, rhs = [], []
-    fold_from = lax.broadcasted_iota(I32, (128, 128), 0)
-    fold_to = lax.broadcasted_iota(I32, (128, 128), 1)
-    for at_row, low, width, base in (
-        (row + group // 2, slot * SLOT + group % 2 * 8, 8, 0),
-        (row + 3, slot * SLOT + group * 2, 2, 8),
-    ):
-        hot = (lanes == at_row)[:, : table_ref.shape[0]].astype(F32).astype(jnp.bfloat16)
-        rows = jnp.dot(hot, table, preferred_element_type=F32)
-        keep = (lanes >= low) & (lanes < low + width)
-        fold = (fold_from % width + base == fold_to).astype(F32).astype(jnp.bfloat16)
+    for half in range(2):
+        rows = jnp.dot(hot_ref[half], table, preferred_element_type=F32)
         for part in range(3):
-            chosen = jnp.where(keep, rows[:, part * 128 : (part + 1) * 128], 0.0)
+            chosen = jnp.where(keep_ref[half] > 0.0, rows[:, part * 128 : (part + 1) * 128], 0.0)
             lhs.append(chosen.astype(jnp.bfloat16))
-            rhs.append(fold)
+            rhs.append(fold_ref[half])
     folded = jnp.dot(jnp.concatenate(lhs, axis=1), jnp.concatenate(rhs, axis=0), preferred_element_type=F32)
     hi, mid, low = (part.astype(F32) for part in three_parts(folded))
     parts = (hi + pltpu.roll(mid, SLOT, 1) + pltpu.roll(low, 2 * SLOT, 1)).astype(jnp.bfloat16)
-    k = lax.broadcasted_iota(I32, (128, 10 * 128), 0)
-    n = lax.broadcasted_iota(I32, (128, 10 * 128), 1)
-    ones = ((k % SLOT == n // 128) & (k < 3 * SLOT)).astype(F32).astype(jnp.bfloat16)
-    spread = jnp.dot(parts, ones, preferred_element_type=F32)
+    spread = jnp.dot(parts, ones_ref[...], preferred_element_type=F32)
     x, y, z, _ = planes(own)
     for v in range(far_count):
         mass, cx, cy, cz, xx, yy, zz, xy, xz, yz = (
@@ -431,55 +385,61 @@
     sums = pl.pallas_call(
         near_one_kernel,
         out_shape=state,
-        in_specs=[SMEM] + [VMEM] * 3,
+        in_specs=[SMEM] + [VMEM] * 4,
         out_specs=VMEM,
-        scratch_shapes=[pltpu.VMEM(state.shape, F32), *sources(3)],
+        scratch_shapes=[pltpu.VMEM(state.shape, F32), *sources(4)],
         compiler_params=params(8),
         cost_estimate=cost(20 << 20),
         name="near_one",
-    )(control, own, pair, wide[0])
+    )(control, own, pair, wide[0], wide[1])
     mine = small_call(mine_kernel, BODY + 16, own, y_all)
     z_one = exchange(mine, "oct", lambda i: i ^ 1)
     targets, sums = pl.pallas_call(
         near_two_kernel,
         out_shape=[state, state],
-        in_specs=[SMEM] + [VMEM] * 5,
-        out_specs=[VMEM, VMEM],
-        scratch_shapes=sources(3),
-        input_output_aliases={5: 1},
-        compiler_params=params(8),
-        cost_estimate=cost(20 << 20),
-        name="near_two",
-    )(control, *wide[1:], mine, sums)
-    relay = small_call(relay_kernel, BODY + 32, mine, z_one)
-    z_two = exchange(relay, "oct", lambda i: (i & ~3) | RELAY[i & 3])
-    sums = pl.pallas_call(
-        near_three_kernel,
-        out_shape=[jax.ShapeDtypeStruct((3, BLK, LEAF), F32), state],
         in_specs=[SMEM] + [VMEM] * 4,
         out_specs=[VMEM, VMEM],
         scratch_shapes=sources(3),
         input_output_aliases={4: 1},
         compiler_params=params(8),
         cost_estimate=cost(20 << 20),
+        name="near_two",
+    )(control, *wide[2:], mine, sums)
+    relay = small_call(relay_kernel, BODY + 32, mine, z_one)
+    z_two = exchange(relay, "oct", lambda i: (i & ~3) | RELAY[i & 3])
+    far_count = far_list.shape[1]
+    picks = [
+        jax.ShapeDtypeStruct((2, BLK * far_count, 128), jnp.bfloat16),
+        jax.ShapeDtypeStruct((2, BLK * far_count, 128), F32),
+        jax.ShapeDtypeStruct((2, 128, 128), jnp.bfloat16),
+        jax.ShapeDtypeStruct((128, 10 * 128), jnp.bfloat16),
+    ]
+    sums, *picked = pl.pallas_call(
+        near_three_kernel,
+        out_shape=[state, *picks],
+        in_specs=[SMEM] + [VMEM] * 5,
+        out_specs=[VMEM] * 5,
+        scratch_shapes=sources(3),
+        input_output_aliases={5: 0},
+        compiler_params=params(8),
+        cost_estimate=cost(20 << 20),
         name="near_three",
-    )(control, relay, y_all, targets, sums)[0]
+    )(control, far_list, relay, y_all, targets, sums)
     return pl.pallas_call(
-        functools.partial(last_kernel, entries=entries),
-        out_shape=jax.ShapeDtypeStruct(positions.shape, F32),
-        in_specs=[SMEM] + [VMEM] * 5,
-        out_specs=VMEM,
+        functools.partial(last_kernel, entries=entries, far_count=far_count),
+        out_shape=[jax.ShapeDtypeStruct(positions.shape, F32), state],
+        in_specs=[SMEM] + [VMEM] * 9,
+        out_specs=[VMEM, VMEM],
         scratch_shapes=[
-            pltpu.VMEM((6, BLK, 128), F32),
-            pltpu.VMEM((64, 128), F32),
+            pltpu.VMEM((128, 128), F32),
             pltpu.VMEM((3, BLK, LEAF), F32),
-            pltpu.VMEM((BLK, 128, 8), F32),
-            pltpu.VMEM((4, 128, 128), F32),
+            *sources(1),
         ],
+        input_output_aliases={9: 1},
         compiler_params=params(8),
         cost_estimate=cost(20 << 20),
         name="last",
-    )(control, far_list, mine, z_one, z_two, sums)
+    )(control, *picked, mine, z_one, z_two, targets, sums)[0]
 
 
 def solution(mesh):

time: 68 us -> 66.3 us (0.975)
  the two profiles are of different devices: /device:TPU:8 before, /device:TPU:6 now
where the time goes in v5:
time: 66.3 us; the launch traced here: 66 us
  starting transfers between devices  32.5 us (49%)
  Pallas kernels  16.6 us (25%)
  blocking collectives  12.2 us (18%)
  waiting for transfers between devices  4.58 us (7%)
    ppermute x6, starting transfers between devices, exchange(): lax.ppermute(payload, axis, [(i, flip(i)) for i in range(lax.axis_size(ax...  32.5 us
    all_to_all x1, blocking collectives, step(): y_all = lax.all_to_all(message, 'oct', 0, 0, axis_index_groups=y_groups)  10.3 us
    pallas_call x1, Pallas kernels, step(): pl.pallas_call(near_one_kernel, out_shape=state, in_specs=[SMEM] + [VMEM]...  4.98 us
    ppermute x6, waiting for transfers between devices, exchange(): lax.ppermute(payload, axis, [(i, flip(i)) for i in range(lax.axis_size(ax...  4.58 us
    pallas_call x1, Pallas kernels, step(): pl.pallas_call(near_three_kernel, out_shape=[state, *picks], in_specs=[SM...  4.15 us
    pallas_call x1, Pallas kernels, step(): pl.pallas_call(functools.partial(last_kernel, entries=entries, far_count=...  3.47 us
    pallas_call x1, Pallas kernels, step(): pl.pallas_call(near_two_kernel, out_shape=[state, state], in_specs=[SMEM]...  2.76 us
    all_gather x1, blocking collectives, step(): pair = lax.all_gather(own, 'wide', axis_index_groups=cores)  1.86 us
  transfers between devices with their start and end apart: 6, of which 2 were waited for; matrix products, arithmetic and copies ran while one was open for 0% of the time, Pallas kernels for 18%

profile of v5, /device:TPU:6, one launch (start us, length us, event | category | flops | bytes accessed | tf_op | source)
XLA Modules:
  0.0 66.0 jit_solution(2864471139338517708)
XLA Ops:
  0.0 1.2 %pack.1 = (f32[72,128]{1,0:T(8,128)S(1)}, s32[8,128]{1,0:T(8,128)S(1)}) custom-call(s32[8]{0:T(128)} %counts_hbm.1, f32[3,2048]{1,0:T(4,128)} %pos_hbm.1, f32[16,128]{1,0:T(8,128)} %bitcast.4, s32[8,8]{1,0:T(8,128)} %near_hbm.1), custom_call_target="tpu_custom_call" | custom-call | tf_op jit(solution)/shard_map/pack/pallas_call | solution.py:354
  1.2 3.8 %collective-permute-start = (f32[72,128]{1,0:T(8,128)S(1)}, f32[72,128]{1,0:T(8,128)S(1)}, u32[]{:S(2)}, u32[]{:S(2)}) collective-permute-start(f32[72,128]{1,0:T(8,128)S(1)} %get-tuple-element.16.refs_0_.own), channel_id=1, source_target_pairs={{0,32},{16,48},{32,0},{48,16},{64,96},{80,112},{96,64},{112,80},{1... | collective-permute-start | bytes 110600 | tf_op jit(solution)/shard_map/ppermute | solution.py:347
  5.0 5.2 %collective-permute-start.1 = (f32[72,128]{1,0:T(8,128)S(1)}, f32[72,128]{1,0:T(8,128)S(1)}, u32[]{:S(2)}, u32[]{:S(2)}) collective-permute-start(f32[72,128]{1,0:T(8,128)S(1)} %get-tuple-element.16.refs_0_.own), channel_id=1, source_target_pairs={{0,64},{16,80},{32,96},{48,112},{64,0},{80,16},{96,32},{112,48},{1... | collective-permute-start | bytes 110600 | tf_op jit(solution)/shard_map/ppermute | solution.py:347
  10.2 2.7 %collective-permute-start.2 = (f32[72,128]{1,0:T(8,128)S(1)}, f32[72,128]{1,0:T(8,128)S(1)}, u32[]{:S(2)}, u32[]{:S(2)}) collective-permute-start(f32[72,128]{1,0:T(8,128)S(1)} %get-tuple-element.16.refs_0_.own), channel_id=1, source_target_pairs={{0,128},{16,144},{32,160},{48,176},{64,192},{80,208},{96,224},{112... | collective-permute-start | bytes 110600 | tf_op jit(solution)/shard_map/ppermute | solution.py:347
  12.9 3.2 %collective-permute-start.3 = (f32[72,128]{1,0:T(8,128)S(1)}, f32[72,128]{1,0:T(8,128)S(1)}, u32[]{:S(2)}, u32[]{:S(2)}) collective-permute-start(f32[72,128]{1,0:T(8,128)S(1)} %get-tuple-element.16.refs_0_.own), channel_id=1, source_target_pairs={{0,256},{16,272},{32,288},{48,304},{64,320},{80,336},{96,352},{112... | collective-permute-start | bytes 110600 | tf_op jit(solution)/shard_map/ppermute | solution.py:347
  16.1 1.9 %all-gather = f32[144,128]{1,0:T(8,128)S(1)} all-gather(f32[72,128]{1,0:T(8,128)S(1)} %get-tuple-element.16.refs_0_.own), channel_id=2, replica_groups={{0,16},{32,48},{64,80},{96,112},{128,144},{160,176},{192,208},{224,240}..., dimensions={0}, use_global_device_ids=true | all-gather | bytes 110592 | tf_op jit(solution)/shard_map/all_gather | solution.py:371
  18.0 0.0 collective-permute-done.refs_2_.wide_a
  18.0 0.0 collective-permute-done.1.refs_3_.wide_b
  18.0 0.0 collective-permute-done.2.refs_4_.wide_a
  18.0 2.3 %collective-permute-done.3.refs_5_.wide_b = f32[72,128]{1,0:T(8,128)S(1)} collective-permute-done((f32[72,128]{1,0:T(8,128)S(1)}, f32[72,128]{1,0:T(8,128)S(1)}, u32[]{:S(2)}, u32[]{:S(2)}) %collective-permute-start.3) | collective-permute-done | bytes 36896 | tf_op jit(solution)/shard_map/ppermute | solution.py:347
  20.3 0.1 join.1
  20.4 10.3 %all_to_all.5.y_all = f32[4,72,128]{2,1,0:T(8,128)S(1)} all-to-all(f32[4,72,128]{2,1,0:T(8,128)S(1)} %join.1), channel_id=1, replica_groups={{0,4,8,12},{1,5,9,13},{2,6,10,14},{3,7,11,15},{16,20,24,28},{17,21,25,2..., dimensions={0} | all-to-all | bytes 294912 | tf_op jit(solution)/shard_map/all_to_all | solution.py:383
  30.7 9.1 %collective-permute-start.4 = (f32[80,128]{1,0:T(8,128)S(1)}, f32[80,128]{1,0:T(8,128)S(1)}, u32[]{:S(2)}, u32[]{:S(2)}) collective-permute-start(f32[80,128]{1,0:T(8,128)S(1)} %shard_map.55.mine.own), channel_id=1, source_target_pairs={{0,1},{1,0},{2,3},{3,2},{4,5},{5,4},{6,7},{7,6},{8,9},{9,8},{10,11... | collective-permute-start | bytes 122888 | tf_op jit(solution)/shard_map/ppermute | solution.py:347
  39.8 2.3 %collective-permute-done.4.z_one = f32[80,128]{1,0:T(8,128)S(1)} collective-permute-done((f32[80,128]{1,0:T(8,128)S(1)}, f32[80,128]{1,0:T(8,128)S(1)}, u32[]{:S(2)}, u32[]{:S(2)}) %collective-permute-start.4) | collective-permute-done | bytes 40992 | tf_op jit(solution)/shard_map/ppermute | solution.py:347
  42.1 8.4 %collective-permute-start.5 = (f32[96,128]{1,0:T(8,128)S(1)}, f32[96,128]{1,0:T(8,128)S(1)}, u32[]{:S(2)}, u32[]{:S(2)}) collective-permute-start(f32[96,128]{1,0:T(8,128)S(1)} %shard_map.56.z_one), channel_id=1, source_target_pairs={{0,3},{1,2},{2,1},{3,0},{4,7},{5,6},{6,5},{7,4},{8,11},{9,10},{10,... | collective-permute-start | bytes 147464 | tf_op jit(solution)/shard_map/ppermute | solution.py:347
  50.5 0.0 copy-start
  50.5 5.0 %near_one.1.before = f32[3,2048,128]{2,1,0:T(8,128)S(1)} custom-call(s32[8,128]{1,0:T(8,128)S(1)} %get-tuple-element.15.control_ref, f32[72,128]{1,0:T(8,128)S(1)} %get-tuple-element.16.refs_0_.own, f32[2,72,128]{2,1,0:T(8,128)S(1)} %bitcast.3, f32[72,128]{1,0:T(8,128)S(1)} %collective-permute-done.refs_2_.wide_a, ...), custom_call_target="tpu_custom_call" | custom-call | flops 20971520 | bytes 262144 | tf_op jit(solution)/shard_map/near_one/pallas_call | solution.py:385
  55.5 2.8 %near_two.1 = (f32[3,2048,128]{2,1,0:T(8,128)S(1)}, f32[3,2048,128]{2,1,0:T(8,128)S(1)}) custom-call(s32[8,128]{1,0:T(8,128)S(1)} %get-tuple-element.15.control_ref, f32[72,128]{1,0:T(8,128)S(1)} %collective-permute-done.2.refs_4_.wide_a, f32[72,128]{1,0:T(8,128)S(1)} %collective-permute-done.3.refs_5_.wide_b, ...), custom_call_target="tpu_custom_call", output_to_operand_aliasing={{1}: (4, {})} | custom-call | flops 20971520 | bytes 262144 | tf_op jit(solution)/shard_map/near_two/pallas_call | solution.py:397
  58.3 0.0 copy-done
  58.3 4.2 %near_three.1 = (f32[3,2048,128]{2,1,0:T(8,128)S(1)}, bf16[2,128,128]{2,1,0:T(8,128)(2,1)S(1)}, f32[2,128,128]{2,1,0:T(8,128)S(1)}, bf16[2,128,128]{2,1,0:T(8,128)(2,1)S(1)}, bf16[128,1280]{1,0:T(8,128)(2,1)S(1)}) custom-call(s32[8,128]{1,0:T(8,128)S(1)} %get-tuple-element.15.control_ref, s32[8,16]{1,0:T(8,128)S(1)} %copy-done, ...), custom_call_target="tpu_custom_call", output_to_operand_aliasing={{0}: (5, {})} | custom-call | flops 20971520 | bytes 262144 | tf_op jit(solution)/shard_map/near_three/pallas_call | solution.py:417
  62.5 0.0 collective-permute-done.5.z_two
  62.5 3.5 %last.1 = (f32[3,2048]{1,0:T(4,128)}, f32[3,2048,128]{2,1,0:T(8,128)S(1)}) custom-call(s32[8,128]{1,0:T(8,128)S(1)} %get-tuple-element.15.control_ref, bf16[2,128,128]{2,1,0:T(8,128)(2,1)S(1)} %get-tuple-element.19.hot_ref, f32[2,128,128]{2,1,0:T(8,128)S(1)} %get-tuple-element.20.keep_ref, ...), custom_call_target="tpu_custom_call", output_to_operand_aliasing={{1}: (9, {})} | custom-call | flops 20971520 | bytes 262144 | tf_op jit(solution)/shard_map/last/pallas_call | solution.py:428
  (2 shorter events, 0.0 us)
Async XLA Ops:
  1.2 16.8 %collective-permute-start = (f32[72,128]{1,0:T(8,128)S(1)}, f32[72,128]{1,0:T(8,128)S(1)}, u32[]{:S(2)}, u32[]{:S(2)}) collective-permute-start(f32[72,128]{1,0:T(8,128)S(1)} %get-tuple-element.16.refs_0_.own), channel_id=1, source_target_pairs={{0,32},{16,48},{32,0},{48,16},{64,96},{80,112},{96,64},{112,80},{1... | collective-permute-start | bytes 110600 | tf_op jit(solution)/shard_map/ppermute | solution.py:347
  5.0 13.0 %collective-permute-start.1 = (f32[72,128]{1,0:T(8,128)S(1)}, f32[72,128]{1,0:T(8,128)S(1)}, u32[]{:S(2)}, u32[]{:S(2)}) collective-permute-start(f32[72,128]{1,0:T(8,128)S(1)} %get-tuple-element.16.refs_0_.own), channel_id=1, source_target_pairs={{0,64},{16,80},{32,96},{48,112},{64,0},{80,16},{96,32},{112,48},{1... | collective-permute-start | bytes 110600 | tf_op jit(solution)/shard_map/ppermute | solution.py:347
  10.2 7.8 %collective-permute-start.2 = (f32[72,128]{1,0:T(8,128)S(1)}, f32[72,128]{1,0:T(8,128)S(1)}, u32[]{:S(2)}, u32[]{:S(2)}) collective-permute-start(f32[72,128]{1,0:T(8,128)S(1)} %get-tuple-element.16.refs_0_.own), channel_id=1, source_target_pairs={{0,128},{16,144},{32,160},{48,176},{64,192},{80,208},{96,224},{112... | collective-permute-start | bytes 110600 | tf_op jit(solution)/shard_map/ppermute | solution.py:347
  12.9 7.4 %collective-permute-start.3 = (f32[72,128]{1,0:T(8,128)S(1)}, f32[72,128]{1,0:T(8,128)S(1)}, u32[]{:S(2)}, u32[]{:S(2)}) collective-permute-start(f32[72,128]{1,0:T(8,128)S(1)} %get-tuple-element.16.refs_0_.own), channel_id=1, source_target_pairs={{0,256},{16,272},{32,288},{48,304},{64,320},{80,336},{96,352},{112... | collective-permute-start | bytes 110600 | tf_op jit(solution)/shard_map/ppermute | solution.py:347
  30.7 11.4 %collective-permute-start.4 = (f32[80,128]{1,0:T(8,128)S(1)}, f32[80,128]{1,0:T(8,128)S(1)}, u32[]{:S(2)}, u32[]{:S(2)}) collective-permute-start(f32[80,128]{1,0:T(8,128)S(1)} %shard_map.55.mine.own), channel_id=1, source_target_pairs={{0,1},{1,0},{2,3},{3,2},{4,5},{5,4},{6,7},{7,6},{8,9},{9,8},{10,11... | collective-permute-start | bytes 122888 | tf_op jit(solution)/shard_map/ppermute | solution.py:347
  42.1 20.4 %collective-permute-start.5 = (f32[96,128]{1,0:T(8,128)S(1)}, f32[96,128]{1,0:T(8,128)S(1)}, u32[]{:S(2)}, u32[]{:S(2)}) collective-permute-start(f32[96,128]{1,0:T(8,128)S(1)} %shard_map.56.z_one), channel_id=1, source_target_pairs={{0,3},{1,2},{2,1},{3,0},{4,7},{5,6},{6,5},{7,4},{8,11},{9,10},{10,... | collective-permute-start | bytes 147464 | tf_op jit(solution)/shard_map/ppermute | solution.py:347
  50.5 7.8 %copy-start = (s32[8,16]{1,0:T(8,128)S(1)}, s32[8,16]{1,0:T(8,128)}, u32[]{:S(2)}) copy-start(s32[8,16]{1,0:T(8,128)} %far_ref.1) | copy-start | bytes 1540

commit v6 on v5

--- a/solution.py
+++ b/solution.py
@@ -24,7 +24,8 @@
 RELAY = (3, 2, 1, 0)
 COUNT = 127
 ITEMS = 64
-STAGES = ((0, 5, 6, 7), (8, 9), (1, 3, 4), (2,))
+STAGES = ((0, 5, 6), (7, 8, 9, 3, 4), (1, 3, 4), (2,))
+PLACES = 64
 
 
 def planes(ref):
@@ -75,11 +76,15 @@
     code = near_ref[...]
     entries = code.shape[1]
     stage = jnp.zeros_like(code)
-    value = lax.broadcasted_iota(I32, code.shape, 0) * 32 + code % BLK
+    value = lax.broadcasted_iota(I32, code.shape, 0) * PLACES + code % BLK
+    early = lax.axis_index("oct") % 4 < 2
     for number, names in enumerate(STAGES):
         for place, name in enumerate(names):
-            stage = jnp.where(code // BLK == name, number, stage)
-            value = value + jnp.where(code // BLK == name, place * BLK, 0)
+            mine = code // BLK == name
+            if name in (3, 4):
+                mine = mine & (early if number == 1 else jnp.logical_not(early))
+            stage = jnp.where(mine, number, stage)
+            value = value + jnp.where(mine, place * BLK, 0)
 
     def column(a):
         return jnp.concatenate([jnp.broadcast_to(a[:, v : v + 1], (BLK, 128)) for v in range(entries)], axis=0).astype(F32)
@@ -145,7 +150,7 @@
 
     def decode(k):
         value = control_ref[0, jnp.minimum(k, last)]
-        b, place = value // 32, value % 32
+        b, place = value // PLACES, value % PLACES
         steps = (control_ref[b, COUNT] + STEP - 1) // STEP
         both = jnp.right_shift(masks_ref[place // BLK], place % BLK) % 2
         return place * 8, b * LEAF, jnp.maximum(steps - FEWEST, 0), both
@@ -201,16 +206,16 @@
     return lambda b: y_all[y ^ flip, b * 8 : b * 8 + 8, :]
 
 
-def near_one_kernel(control_ref, own, pair, wide_a, wide_b, sums_ref, target_ref, source_ref, masks_ref):
+def near_one_kernel(control_ref, own, pair, wide_a, sums_ref, target_ref, source_ref, masks_ref):
     spread_targets(own, target_ref)
     sums_ref[...] = jnp.zeros_like(sums_ref)
-    bodies = [block_of(own), block_of(pair.at[other_core()]), block_of(wide_a), block_of(wide_b)]
+    bodies = [block_of(own), block_of(pair.at[other_core()]), block_of(wide_a)]
     near_part(control_ref, target_ref, sums_ref, source_ref, masks_ref, bodies, 0)
 
 
-def near_two_kernel(control_ref, wide_a, wide_b, mine, before, target_ref, sums_ref, source_ref, masks_ref):
+def near_two_kernel(control_ref, wide_a, wide_b, wide_c, y_all, mine, before, target_ref, sums_ref, source_ref, masks_ref):
     spread_targets(mine, target_ref)
-    bodies = [block_of(wide_a), block_of(wide_b)]
+    bodies = [*map(block_of, (wide_a, wide_b, wide_c)), y_member(y_all, 1), y_member(y_all, 2)]
     near_part(control_ref, target_ref, sums_ref, source_ref, masks_ref, bodies, 1)
 
 
@@ -309,7 +314,7 @@
 
 
 def sources(sets):
-    return [pltpu.VMEM((sets * BODY, 128), F32), pltpu.SMEM((4,), I32)]
+    return [pltpu.VMEM((sets * BODY, 128), F32), pltpu.SMEM((PLACES // BLK,), I32)]
 
 
 def params(mib):
@@ -385,26 +390,26 @@
     sums = pl.pallas_call(
         near_one_kernel,
         out_shape=state,
-        in_specs=[SMEM] + [VMEM] * 4,
+        in_specs=[SMEM] + [VMEM] * 3,
         out_specs=VMEM,
-        scratch_shapes=[pltpu.VMEM(state.shape, F32), *sources(4)],
+        scratch_shapes=[pltpu.VMEM(state.shape, F32), *sources(3)],
         compiler_params=params(8),
         cost_estimate=cost(20 << 20),
         name="near_one",
-    )(control, own, pair, wide[0], wide[1])
+    )(control, own, pair, wide[0])
     mine = small_call(mine_kernel, BODY + 16, own, y_all)
     z_one = exchange(mine, "oct", lambda i: i ^ 1)
     targets, sums = pl.pallas_call(
         near_two_kernel,
         out_shape=[state, state],
-        in_specs=[SMEM] + [VMEM] * 4,
+        in_specs=[SMEM] + [VMEM] * 6,
         out_specs=[VMEM, VMEM],
-        scratch_shapes=sources(3),
-        input_output_aliases={4: 1},
+        scratch_shapes=sources(5),
+        input_output_aliases={6: 1},
         compiler_params=params(8),
         cost_estimate=cost(20 << 20),
         name="near_two",
-    )(control, *wide[2:], mine, sums)
+    )(control, *wide[1:], y_all, mine, sums)
     relay = small_call(relay_kernel, BODY + 32, mine, z_one)
     z_two = exchange(relay, "oct", lambda i: (i & ~3) | RELAY[i & 3])
     far_count = far_list.shape[1]

time: 66.3 us -> 66.3 us (level)
    pallas_call x1, Pallas kernels: 2.76 us -> 5.46 us  [step(): pl.pallas_call(near_two_kernel, out_shape=[state, state], in_specs=[SMEM]...]
    pallas_call x1, Pallas kernels: 4.15 us -> 2.29 us  [step(): pl.pallas_call(near_three_kernel, out_shape=[state, *picks], in_specs=[SM...]
    pallas_call x1, Pallas kernels: 4.98 us -> 4.13 us  [step(): pl.pallas_call(near_one_kernel, out_shape=state, in_specs=[SMEM] + [VMEM]...]
where the time goes in v6:
time: 66.3 us; the launch traced here: 66 us
  starting transfers between devices  32.5 us (49%)
  Pallas kernels  16.6 us (25%)
  blocking collectives  12.2 us (18%)
  waiting for transfers between devices  4.58 us (7%)
    ppermute x6, starting transfers between devices, exchange(): lax.ppermute(payload, axis, [(i, flip(i)) for i in range(lax.axis_size(ax...  32.5 us
    all_to_all x1, blocking collectives, step(): y_all = lax.all_to_all(message, 'oct', 0, 0, axis_index_groups=y_groups)  10.3 us
    pallas_call x1, Pallas kernels, step(): pl.pallas_call(near_two_kernel, out_shape=[state, state], in_specs=[SMEM]...  5.46 us
    ppermute x6, waiting for transfers between devices, exchange(): lax.ppermute(payload, axis, [(i, flip(i)) for i in range(lax.axis_size(ax...  4.58 us
    pallas_call x1, Pallas kernels, step(): pl.pallas_call(near_one_kernel, out_shape=state, in_specs=[SMEM] + [VMEM]...  4.13 us
    pallas_call x1, Pallas kernels, step(): pl.pallas_call(functools.partial(last_kernel, entries=entries, far_count=...  3.48 us
    pallas_call x1, Pallas kernels, step(): pl.pallas_call(near_three_kernel, out_shape=[state, *picks], in_specs=[SM...  2.29 us
    all_gather x1, blocking collectives, step(): pair = lax.all_gather(own, 'wide', axis_index_groups=cores)  1.86 us
  transfers between devices with their start and end apart: 6, of which 2 were waited for; matrix products, arithmetic and copies ran while one was open for 0% of the time, Pallas kernels for 18%

profile of v6, /device:TPU:6, one launch (start us, length us, event | category | flops | bytes accessed | tf_op | source)
XLA Modules:
  0.0 66.0 jit_solution(11335422073970128878)
XLA Ops:
  0.0 1.2 %pack.1 = (f32[72,128]{1,0:T(8,128)S(1)}, s32[8,128]{1,0:T(8,128)S(1)}) custom-call(s32[8]{0:T(128)} %counts_hbm.1, f32[3,2048]{1,0:T(4,128)} %pos_hbm.1, f32[16,128]{1,0:T(8,128)} %bitcast.4, s32[8,8]{1,0:T(8,128)} %near_hbm.1), custom_call_target="tpu_custom_call" | custom-call | tf_op jit(solution)/shard_map/pack/pallas_call | solution.py:359
  1.2 3.8 %collective-permute-start = (f32[72,128]{1,0:T(8,128)S(1)}, f32[72,128]{1,0:T(8,128)S(1)}, u32[]{:S(2)}, u32[]{:S(2)}) collective-permute-start(f32[72,128]{1,0:T(8,128)S(1)} %get-tuple-element.16.refs_0_.own), channel_id=1, source_target_pairs={{0,32},{16,48},{32,0},{48,16},{64,96},{80,112},{96,64},{112,80},{1... | collective-permute-start | bytes 110600 | tf_op jit(solution)/shard_map/ppermute | solution.py:352
  5.0 5.2 %collective-permute-start.1 = (f32[72,128]{1,0:T(8,128)S(1)}, f32[72,128]{1,0:T(8,128)S(1)}, u32[]{:S(2)}, u32[]{:S(2)}) collective-permute-start(f32[72,128]{1,0:T(8,128)S(1)} %get-tuple-element.16.refs_0_.own), channel_id=1, source_target_pairs={{0,64},{16,80},{32,96},{48,112},{64,0},{80,16},{96,32},{112,48},{1... | collective-permute-start | bytes 110600 | tf_op jit(solution)/shard_map/ppermute | solution.py:352
  10.2 2.7 %collective-permute-start.2 = (f32[72,128]{1,0:T(8,128)S(1)}, f32[72,128]{1,0:T(8,128)S(1)}, u32[]{:S(2)}, u32[]{:S(2)}) collective-permute-start(f32[72,128]{1,0:T(8,128)S(1)} %get-tuple-element.16.refs_0_.own), channel_id=1, source_target_pairs={{0,128},{16,144},{32,160},{48,176},{64,192},{80,208},{96,224},{112... | collective-permute-start | bytes 110600 | tf_op jit(solution)/shard_map/ppermute | solution.py:352
  12.9 3.2 %collective-permute-start.3 = (f32[72,128]{1,0:T(8,128)S(1)}, f32[72,128]{1,0:T(8,128)S(1)}, u32[]{:S(2)}, u32[]{:S(2)}) collective-permute-start(f32[72,128]{1,0:T(8,128)S(1)} %get-tuple-element.16.refs_0_.own), channel_id=1, source_target_pairs={{0,256},{16,272},{32,288},{48,304},{64,320},{80,336},{96,352},{112... | collective-permute-start | bytes 110600 | tf_op jit(solution)/shard_map/ppermute | solution.py:352
  16.1 1.9 %all-gather = f32[144,128]{1,0:T(8,128)S(1)} all-gather(f32[72,128]{1,0:T(8,128)S(1)} %get-tuple-element.16.refs_0_.own), channel_id=2, replica_groups={{0,16},{32,48},{64,80},{96,112},{128,144},{160,176},{192,208},{224,240}..., dimensions={0}, use_global_device_ids=true | all-gather | bytes 110592 | tf_op jit(solution)/shard_map/all_gather | solution.py:376
  18.0 0.0 collective-permute-done.refs_2_.wide_a
  18.0 0.0 collective-permute-done.1.refs_3_.wide_a
  18.0 0.0 collective-permute-done.2.refs_4_.wide_b
  18.0 2.3 %collective-permute-done.3.refs_5_.wide_c = f32[72,128]{1,0:T(8,128)S(1)} collective-permute-done((f32[72,128]{1,0:T(8,128)S(1)}, f32[72,128]{1,0:T(8,128)S(1)}, u32[]{:S(2)}, u32[]{:S(2)}) %collective-permute-start.3) | collective-permute-done | bytes 36896 | tf_op jit(solution)/shard_map/ppermute | solution.py:352
  20.3 0.1 join.1
  20.4 10.3 %all_to_all.5.y_all = f32[4,72,128]{2,1,0:T(8,128)S(1)} all-to-all(f32[4,72,128]{2,1,0:T(8,128)S(1)} %join.1), channel_id=1, replica_groups={{0,4,8,12},{1,5,9,13},{2,6,10,14},{3,7,11,15},{16,20,24,28},{17,21,25,2..., dimensions={0} | all-to-all | bytes 294912 | tf_op jit(solution)/shard_map/all_to_all | solution.py:388
  30.7 9.1 %collective-permute-start.4 = (f32[80,128]{1,0:T(8,128)S(1)}, f32[80,128]{1,0:T(8,128)S(1)}, u32[]{:S(2)}, u32[]{:S(2)}) collective-permute-start(f32[80,128]{1,0:T(8,128)S(1)} %shard_map.55.mine.own), channel_id=1, source_target_pairs={{0,1},{1,0},{2,3},{3,2},{4,5},{5,4},{6,7},{7,6},{8,9},{9,8},{10,11... | collective-permute-start | bytes 122888 | tf_op jit(solution)/shard_map/ppermute | solution.py:352
  39.8 2.3 %collective-permute-done.4.z_one = f32[80,128]{1,0:T(8,128)S(1)} collective-permute-done((f32[80,128]{1,0:T(8,128)S(1)}, f32[80,128]{1,0:T(8,128)S(1)}, u32[]{:S(2)}, u32[]{:S(2)}) %collective-permute-start.4) | collective-permute-done | bytes 40992 | tf_op jit(solution)/shard_map/ppermute | solution.py:352
  42.1 8.4 %collective-permute-start.5 = (f32[96,128]{1,0:T(8,128)S(1)}, f32[96,128]{1,0:T(8,128)S(1)}, u32[]{:S(2)}, u32[]{:S(2)}) collective-permute-start(f32[96,128]{1,0:T(8,128)S(1)} %shard_map.56.z_one), channel_id=1, source_target_pairs={{0,3},{1,2},{2,1},{3,0},{4,7},{5,6},{6,5},{7,4},{8,11},{9,10},{10,... | collective-permute-start | bytes 147464 | tf_op jit(solution)/shard_map/ppermute | solution.py:352
  50.5 0.0 copy-start
  50.5 4.1 %near_one.1.before = f32[3,2048,128]{2,1,0:T(8,128)S(1)} custom-call(s32[8,128]{1,0:T(8,128)S(1)} %get-tuple-element.15.control_ref, f32[72,128]{1,0:T(8,128)S(1)} %get-tuple-element.16.refs_0_.own, f32[2,72,128]{2,1,0:T(8,128)S(1)} %bitcast.3, f32[72,128]{1,0:T(8,128)S(1)} %collective-permute-done.refs_2_.wide_a), custom_call_target="tpu_custom_call" | custom-call | flops 20971520 | bytes 262144 | tf_op jit(solution)/shard_map/near_one/pallas_call | solution.py:390
  54.7 5.5 %near_two.1 = (f32[3,2048,128]{2,1,0:T(8,128)S(1)}, f32[3,2048,128]{2,1,0:T(8,128)S(1)}) custom-call(s32[8,128]{1,0:T(8,128)S(1)} %get-tuple-element.15.control_ref, f32[72,128]{1,0:T(8,128)S(1)} %collective-permute-done.1.refs_3_.wide_a, f32[72,128]{1,0:T(8,128)S(1)} %collective-permute-done.2.refs_4_.wide_b, ...), custom_call_target="tpu_custom_call", output_to_operand_aliasing={{1}: (6, {})} | custom-call | flops 20971520 | bytes 262144 | tf_op jit(solution)/shard_map/near_two/pallas_call | solution.py:402
  60.2 0.0 copy-done
  60.2 2.3 %near_three.1 = (f32[3,2048,128]{2,1,0:T(8,128)S(1)}, bf16[2,128,128]{2,1,0:T(8,128)(2,1)S(1)}, f32[2,128,128]{2,1,0:T(8,128)S(1)}, bf16[2,128,128]{2,1,0:T(8,128)(2,1)S(1)}, bf16[128,1280]{1,0:T(8,128)(2,1)S(1)}) custom-call(s32[8,128]{1,0:T(8,128)S(1)} %get-tuple-element.15.control_ref, s32[8,16]{1,0:T(8,128)S(1)} %copy-done, ...), custom_call_target="tpu_custom_call", output_to_operand_aliasing={{0}: (5, {})} | custom-call | flops 20971520 | bytes 262144 | tf_op jit(solution)/shard_map/near_three/pallas_call | solution.py:422
  62.5 0.0 collective-permute-done.5.z_two
  62.5 3.5 %last.1 = (f32[3,2048]{1,0:T(4,128)}, f32[3,2048,128]{2,1,0:T(8,128)S(1)}) custom-call(s32[8,128]{1,0:T(8,128)S(1)} %get-tuple-element.15.control_ref, bf16[2,128,128]{2,1,0:T(8,128)(2,1)S(1)} %get-tuple-element.19.hot_ref, f32[2,128,128]{2,1,0:T(8,128)S(1)} %get-tuple-element.20.keep_ref, ...), custom_call_target="tpu_custom_call", output_to_operand_aliasing={{1}: (9, {})} | custom-call | flops 20971520 | bytes 262144 | tf_op jit(solution)/shard_map/last/pallas_call | solution.py:433
  (2 shorter events, 0.0 us)
Async XLA Ops:
  1.2 16.8 %collective-permute-start = (f32[72,128]{1,0:T(8,128)S(1)}, f32[72,128]{1,0:T(8,128)S(1)}, u32[]{:S(2)}, u32[]{:S(2)}) collective-permute-start(f32[72,128]{1,0:T(8,128)S(1)} %get-tuple-element.16.refs_0_.own), channel_id=1, source_target_pairs={{0,32},{16,48},{32,0},{48,16},{64,96},{80,112},{96,64},{112,80},{1... | collective-permute-start | bytes 110600 | tf_op jit(solution)/shard_map/ppermute | solution.py:352
  5.0 13.0 %collective-permute-start.1 = (f32[72,128]{1,0:T(8,128)S(1)}, f32[72,128]{1,0:T(8,128)S(1)}, u32[]{:S(2)}, u32[]{:S(2)}) collective-permute-start(f32[72,128]{1,0:T(8,128)S(1)} %get-tuple-element.16.refs_0_.own), channel_id=1, source_target_pairs={{0,64},{16,80},{32,96},{48,112},{64,0},{80,16},{96,32},{112,48},{1... | collective-permute-start | bytes 110600 | tf_op jit(solution)/shard_map/ppermute | solution.py:352
  10.2 7.8 %collective-permute-start.2 = (f32[72,128]{1,0:T(8,128)S(1)}, f32[72,128]{1,0:T(8,128)S(1)}, u32[]{:S(2)}, u32[]{:S(2)}) collective-permute-start(f32[72,128]{1,0:T(8,128)S(1)} %get-tuple-element.16.refs_0_.own), channel_id=1, source_target_pairs={{0,128},{16,144},{32,160},{48,176},{64,192},{80,208},{96,224},{112... | collective-permute-start | bytes 110600 | tf_op jit(solution)/shard_map/ppermute | solution.py:352
  12.9 7.4 %collective-permute-start.3 = (f32[72,128]{1,0:T(8,128)S(1)}, f32[72,128]{1,0:T(8,128)S(1)}, u32[]{:S(2)}, u32[]{:S(2)}) collective-permute-start(f32[72,128]{1,0:T(8,128)S(1)} %get-tuple-element.16.refs_0_.own), channel_id=1, source_target_pairs={{0,256},{16,272},{32,288},{48,304},{64,320},{80,336},{96,352},{112... | collective-permute-start | bytes 110600 | tf_op jit(solution)/shard_map/ppermute | solution.py:352
  30.7 11.4 %collective-permute-start.4 = (f32[80,128]{1,0:T(8,128)S(1)}, f32[80,128]{1,0:T(8,128)S(1)}, u32[]{:S(2)}, u32[]{:S(2)}) collective-permute-start(f32[80,128]{1,0:T(8,128)S(1)} %shard_map.55.mine.own), channel_id=1, source_target_pairs={{0,1},{1,0},{2,3},{3,2},{4,5},{5,4},{6,7},{7,6},{8,9},{9,8},{10,11... | collective-permute-start | bytes 122888 | tf_op jit(solution)/shard_map/ppermute | solution.py:352
  42.1 20.4 %collective-permute-start.5 = (f32[96,128]{1,0:T(8,128)S(1)}, f32[96,128]{1,0:T(8,128)S(1)}, u32[]{:S(2)}, u32[]{:S(2)}) collective-permute-start(f32[96,128]{1,0:T(8,128)S(1)} %shard_map.56.z_one), channel_id=1, source_target_pairs={{0,3},{1,2},{2,1},{3,0},{4,7},{5,6},{6,5},{7,4},{8,11},{9,10},{10,... | collective-permute-start | bytes 147464 | tf_op jit(solution)/shard_map/ppermute | solution.py:352
  50.5 9.6 %copy-start = (s32[8,16]{1,0:T(8,128)S(1)}, s32[8,16]{1,0:T(8,128)}, u32[]{:S(2)}) copy-start(s32[8,16]{1,0:T(8,128)} %far_ref.1) | copy-start | bytes 1540

commit v7 on v6

--- a/solution.py
+++ b/solution.py
@@ -24,7 +24,8 @@
 RELAY = (3, 2, 1, 0)
 COUNT = 127
 ITEMS = 64
-STAGES = ((0, 5, 6), (7, 8, 9, 3, 4), (1, 3, 4), (2,))
+STAGES = ((0, 5, 6), (7, 8, 9, 3, 4), (1, 3, 4, 7), (2,))
+LATER = {3: (2, 3), 4: (2, 3), 7: (3,)}
 PLACES = 64
 
 
@@ -77,12 +78,13 @@
     entries = code.shape[1]
     stage = jnp.zeros_like(code)
     value = lax.broadcasted_iota(I32, code.shape, 0) * PLACES + code % BLK
-    early = lax.axis_index("oct") % 4 < 2
+    z_hi = lax.axis_index("oct") % 4
     for number, names in enumerate(STAGES):
         for place, name in enumerate(names):
             mine = code // BLK == name
-            if name in (3, 4):
-                mine = mine & (early if number == 1 else jnp.logical_not(early))
+            if name in LATER:
+                later = functools.reduce(jnp.logical_or, [z_hi == z for z in LATER[name]])
+                mine = mine & (later if number == 2 else jnp.logical_not(later))
             stage = jnp.where(mine, number, stage)
             value = value + jnp.where(mine, place * BLK, 0)
 
@@ -220,9 +222,10 @@
 
 
 def near_three_kernel(
-    control_ref, far_ref, z_one, y_all, target_ref, before, sums_ref, hot_ref, keep_ref, fold_ref, ones_ref, source_ref, masks_ref
+    control_ref, far_ref, z_one, y_all, wide_a, target_ref, before,
+    sums_ref, hot_ref, keep_ref, fold_ref, ones_ref, source_ref, masks_ref,
 ):
-    bodies = [block_of(z_one), y_member(y_all, 1), y_member(y_all, 2)]
+    bodies = [block_of(z_one), y_member(y_all, 1), y_member(y_all, 2), block_of(wide_a)]
     near_part(control_ref, target_ref, sums_ref, source_ref, masks_ref, bodies, 2)
     members = lax.axis_size("oct")
     far_count = far_ref.shape[1]
@@ -422,14 +425,14 @@
     sums, *picked = pl.pallas_call(
         near_three_kernel,
         out_shape=[state, *picks],
-        in_specs=[SMEM] + [VMEM] * 5,
+        in_specs=[SMEM] + [VMEM] * 6,
         out_specs=[VMEM] * 5,
-        scratch_shapes=sources(3),
-        input_output_aliases={5: 0},
+        scratch_shapes=sources(4),
+        input_output_aliases={6: 0},
         compiler_params=params(8),
         cost_estimate=cost(20 << 20),
         name="near_three",
-    )(control, far_list, relay, y_all, targets, sums)
+    )(control, far_list, relay, y_all, wide[1], targets, sums)
     return pl.pallas_call(
         functools.partial(last_kernel, entries=entries, far_count=far_count),
         out_shape=[jax.ShapeDtypeStruct(positions.shape, F32), state],

time: 66.3 us -> 66.3 us (level)
  no operation moved by 1% of the time
where the time goes in v7:
time: 66.3 us; the launch traced here: 66 us
  starting transfers between devices  32.5 us (49%)
  Pallas kernels  16.6 us (25%)
  blocking collectives  12.2 us (18%)
  waiting for transfers between devices  4.58 us (7%)
    ppermute x6, starting transfers between devices, exchange(): lax.ppermute(payload, axis, [(i, flip(i)) for i in range(lax.axis_size(ax...  32.5 us
    all_to_all x1, blocking collectives, step(): y_all = lax.all_to_all(message, 'oct', 0, 0, axis_index_groups=y_groups)  10.3 us
    pallas_call x1, Pallas kernels, step(): pl.pallas_call(near_two_kernel, out_shape=[state, state], in_specs=[SMEM]...  5.46 us
    ppermute x6, waiting for transfers between devices, exchange(): lax.ppermute(payload, axis, [(i, flip(i)) for i in range(lax.axis_size(ax...  4.58 us
    pallas_call x1, Pallas kernels, step(): pl.pallas_call(near_one_kernel, out_shape=state, in_specs=[SMEM] + [VMEM]...  4.16 us
    pallas_call x1, Pallas kernels, step(): pl.pallas_call(functools.partial(last_kernel, entries=entries, far_count=...  3.47 us
    pallas_call x1, Pallas kernels, step(): pl.pallas_call(near_three_kernel, out_shape=[state, *picks], in_specs=[SM...  2.3 us
    all_gather x1, blocking collectives, step(): pair = lax.all_gather(own, 'wide', axis_index_groups=cores)  1.86 us
  transfers between devices with their start and end apart: 6, of which 2 were waited for; matrix products, arithmetic and copies ran while one was open for 0% of the time, Pallas kernels for 18%

profile of v7, /device:TPU:6, one launch (start us, length us, event | category | flops | bytes accessed | tf_op | source)
XLA Modules:
  0.0 66.0 jit_solution(2119440283971952080)
XLA Ops:
  0.0 1.2 %pack.1 = (f32[72,128]{1,0:T(8,128)S(1)}, s32[8,128]{1,0:T(8,128)S(1)}) custom-call(s32[8]{0:T(128)} %counts_hbm.1, f32[3,2048]{1,0:T(4,128)} %pos_hbm.1, f32[16,128]{1,0:T(8,128)} %bitcast.4, s32[8,8]{1,0:T(8,128)} %near_hbm.1), custom_call_target="tpu_custom_call" | custom-call | tf_op jit(solution)/shard_map/pack/pallas_call | solution.py:362
  1.2 5.2 %collective-permute-start.1 = (f32[72,128]{1,0:T(8,128)S(1)}, f32[72,128]{1,0:T(8,128)S(1)}, u32[]{:S(2)}, u32[]{:S(2)}) collective-permute-start(f32[72,128]{1,0:T(8,128)S(1)} %get-tuple-element.16.refs_0_.own), channel_id=1, source_target_pairs={{0,64},{16,80},{32,96},{48,112},{64,0},{80,16},{96,32},{112,48},{1... | collective-permute-start | bytes 110600 | tf_op jit(solution)/shard_map/ppermute | solution.py:355
  6.4 3.8 %collective-permute-start = (f32[72,128]{1,0:T(8,128)S(1)}, f32[72,128]{1,0:T(8,128)S(1)}, u32[]{:S(2)}, u32[]{:S(2)}) collective-permute-start(f32[72,128]{1,0:T(8,128)S(1)} %get-tuple-element.16.refs_0_.own), channel_id=1, source_target_pairs={{0,32},{16,48},{32,0},{48,16},{64,96},{80,112},{96,64},{112,80},{1... | collective-permute-start | bytes 110600 | tf_op jit(solution)/shard_map/ppermute | solution.py:355
  10.2 2.7 %collective-permute-start.2 = (f32[72,128]{1,0:T(8,128)S(1)}, f32[72,128]{1,0:T(8,128)S(1)}, u32[]{:S(2)}, u32[]{:S(2)}) collective-permute-start(f32[72,128]{1,0:T(8,128)S(1)} %get-tuple-element.16.refs_0_.own), channel_id=1, source_target_pairs={{0,128},{16,144},{32,160},{48,176},{64,192},{80,208},{96,224},{112... | collective-permute-start | bytes 110600 | tf_op jit(solution)/shard_map/ppermute | solution.py:355
  12.9 3.2 %collective-permute-start.3 = (f32[72,128]{1,0:T(8,128)S(1)}, f32[72,128]{1,0:T(8,128)S(1)}, u32[]{:S(2)}, u32[]{:S(2)}) collective-permute-start(f32[72,128]{1,0:T(8,128)S(1)} %get-tuple-element.16.refs_0_.own), channel_id=1, source_target_pairs={{0,256},{16,272},{32,288},{48,304},{64,320},{80,336},{96,352},{112... | collective-permute-start | bytes 110600 | tf_op jit(solution)/shard_map/ppermute | solution.py:355
  16.2 1.9 %all-gather = f32[144,128]{1,0:T(8,128)S(1)} all-gather(f32[72,128]{1,0:T(8,128)S(1)} %get-tuple-element.16.refs_0_.own), channel_id=2, replica_groups={{0,16},{32,48},{64,80},{96,112},{128,144},{160,176},{192,208},{224,240}..., dimensions={0}, use_global_device_ids=true | all-gather | bytes 110592 | tf_op jit(solution)/shard_map/all_gather | solution.py:379
  18.0 0.0 collective-permute-done.1.refs_3_.wide_a
  18.0 0.0 collective-permute-done.refs_2_.wide_a
  18.0 0.0 collective-permute-done.2.refs_4_.wide_b
  18.0 2.3 %collective-permute-done.3.refs_5_.wide_c = f32[72,128]{1,0:T(8,128)S(1)} collective-permute-done((f32[72,128]{1,0:T(8,128)S(1)}, f32[72,128]{1,0:T(8,128)S(1)}, u32[]{:S(2)}, u32[]{:S(2)}) %collective-permute-start.3) | collective-permute-done | bytes 36896 | tf_op jit(solution)/shard_map/ppermute | solution.py:355
  20.3 0.1 join.1
  20.4 10.3 %all_to_all.5.y_all = f32[4,72,128]{2,1,0:T(8,128)S(1)} all-to-all(f32[4,72,128]{2,1,0:T(8,128)S(1)} %join.1), channel_id=1, replica_groups={{0,4,8,12},{1,5,9,13},{2,6,10,14},{3,7,11,15},{16,20,24,28},{17,21,25,2..., dimensions={0} | all-to-all | bytes 294912 | tf_op jit(solution)/shard_map/all_to_all | solution.py:391
  30.7 9.1 %collective-permute-start.4 = (f32[80,128]{1,0:T(8,128)S(1)}, f32[80,128]{1,0:T(8,128)S(1)}, u32[]{:S(2)}, u32[]{:S(2)}) collective-permute-start(f32[80,128]{1,0:T(8,128)S(1)} %shard_map.55.mine.own), channel_id=1, source_target_pairs={{0,1},{1,0},{2,3},{3,2},{4,5},{5,4},{6,7},{7,6},{8,9},{9,8},{10,11... | collective-permute-start | bytes 122888 | tf_op jit(solution)/shard_map/ppermute | solution.py:355
  39.8 2.3 %collective-permute-done.4.z_one = f32[80,128]{1,0:T(8,128)S(1)} collective-permute-done((f32[80,128]{1,0:T(8,128)S(1)}, f32[80,128]{1,0:T(8,128)S(1)}, u32[]{:S(2)}, u32[]{:S(2)}) %collective-permute-start.4) | collective-permute-done | bytes 40992 | tf_op jit(solution)/shard_map/ppermute | solution.py:355
  42.1 8.4 %collective-permute-start.5 = (f32[96,128]{1,0:T(8,128)S(1)}, f32[96,128]{1,0:T(8,128)S(1)}, u32[]{:S(2)}, u32[]{:S(2)}) collective-permute-start(f32[96,128]{1,0:T(8,128)S(1)} %shard_map.56.z_one), channel_id=1, source_target_pairs={{0,3},{1,2},{2,1},{3,0},{4,7},{5,6},{6,5},{7,4},{8,11},{9,10},{10,... | collective-permute-start | bytes 147464 | tf_op jit(solution)/shard_map/ppermute | solution.py:355
  50.5 0.0 copy-start
  50.6 4.2 %near_one.1.before = f32[3,2048,128]{2,1,0:T(8,128)S(1)} custom-call(s32[8,128]{1,0:T(8,128)S(1)} %get-tuple-element.15.control_ref, f32[72,128]{1,0:T(8,128)S(1)} %get-tuple-element.16.refs_0_.own, f32[2,72,128]{2,1,0:T(8,128)S(1)} %bitcast.3, f32[72,128]{1,0:T(8,128)S(1)} %collective-permute-done.refs_2_.wide_a), custom_call_target="tpu_custom_call" | custom-call | flops 20971520 | bytes 262144 | tf_op jit(solution)/shard_map/near_one/pallas_call | solution.py:393
  54.7 5.5 %near_two.1 = (f32[3,2048,128]{2,1,0:T(8,128)S(1)}, f32[3,2048,128]{2,1,0:T(8,128)S(1)}) custom-call(s32[8,128]{1,0:T(8,128)S(1)} %get-tuple-element.15.control_ref, f32[72,128]{1,0:T(8,128)S(1)} %collective-permute-done.1.refs_3_.wide_a, f32[72,128]{1,0:T(8,128)S(1)} %collective-permute-done.2.refs_4_.wide_b, ...), custom_call_target="tpu_custom_call", output_to_operand_aliasing={{1}: (6, {})} | custom-call | flops 20971520 | bytes 262144 | tf_op jit(solution)/shard_map/near_two/pallas_call | solution.py:405
  60.2 0.0 copy-done
  60.2 2.3 %near_three.1 = (f32[3,2048,128]{2,1,0:T(8,128)S(1)}, bf16[2,128,128]{2,1,0:T(8,128)(2,1)S(1)}, f32[2,128,128]{2,1,0:T(8,128)S(1)}, bf16[2,128,128]{2,1,0:T(8,128)(2,1)S(1)}, bf16[128,1280]{1,0:T(8,128)(2,1)S(1)}) custom-call(s32[8,128]{1,0:T(8,128)S(1)} %get-tuple-element.15.control_ref, s32[8,16]{1,0:T(8,128)S(1)} %copy-done, ...), custom_call_target="tpu_custom_call", output_to_operand_aliasing={{0}: (6, {})} | custom-call | flops 20971520 | bytes 262144 | tf_op jit(solution)/shard_map/near_three/pallas_call | solution.py:425
  62.5 0.0 collective-permute-done.5.z_two
  62.5 3.5 %last.1 = (f32[3,2048]{1,0:T(4,128)}, f32[3,2048,128]{2,1,0:T(8,128)S(1)}) custom-call(s32[8,128]{1,0:T(8,128)S(1)} %get-tuple-element.15.control_ref, bf16[2,128,128]{2,1,0:T(8,128)(2,1)S(1)} %get-tuple-element.19.hot_ref, f32[2,128,128]{2,1,0:T(8,128)S(1)} %get-tuple-element.20.keep_ref, ...), custom_call_target="tpu_custom_call", output_to_operand_aliasing={{1}: (9, {})} | custom-call | flops 20971520 | bytes 262144 | tf_op jit(solution)/shard_map/last/pallas_call | solution.py:436
  (2 shorter events, 0.0 us)
Async XLA Ops:
  1.2 16.8 %collective-permute-start.1 = (f32[72,128]{1,0:T(8,128)S(1)}, f32[72,128]{1,0:T(8,128)S(1)}, u32[]{:S(2)}, u32[]{:S(2)}) collective-permute-start(f32[72,128]{1,0:T(8,128)S(1)} %get-tuple-element.16.refs_0_.own), channel_id=1, source_target_pairs={{0,64},{16,80},{32,96},{48,112},{64,0},{80,16},{96,32},{112,48},{1... | collective-permute-start | bytes 110600 | tf_op jit(solution)/shard_map/ppermute | solution.py:355
  6.4 11.7 %collective-permute-start = (f32[72,128]{1,0:T(8,128)S(1)}, f32[72,128]{1,0:T(8,128)S(1)}, u32[]{:S(2)}, u32[]{:S(2)}) collective-permute-start(f32[72,128]{1,0:T(8,128)S(1)} %get-tuple-element.16.refs_0_.own), channel_id=1, source_target_pairs={{0,32},{16,48},{32,0},{48,16},{64,96},{80,112},{96,64},{112,80},{1... | collective-permute-start | bytes 110600 | tf_op jit(solution)/shard_map/ppermute | solution.py:355
  10.2 7.8 %collective-permute-start.2 = (f32[72,128]{1,0:T(8,128)S(1)}, f32[72,128]{1,0:T(8,128)S(1)}, u32[]{:S(2)}, u32[]{:S(2)}) collective-permute-start(f32[72,128]{1,0:T(8,128)S(1)} %get-tuple-element.16.refs_0_.own), channel_id=1, source_target_pairs={{0,128},{16,144},{32,160},{48,176},{64,192},{80,208},{96,224},{112... | collective-permute-start | bytes 110600 | tf_op jit(solution)/shard_map/ppermute | solution.py:355
  12.9 7.4 %collective-permute-start.3 = (f32[72,128]{1,0:T(8,128)S(1)}, f32[72,128]{1,0:T(8,128)S(1)}, u32[]{:S(2)}, u32[]{:S(2)}) collective-permute-start(f32[72,128]{1,0:T(8,128)S(1)} %get-tuple-element.16.refs_0_.own), channel_id=1, source_target_pairs={{0,256},{16,272},{32,288},{48,304},{64,320},{80,336},{96,352},{112... | collective-permute-start | bytes 110600 | tf_op jit(solution)/shard_map/ppermute | solution.py:355
  30.7 11.4 %collective-permute-start.4 = (f32[80,128]{1,0:T(8,128)S(1)}, f32[80,128]{1,0:T(8,128)S(1)}, u32[]{:S(2)}, u32[]{:S(2)}) collective-permute-start(f32[80,128]{1,0:T(8,128)S(1)} %shard_map.55.mine.own), channel_id=1, source_target_pairs={{0,1},{1,0},{2,3},{3,2},{4,5},{5,4},{6,7},{7,6},{8,9},{9,8},{10,11... | collective-permute-start | bytes 122888 | tf_op jit(solution)/shard_map/ppermute | solution.py:355
  42.1 20.4 %collective-permute-start.5 = (f32[96,128]{1,0:T(8,128)S(1)}, f32[96,128]{1,0:T(8,128)S(1)}, u32[]{:S(2)}, u32[]{:S(2)}) collective-permute-start(f32[96,128]{1,0:T(8,128)S(1)} %shard_map.56.z_one), channel_id=1, source_target_pairs={{0,3},{1,2},{2,1},{3,0},{4,7},{5,6},{6,5},{7,4},{8,11},{9,10},{10,... | collective-permute-start | bytes 147464 | tf_op jit(solution)/shard_map/ppermute | solution.py:355
  50.5 9.6 %copy-start = (s32[8,16]{1,0:T(8,128)S(1)}, s32[8,16]{1,0:T(8,128)}, u32[]{:S(2)}) copy-start(s32[8,16]{1,0:T(8,128)} %far_ref.1) | copy-start | bytes 1540
